TPU v7x, 32 devices: a whole 2x2x4 slice. The times are simulated.
32 devices in a mesh: seq: 16 (over z, y, core), tp: 2 (over x).
Axes of the slice: x: 2, y: 2, z: 4, core: 2. Of those that a mesh axis runs over, the one named last changes fastest.
Arguments:
- tokens: bfloat16 [8192, 2048], P('seq'), may hold values from -6 to 6
- doc_lengths: int32 [1, 32], replicated, may hold values from 1 to 768, 8192 in all within a row
- gain_one: bfloat16 [2048], P('seq'), may hold values from 0.099609375 to 1.8984375
- w_qkv: bfloat16 [2048, 3, 2048], P('seq', None, 'tp'), may hold values from -0.125 to 0.125
- w_out: bfloat16 [2048, 2048], P('tp', 'seq'), may hold values from -0.375 to 0.375
- gain_two: bfloat16 [2048], P('seq'), may hold values from 0.099609375 to 1.8984375
- w_gate_up: bfloat16 [2048, 2, 5504], P('seq', None, 'tp'), may hold values from -0.125 to 0.125
- w_down: bfloat16 [5504, 2048], P('tp', 'seq'), may hold values from -0.078125 to 0.078125
- cotangent: bfloat16 [8192, 2048], P('seq'), may hold values from -6 to 6
Outputs:
- result: bfloat16 [8192, 2048], P('seq')
- grad_tokens: float32 [8192, 2048], P('seq')
- grad_gain_one: float32 [2048], P('seq')
- grad_w_qkv: float32 [2048, 3, 2048], P('seq', None, 'tp')
- grad_w_out: float32 [2048, 2048], P('tp', 'seq')
- grad_gain_two: float32 [2048], P('seq')
- grad_w_gate_up: float32 [2048, 2, 5504], P('seq', None, 'tp')
- grad_w_down: float32 [5504, 2048], P('tp', 'seq')
Inputs may be any that keep to these rules, and one draw needn't show every extreme that they name: `doc_lengths`: each row lists the lengths of its 32 documents in order; they fill the row's 8192 tokens, and the longest document of every row has exactly 768 tokens.
All inputs are finite; a program needn't handle non-finite values.
Results may differ from a plain program's by a relative error of at most 0.014.
Values may be sent and summed in bfloat16 or wider, within the bound.
No kernel may reach another device: no remote copies, remote signals or barrier semaphores. Data moves between devices by JAX's collectives and lax.ppermute only.
A program may use at most 256 MiB of HBM per device.

v0:
```python
import jax
import jax.numpy as jnp
from jax import lax
from jax.sharding import PartitionSpec as P

HEAD_DIM = 128
WINDOW = 64


EPSILON = 1e-05
NEGATIVE = -1e30


def shifted(block, axis, distance):
    devices = range(lax.axis_size(axis))
    route = [(i - distance, i) for i in devices if i - distance in devices]
    return lax.ppermute(block, axis, route)


def rms_scale(values_in, gain_vec):
    return (
        values_in
        * lax.rsqrt(jnp.mean(values_in * values_in, axis=-1, keepdims=True) + EPSILON)
        * gain_vec
    )


def gated(gate_part, up_part):
    return gate_part / (1.0 + jnp.exp(-gate_part)) * up_part


def doc_starts(lengths, positions):
    doc_ends = jnp.cumsum(lengths)
    return jnp.sum(jnp.where(doc_ends[None, :] <= positions[:, None], lengths[None, :], 0), axis=1)


def block_mask(query_pos, key_pos, block_starts):
    return (
        (key_pos[None, :] >= block_starts[:, None])
        & (key_pos[None, :] <= query_pos[:, None])
        & (query_pos[:, None] - key_pos[None, :] < WINDOW)
    )


def local(tokens, doc_lengths, gain_one, w_qkv, w_out, gain_two, w_gate_up, w_down, cotangent):
    token_count = tokens.shape[0]
    local_width = w_qkv.shape[2]
    local_heads = local_width // HEAD_DIM
    score_scale = HEAD_DIM ** (-0.5)
    block_rows = min(512, token_count)
    row_length = token_count * lax.axis_size("seq") // doc_lengths.shape[0]
    first_token = lax.axis_index("seq") * token_count
    lengths = doc_lengths[0]
    positions = first_token % row_length + jnp.arange(token_count, dtype=jnp.int32)
    starts = doc_starts(lengths, positions)
    f32 = jnp.float32
    bf16 = jnp.bfloat16
    qkv_full, gain_one_full, out_full = (
        lax.all_gather(w_qkv, "seq", axis=0, tiled=True),
        lax.all_gather(gain_one, "seq", axis=0, tiled=True),
        lax.all_gather(w_out, "seq", axis=1, tiled=True),
    )
    token_rows = tokens.astype(f32)
    gain_a = gain_one_full.astype(f32)
    normed = rms_scale(token_rows, gain_a).astype(bf16)
    proj_qkv = jnp.einsum("td,dcf->tcf", normed, qkv_full, preferred_element_type=f32).astype(bf16)
    queries = proj_qkv[:, 0]
    key_rows = proj_qkv[:, 1]
    values = proj_qkv[:, 2]
    key_rim = jnp.stack([key_rows[token_count - WINDOW :], values[token_count - WINDOW :]])
    before = shifted(key_rim, "seq", 1)
    keys_ext = jnp.concatenate([before[0], key_rows], axis=0)
    values_ext = jnp.concatenate([before[1], values], axis=0)

    def scores_for():
        query_block = queries.reshape(block_rows, local_heads, HEAD_DIM)
        key_block = keys_ext.reshape(block_rows + WINDOW, local_heads, HEAD_DIM)
        value_block = values_ext.reshape(block_rows + WINDOW, local_heads, HEAD_DIM)
        key_pos = positions[0] - WINDOW + jnp.arange(block_rows + WINDOW, dtype=jnp.int32)
        scores = (
            jnp.einsum("qhd,khd->hqk", query_block, key_block, preferred_element_type=f32)
            * score_scale
        )
        scores = jnp.where(block_mask(positions, key_pos, starts)[None], scores, NEGATIVE)
        return (query_block, key_block, value_block, scores)

    def attend(block_start):
        query_block, key_block, value_block, scores = scores_for()
        row_max = jnp.max(scores, axis=-1, keepdims=True)
        exponent = jnp.exp(scores - row_max)
        row_total = jnp.sum(exponent, axis=-1, keepdims=True)
        probabilities = (exponent / row_total).astype(bf16)
        block_out = jnp.einsum(
            "hqk,khd->qhd", probabilities, value_block, preferred_element_type=f32
        )
        return (block_out.reshape(block_rows, local_width), (row_max + jnp.log(row_total))[..., 0])

    block_firsts = jnp.arange(token_count // block_rows, dtype=jnp.int32) * block_rows
    mixed_blocks, log_totals = lax.map(attend, block_firsts)
    attn_mixed = mixed_blocks.reshape(token_count, local_width).astype(bf16)
    attn_out = lax.psum(jnp.dot(attn_mixed, out_full, preferred_element_type=f32), "tp")
    middle = token_rows + attn_out
    gate_up_full, gain_two_full, down_full = (
        lax.all_gather(w_gate_up, "seq", axis=0, tiled=True),
        lax.all_gather(gain_two, "seq", axis=0, tiled=True),
        lax.all_gather(w_down, "seq", axis=1, tiled=True),
    )
    gain_b = gain_two_full.astype(f32)
    normed_two = rms_scale(middle, gain_b).astype(bf16)
    gate_up = jnp.einsum("td,dcf->tcf", normed_two, gate_up_full, preferred_element_type=f32)
    gate_part = gate_up[:, 0]
    up_part = gate_up[:, 1]
    hidden = gated(gate_part, up_part).astype(bf16)
    branch = lax.psum(
        jnp.dot(hidden, down_full, preferred_element_type=f32).astype(jnp.bfloat16), "tp"
    ).astype(jnp.float32)
    result = (middle + branch).astype(bf16)
    gate_up_back, gain_two_back, down_back = (
        lax.all_gather(w_gate_up, "seq", axis=0, tiled=True),
        lax.all_gather(gain_two, "seq", axis=0, tiled=True),
        lax.all_gather(w_down, "seq", axis=1, tiled=True),
    )
    qkv_back, gain_one_back, out_back = (
        lax.all_gather(w_qkv, "seq", axis=0, tiled=True),
        lax.all_gather(gain_one, "seq", axis=0, tiled=True),
        lax.all_gather(w_out, "seq", axis=1, tiled=True),
    )
    gain_b = gain_two_back.astype(f32)
    gain_a = gain_one_back.astype(f32)
    grad_w_down = jnp.einsum("tf,td->fd", hidden, cotangent, preferred_element_type=f32)
    grad_hidden = jnp.einsum("td,fd->tf", cotangent, down_back, preferred_element_type=f32)
    unused_value, gate_pull = jax.vjp(gated, gate_part, up_part)
    grad_gate, grad_up = gate_pull(grad_hidden)
    grad_gate_up = jnp.stack([grad_gate, grad_up], axis=1).astype(bf16)
    grad_w_gate_up = jnp.einsum("td,tcf->dcf", normed_two, grad_gate_up, preferred_element_type=f32)
    grad_normed_two = lax.psum(
        jnp.einsum("tcf,dcf->td", grad_gate_up, gate_up_back, preferred_element_type=f32), "tp"
    )
    unused_norm, norm_pull = jax.vjp(rms_scale, middle, gain_b)
    grad_mid_norm, grad_gain_two = norm_pull(grad_normed_two)
    grad_middle = cotangent.astype(f32) + grad_mid_norm
    mlp_terms = (grad_w_gate_up, grad_gain_two, grad_w_down)
    mlp_grads = (
        lax.psum_scatter(mlp_terms[0], "seq", scatter_dimension=0, tiled=True),
        lax.psum_scatter(mlp_terms[1], "seq", scatter_dimension=0, tiled=True),
        lax.psum_scatter(mlp_terms[2], "seq", scatter_dimension=1, tiled=True),
    )
    grad_attn = grad_middle.astype(bf16)
    grad_w_out = jnp.einsum("tf,td->fd", attn_mixed, grad_attn, preferred_element_type=f32)
    grad_mixed = jnp.einsum("td,fd->tf", grad_attn, out_back, preferred_element_type=f32).astype(
        bf16
    )

    def attend_back(carried, scan_item):
        grad_keys_ext, grad_values_ext = carried
        block_start, block_totals = scan_item
        query_block, key_block, value_block, scores = scores_for()
        probabilities = jnp.exp(scores - block_totals[..., None])
        grad_block = grad_mixed.reshape(block_rows, local_heads, HEAD_DIM)
        grad_probs = jnp.einsum("qhd,khd->hqk", grad_block, value_block, preferred_element_type=f32)
        grad_value_block = jnp.einsum(
            "hqk,qhd->khd", probabilities.astype(bf16), grad_block, preferred_element_type=f32
        )
        row_inner = jnp.sum(probabilities * grad_probs, axis=-1, keepdims=True)
        grad_scores = (probabilities * (grad_probs - row_inner)).astype(bf16)
        grad_query_block = (
            jnp.einsum("hqk,khd->qhd", grad_scores, key_block, preferred_element_type=f32)
            * score_scale
        )
        grad_key_block = (
            jnp.einsum("hqk,qhd->khd", grad_scores, query_block, preferred_element_type=f32)
            * score_scale
        )
        span = block_rows + WINDOW
        old_keys = grad_keys_ext
        old_values = grad_values_ext
        grad_keys_ext = old_keys + grad_key_block.reshape(span, local_width)
        grad_values_ext = old_values + grad_value_block.reshape(span, local_width)
        return ((grad_keys_ext, grad_values_ext), grad_query_block.reshape(block_rows, local_width))

    zero_ext = jnp.zeros((token_count + WINDOW, local_width), f32)
    (grad_keys_ext, grad_values_ext), grad_query_blocks = lax.scan(
        attend_back, (zero_ext, zero_ext), (block_firsts, log_totals)
    )
    grad_queries = grad_query_blocks.reshape(token_count, local_width)
    edge_grads = jnp.stack([grad_keys_ext[:WINDOW], grad_values_ext[:WINDOW]])
    arrived = shifted(edge_grads.astype(jnp.bfloat16), "seq", -1).astype(edge_grads.dtype)
    grad_keys = grad_keys_ext[WINDOW:].at[token_count - WINDOW :].add(arrived[0])
    grad_values = grad_values_ext[WINDOW:].at[token_count - WINDOW :].add(arrived[1])
    grad_proj = jnp.stack([grad_queries, grad_keys, grad_values], axis=1).astype(bf16)
    grad_w_qkv = jnp.einsum("td,tcf->dcf", normed, grad_proj, preferred_element_type=f32)
    grad_normed = lax.psum(
        jnp.einsum("tcf,dcf->td", grad_proj, qkv_back, preferred_element_type=f32), "tp"
    )
    unused_first, first_pull = jax.vjp(rms_scale, token_rows, gain_a)
    grad_rows_norm, grad_gain_one = first_pull(grad_normed)
    grad_tokens = grad_middle + grad_rows_norm
    attn_grads = (
        lax.psum_scatter(grad_w_qkv, "seq", scatter_dimension=0, tiled=True),
        lax.psum_scatter(grad_gain_one, "seq", scatter_dimension=0, tiled=True),
        lax.psum_scatter(grad_w_out, "seq", scatter_dimension=1, tiled=True),
    )
    return (
        result,
        grad_tokens,
        attn_grads[1],
        attn_grads[0],
        attn_grads[2],
        mlp_grads[1],
        mlp_grads[0],
        mlp_grads[2],
    )


def solution(mesh):
    return jax.shard_map(
        local,
        mesh=mesh,
        in_specs=(
            P("seq", None),
            P(),
            P("seq"),
            P("seq", None, "tp"),
            P("tp", "seq"),
            P("seq"),
            P("seq", None, "tp"),
            P("tp", "seq"),
            P("seq", None),
        ),
        out_specs=(
            P("seq", None),
            P("seq", None),
            P("seq"),
            P("seq", None, "tp"),
            P("tp", "seq"),
            P("seq"),
            P("seq", None, "tp"),
            P("tp", "seq"),
        ),
        check_vma=False,
    )
```

profile of v0, /device:TPU:0, one launch (start us, length us, event | category | flops | bytes accessed | tf_op | source)
XLA Modules:
  0.0 1914.5 jit_solution(14942717814333129567)
XLA Ops:
  9.2 23.7 %all-gather = bf16[16,1,128]{2,1,0:T(2,128)(2,1)S(1)} all-gather(bf16[1,1,128]{2,1,0:T(2,128)(2,1)} %bitcast.148), channel_id=1, replica_groups=mesh['seq'=16,'tp'=2] {'seq'}, dimensions={0}, use_global_device_ids=true | all-gather | bytes 4352 | tf_op jit(solution)/shard_map/all_gather | solution.py:60
  34.5 0.7 select_reduce_fusion
  35.2 2.1 fusion.12
  38.3 75.0 %all-gather.7.cloned.1.call-done = bf16[2048,3,1024]{2,0,1:T(8,128)(2,1)} async-done(((bf16[128,3,1024]{2,0,1:T(8,128)(2,1)}), bf16[2048,3,1024]{2,0,1:T(8,128)(2,1)}) %all-gather.7.cloned.1.call-update) | async-done | bytes 12582928 | tf_op jit(solution)/shard_map/all_gather | solution.py:59
  113.4 10.3 convolution_convert_fusion.1
  123.8 2.3 collective-permute-start
  128.4 1.8 fusion.53
  130.2 1.4 fusion
  131.6 2.2 copy-done
  133.8 2.3 fusion.24
  136.1 31.4 %all-gather.9.cloned.1.call-done = bf16[1024,2048]{1,0:T(8,128)(2,1)} async-done(((bf16[1024,128]{1,0:T(8,128)(2,1)}), bf16[1024,2048]{1,0:T(8,128)(2,1)}) %all-gather.9.cloned.1.call-update) | async-done | bytes 4194320 | tf_op jit(solution)/shard_map/all_gather | solution.py:61
  167.5 6.6 fusion.54
  175.3 18.8 all-gather.1
  194.1 86.2 %all-reduce.8.cloned.1.call-done = f32[512,2048]{1,0:T(8,128)} async-done(((f32[512,2048]{1,0:T(8,128)}), f32[512,2048]{1,0:T(8,128)}) %all-reduce.8.cloned.1.call-update) | async-done | bytes 4194320 | tf_op jit(solution)/shard_map/psum | solution.py:101
  280.3 4.7 multiply_reduce_fusion.3
  285.1 119.8 %all-gather.11.cloned.1.call-done = bf16[2048,2,2752]{0,2,1:T(8,128)(2,1)} async-done(((bf16[128,2,2752]{0,2,1:T(8,128)(2,1)}), bf16[2048,2,2752]{0,2,1:T(8,128)(2,1)}) %all-gather.11.cloned.1.call-update) | async-done | bytes 22544400 | tf_op jit(solution)/shard_map/all_gather | solution.py:104
  404.9 20.1 %fusion.45 = f32[512,2,2752]{0,2,1:T(8,128)} fusion(bf16[2048,2,2752]{0,2,1:T(8,128)(2,1)} %all-gather.11.cloned.1.call-done, f32[512,2048]{1,0:T(8,128)} %get-tuple-element.96, f32[2048]{0:T(1024)S(1)} %bitcast.142, f32[512]{0:T(512)S(1)} %fusion.48), kind=kOutput, calls=%fused_computation.91 | convolution fusion | flops 11545870336 | bytes 38021120 | tf_op jit(solution)/shard_map/td,dcf->tcf/dot_general | solution.py:110
  425.0 75.3 %all-gather.13.cloned.1.call-done = bf16[2752,2048]{1,0:T(8,128)(2,1)} async-done(((bf16[2752,128]{1,0:T(8,128)(2,1)}), bf16[2752,2048]{1,0:T(8,128)(2,1)}) %all-gather.13.cloned.1.call-update) | async-done | bytes 11272208 | tf_op jit(solution)/shard_map/all_gather | solution.py:106
  500.3 16.1 fusion.18
  516.4 1.5 copy-done.22
  517.9 0.9 copy-done.23
  518.8 18.5 fusion.16
  537.4 10.8 convolution_convert_fusion
  548.3 95.3 %all-reduce.12.cloned.1.call-done = f32[512,2048]{1,0:T(8,128)} async-done(((f32[512,2048]{1,0:T(8,128)}), f32[512,2048]{1,0:T(8,128)}) %all-reduce.12.cloned.1.call-update) | async-done | bytes 4194320 | tf_op jit(solution)/shard_map/psum | solution.py:136
  643.6 4.5 multiply_reduce_fusion.1
  648.1 61.4 %all-reduce.10.cloned.1.call-done = bf16[512,2048]{1,0:T(8,128)(2,1)} async-done(((bf16[512,2048]{1,0:T(8,128)(2,1)}), bf16[512,2048]{1,0:T(8,128)(2,1)}) %all-reduce.10.cloned.1.call-update) | async-done | bytes 2097168 | tf_op jit(solution)/shard_map/psum | solution.py:114
  709.5 6.8 fusion.10
  716.3 2.1 copy-done.1
  718.4 2.4 fusion.25
  720.9 1.4 fusion.21
  722.3 1.3 slice.135
  723.6 4.6 multiply_reduce_fusion
  728.3 11.3 multiply_convert_fusion
  739.6 4.0 multiply_bitcast_fusion
  745.0 1.1 slice.130
  746.9 1.6 stack.51
  748.5 2.3 copy.80
  750.8 2.3 copy.82
  753.0 0.8 copy.81
  753.9 1.7 reshape.317
  755.7 1.6 pad_maximum_fusion.9
  757.4 1.3 collective-permute-start.1
  758.7 4.7 multiply_convert_fusion.4
  763.4 2.5 copy.83
  765.9 2.3 copy.74
  768.1 2.3 copy.79
  770.4 0.9 copy.75
  771.3 1.0 reshape.315
  772.3 1.0 convert_element_type.87
  773.3 1.7 fusion.43
  775.0 11.9 convolution_bitcast_fusion
  787.0 8.0 fusion.33
  795.1 12.7 fusion.55
  807.9 1.2 copy-done.9
  809.1 13.7 fusion.26
  823.5 22.6 %fusion.14 = f32[2048,2,2752]{0,2,1:T(8,128)} fusion(bf16[512,1,2752]{0,2,1:T(8,128)(2,1)} %copy-done.23, bf16[512,1,2752]{0,2,1:T(8,128)(2,1)} %copy-done.22, f32[512,2048]{1,0:T(8,128)} %get-tuple-element.96, f32[2048]{0:T(1024)S(1)} %bitcast.145, f32[512]{0:T(512)S(1)} %copy-done.17), kind=kOutput, calls=%fused_computation.39 | convolution fusion | flops 11557142528 | bytes 54929408 | tf_op jit(solution)/shard_map/td,tcf->dcf/dot_general | solution.py:135
  848.0 48.5 %all-reduce.14.cloned.1.call-done = f32[512,2048]{1,0:T(8,128)} async-done(((f32[512,2048]{1,0:T(8,128)}), f32[512,2048]{1,0:T(8,128)}) %all-reduce.14.cloned.1.call-update) | async-done | bytes 4194320 | tf_op jit(solution)/shard_map/psum | solution.py:192
  896.5 3.5 fusion.9
  900.0 63.3 %all-reduce.2 = (f32[2048]{0:T(1024)S(1)}, f32[2048]{0:T(1024)S(1)}) all-reduce(f32[2048]{0:T(1024)S(1)} %get-tuple-element.91, f32[2048]{0:T(1024)S(1)} %get-tuple-element.89), channel_id=2, replica_groups=mesh['seq'=16,'tp'=2] {'seq'}, use_global_device_ids=true, to_apply=%region_14.15.clone | all-reduce | flops 4096 | bytes 32768
  964.4 6.6 fusion.11
  971.1 34.0 %reduce-scatter.7.cloned.1.call-done = f32[1024,128]{1,0:T(8,128)} async-done(((f32[1024,2048]{1,0:T(8,128)}), f32[1024,128]{1,0:T(8,128)}) %reduce-scatter.7.cloned.1.call-update) | async-done | bytes 524304 | tf_op jit(solution)/shard_map/reduce_scatter | solution.py:201
  1005.1 227.3 %reduce-scatter.11.cloned.1.call-done = f32[2752,128]{1,0:T(8,128)} async-done(((f32[2752,2048]{1,0:T(8,128)}), f32[2752,128]{1,0:T(8,128)}) %reduce-scatter.11.cloned.1.call-update) | async-done | bytes 1409040 | tf_op jit(solution)/shard_map/reduce_scatter | solution.py:146
  1232.3 247.1 %reduce-scatter.5.cloned.1.call-done = f32[128,3,1024]{2,0,1:T(8,128)} async-done(((f32[2048,3,1024]{2,0,1:T(8,128)}), f32[128,3,1024]{2,0,1:T(8,128)}) %reduce-scatter.5.cloned.1.call-update) | async-done | bytes 1572880 | tf_op jit(solution)/shard_map/reduce_scatter | solution.py:199
  1479.5 427.9 %reduce-scatter.9.cloned.1.call-done = f32[128,2,2752]{0,2,1:T(8,128)} async-done(((f32[2048,2,2752]{0,2,1:T(8,128)}), f32[128,2,2752]{0,2,1:T(8,128)}) %reduce-scatter.9.cloned.1.call-update) | async-done | bytes 2818064 | tf_op jit(solution)/shard_map/reduce_scatter | solution.py:144
  (114 shorter events, 13.1 us)
Async XLA Ops:
  7.2 106.2 %all-gather.7.cloned.1.call-start = ((), (), s32[]{:S(2)}) async-start(), calls=%async_computation.4 | async-start | bytes 13369344 | tf_op jit(solution)/shard_map/all_gather | solution.py:59
  7.9 159.6 %all-gather.9.cloned.1.call-start = ((), (), s32[]{:S(2)}) async-start(), calls=%async_computation.5 | async-start | bytes 4456448 | tf_op jit(solution)/shard_map/all_gather | solution.py:61
  8.6 271.7 %all-reduce.8.cloned.1.call-start = ((), (), s32[]{:S(2)}) async-start(), calls=%async_computation.6 | async-start | bytes 8388608 | tf_op jit(solution)/shard_map/psum | solution.py:101
  32.9 90.8 %copy-start.12 = (f32[16,1,128]{2,1,0:T(1,128)}, f32[16,1,128]{2,1,0:T(1,128)S(1)}, u32[]{:S(2)}) copy-start(f32[16,1,128]{2,1,0:T(1,128)S(1)} %convert_element_type.88) | copy-start | bytes 24580
  37.3 0.6 copy-start.14
  37.9 85.8 %copy-start.18 = (f32[512]{0:T(512)}, f32[512]{0:T(512)S(1)}, u32[]{:S(2)}) copy-start(f32[512]{0:T(512)S(1)} %fusion.47) | copy-start | bytes 6148
  123.8 3.9 collective-permute-start
  127.2 1.2 copy-start.6
  128.1 2.1 copy-start.5
  128.4 3.2 copy-start.7
  130.2 3.5 copy-start
  174.1 1.2 copy-start.20
  174.1 106.3 %copy-start.2 = (bf16[512,2048]{1,0:T(8,128)(2,1)S(1)}, bf16[512,2048]{1,0:T(8,128)(2,1)}, u32[]{:S(2)}) copy-start(bf16[512,2048]{1,0:T(8,128)(2,1)} %param.13) | copy-start | bytes 6291460
  174.1 230.8 %all-gather.11.cloned.1.call-start = ((), (), s32[]{:S(2)}) async-start(), calls=%async_computation.7 | async-start | bytes 23953408 | tf_op jit(solution)/shard_map/all_gather | solution.py:104
  174.7 325.6 %all-gather.13.cloned.1.call-start = ((), (), s32[]{:S(2)}) async-start(), calls=%async_computation.8 | async-start | bytes 11976704 | tf_op jit(solution)/shard_map/all_gather | solution.py:106
  175.3 468.3 %all-reduce.12.cloned.1.call-start = ((), (), s32[]{:S(2)}) async-start(), calls=%async_computation.10 | async-start | bytes 8388608 | tf_op jit(solution)/shard_map/psum | solution.py:136
  285.1 424.4 %copy-start.16 = (f32[512]{0:T(512)}, f32[512]{0:T(512)S(1)}, u32[]{:S(2)}) copy-start(f32[512]{0:T(512)S(1)} %fusion.48) | copy-start | bytes 6148
  516.4 1.5 copy-start.22
  516.4 2.5 copy-start.23
  537.3 172.1 %all-reduce.10.cloned.1.call-start = ((), (), s32[]{:S(2)}) async-start(), calls=%async_computation.9 | async-start | bytes 4194304 | tf_op jit(solution)/shard_map/psum | solution.py:114
  548.2 348.3 %all-reduce.14.cloned.1.call-start = ((), (), s32[]{:S(2)}) async-start(), calls=%async_computation.11 | async-start | bytes 8388608 | tf_op jit(solution)/shard_map/psum | solution.py:192
  709.5 8.9 copy-start.3
  709.5 11.4 slice-start
  709.5 11.4 slice-start.1
  716.3 2.1 copy-start.1
  718.4 2.4 slice-start.2
  720.9 2.8 copy-start.8
  722.3 6.0 copy-start.4
  743.6 9.4 slice-start.3
  746.9 8.7 copy-start.11
  757.4 14.9 collective-permute-start.1
  763.4 7.0 copy-start.10
  787.0 218.1 %reduce-scatter.7.cloned.1.call-start = ((), (), s32[]{:S(2)}) async-start(), calls=%async_computation.13 | async-start | bytes 8912896 | tf_op jit(solution)/shard_map/reduce_scatter | solution.py:201
  795.0 437.3 %reduce-scatter.11.cloned.1.call-start = ((), (), s32[]{:S(2)}) async-start(), calls=%async_computation.15 | async-start | bytes 23953408 | tf_op jit(solution)/shard_map/reduce_scatter | solution.py:146
  807.8 1.3 copy-start.9
  807.8 1.3 copy-start.13
  807.8 1.3 copy-start.19
  807.9 671.6 %reduce-scatter.5.cloned.1.call-start = ((), (), s32[]{:S(2)}) async-start(), calls=%async_computation.12 | async-start | bytes 26738688 | tf_op jit(solution)/shard_map/reduce_scatter | solution.py:199
  822.8 0.7 copy-start.17
  822.8 1084.5 %reduce-scatter.9.cloned.1.call-start = ((), (), s32[]{:S(2)}) async-start(), calls=%async_computation.14 | async-start | bytes 47906816 | tf_op jit(solution)/shard_map/reduce_scatter | solution.py:144
  846.1 0.7 copy-start.21
  846.1 118.3 %copy-start.15 = (f32[512]{0:T(512)S(1)}, f32[512]{0:T(512)}, u32[]{:S(2)}) copy-start(f32[512]{0:T(512)} %copy-done.14) | copy-start | bytes 6148
Sparse Core Ops, SparseCore 0:
  10.2 103.1 all-gather.6
  115.5 51.9 all-gather.8
  174.2 106.0 all-reduce.7
  281.7 123.1 all-gather.10
  406.9 93.3 all-gather.12
  537.5 106.0 all-reduce.11
  646.4 62.9 all-reduce.9
  787.1 109.3 all-reduce.13
  901.1 103.8 reduce-scatter.6
  1009.7 222.5 reduce-scatter.10
  1237.0 242.3 reduce-scatter.4
  1484.3 423.0 reduce-scatter.8
where the time goes:
time: 1920 us; the launch traced here: 1910 us
  waiting for transfers between devices  1530 us (80%)
  matrix products  173 us (9%)
  blocking collectives  106 us (6%)
  other arithmetic  46.7 us (2%)
  local copies, waits for them, and re-layouts  37.3 us (2%)
    reduce_scatter x1, waiting for transfers between devices, local(): lax.psum_scatter(mlp_terms[0], 'seq', scatter_dimension=0, tiled=True)  428 us
    reduce_scatter x1, waiting for transfers between devices, local(): lax.psum_scatter(grad_w_qkv, 'seq', scatter_dimension=0, tiled=True)  247 us
    reduce_scatter x1, waiting for transfers between devices, local(): lax.psum_scatter(mlp_terms[2], 'seq', scatter_dimension=1, tiled=True)  227 us
    all_gather x1, waiting for transfers between devices, local(): lax.all_gather(w_gate_up, 'seq', axis=0, tiled=True)  120 us
    psum x1, waiting for transfers between devices, local(): lax.psum(jnp.einsum('tcf,dcf->td', grad_gate_up, gate_up_back, preferred_...  95.3 us
    psum x1, waiting for transfers between devices, local(): lax.psum(jnp.dot(attn_mixed, out_full, preferred_element_type=f32), 'tp')  86.2 us
    all_gather x1, waiting for transfers between devices, local(): lax.all_gather(w_down, 'seq', axis=1, tiled=True)  75.3 us
    all_gather x1, waiting for transfers between devices, local(): lax.all_gather(w_qkv, 'seq', axis=0, tiled=True)  75 us
  transfers between devices with their start and end apart: 14, of which 12 were waited for; matrix products, arithmetic and copies ran while one was open for 8% of the time, Pallas kernels for 0%

commit v1 on v0

--- a/solution.py
+++ b/solution.py
@@ -15,6 +15,11 @@
     devices = range(lax.axis_size(axis))
     route = [(i - distance, i) for i in devices if i - distance in devices]
     return lax.ppermute(block, axis, route)
+
+
+def scattered(terms, dimension):
+    low = terms.astype(jnp.bfloat16)
+    return lax.psum_scatter(low, "seq", scatter_dimension=dimension, tiled=True).astype(jnp.float32)
 
 
 def rms_scale(values_in, gain_vec):
@@ -98,7 +103,9 @@
     block_firsts = jnp.arange(token_count // block_rows, dtype=jnp.int32) * block_rows
     mixed_blocks, log_totals = lax.map(attend, block_firsts)
     attn_mixed = mixed_blocks.reshape(token_count, local_width).astype(bf16)
-    attn_out = lax.psum(jnp.dot(attn_mixed, out_full, preferred_element_type=f32), "tp")
+    attn_out = lax.psum(
+        jnp.dot(attn_mixed, out_full, preferred_element_type=f32).astype(bf16), "tp"
+    ).astype(f32)
     middle = token_rows + attn_out
     gate_up_full, gain_two_full, down_full = (
         lax.all_gather(w_gate_up, "seq", axis=0, tiled=True),
@@ -134,16 +141,19 @@
     grad_gate_up = jnp.stack([grad_gate, grad_up], axis=1).astype(bf16)
     grad_w_gate_up = jnp.einsum("td,tcf->dcf", normed_two, grad_gate_up, preferred_element_type=f32)
     grad_normed_two = lax.psum(
-        jnp.einsum("tcf,dcf->td", grad_gate_up, gate_up_back, preferred_element_type=f32), "tp"
-    )
+        jnp.einsum("tcf,dcf->td", grad_gate_up, gate_up_back, preferred_element_type=f32).astype(
+            bf16
+        ),
+        "tp",
+    ).astype(f32)
     unused_norm, norm_pull = jax.vjp(rms_scale, middle, gain_b)
     grad_mid_norm, grad_gain_two = norm_pull(grad_normed_two)
     grad_middle = cotangent.astype(f32) + grad_mid_norm
     mlp_terms = (grad_w_gate_up, grad_gain_two, grad_w_down)
     mlp_grads = (
-        lax.psum_scatter(mlp_terms[0], "seq", scatter_dimension=0, tiled=True),
+        scattered(mlp_terms[0], 0),
         lax.psum_scatter(mlp_terms[1], "seq", scatter_dimension=0, tiled=True),
-        lax.psum_scatter(mlp_terms[2], "seq", scatter_dimension=1, tiled=True),
+        scattered(mlp_terms[2], 1),
     )
     grad_attn = grad_middle.astype(bf16)
     grad_w_out = jnp.einsum("tf,td->fd", attn_mixed, grad_attn, preferred_element_type=f32)
@@ -190,15 +200,16 @@
     grad_proj = jnp.stack([grad_queries, grad_keys, grad_values], axis=1).astype(bf16)
     grad_w_qkv = jnp.einsum("td,tcf->dcf", normed, grad_proj, preferred_element_type=f32)
     grad_normed = lax.psum(
-        jnp.einsum("tcf,dcf->td", grad_proj, qkv_back, preferred_element_type=f32), "tp"
-    )
+        jnp.einsum("tcf,dcf->td", grad_proj, qkv_back, preferred_element_type=f32).astype(bf16),
+        "tp",
+    ).astype(f32)
     unused_first, first_pull = jax.vjp(rms_scale, token_rows, gain_a)
     grad_rows_norm, grad_gain_one = first_pull(grad_normed)
     grad_tokens = grad_middle + grad_rows_norm
     attn_grads = (
-        lax.psum_scatter(grad_w_qkv, "seq", scatter_dimension=0, tiled=True),
+        scattered(grad_w_qkv, 0),
         lax.psum_scatter(grad_gain_one, "seq", scatter_dimension=0, tiled=True),
-        lax.psum_scatter(grad_w_out, "seq", scatter_dimension=1, tiled=True),
+        scattered(grad_w_out, 1),
     )
     return (
         result,

time: 1920 us -> 1320 us (0.69)
  waiting for transfers between devices: 1530 us -> 895 us
  local copies, waits for them, and re-layouts: 37.3 us -> 87.8 us
    reduce_scatter x4 -> x1, waiting for transfers between devices: 936 us -> 135 us  [scattered(): lax.psum_scatter(low, 'seq', scatter_dimension=dimension, tiled=True)]
    unnamed x12 -> x14, waiting for transfers between devices: 2.56 us -> 358 us
    psum x2 -> x1, waiting for transfers between devices: 135 us -> 41 us  [local(): lax.psum(jnp.dot(attn_mixed, out_full, preferred_element_type=f32).astype...]
    psum x1, waiting for transfers between devices: 61.4 us -> 6.43 us  [local(): lax.psum(jnp.dot(hidden, down_full, preferred_element_type=f32).astype(jn...]
    unnamed x66 -> x78, local copies, waits for them, and re-layouts: 13.2 us -> 65.9 us
    psum x1, waiting for transfers between devices: 95.3 us -> 50.4 us  [local(): lax.psum(jnp.einsum('tcf,dcf->td', grad_gate_up, gate_up_back, preferred_...]
  transfers between devices with their start and end apart: 14 -> 13, of which waited for: 12 -> 11; matrix products, arithmetic and copies ran while one was open for 8% -> 14% of each run, Pallas kernels for 0% -> 0%
where the time goes in v1:
time: 1320 us
  waiting for transfers between devices  895 us (68%)
  matrix products  165 us (12%)
  blocking collectives  105 us (8%)
  local copies, waits for them, and re-layouts  87.8 us (7%)
  other arithmetic  45 us (3%)
  between operations  15.9 us (1%)
    unnamed x14, waiting for transfers between devices  358 us
    reduce_scatter x1, waiting for transfers between devices, scattered(): lax.psum_scatter(low, 'seq', scatter_dimension=dimension, tiled=True)  135 us
    all_gather x1, waiting for transfers between devices, local(): lax.all_gather(w_gate_up, 'seq', axis=0, tiled=True)  122 us
    all_gather x1, waiting for transfers between devices, local(): lax.all_gather(w_down, 'seq', axis=1, tiled=True)  75.8 us
    all_gather x1, waiting for transfers between devices, local(): lax.all_gather(w_qkv, 'seq', axis=0, tiled=True)  74.9 us
    unnamed x78, local copies, waits for them, and re-layouts  65.9 us
    unnamed x1, blocking collectives  62 us
    psum x1, waiting for transfers between devices, local(): lax.psum(jnp.einsum('tcf,dcf->td', grad_gate_up, gate_up_back, preferred_...  50.4 us
  transfers between devices with their start and end apart: 13, of which 11 were waited for; matrix products, arithmetic and copies ran while one was open for 14% of the time, Pallas kernels for 0%

profile of v1, /device:TPU:0, one launch (start us, length us, event | category | flops | bytes accessed | tf_op | source)
XLA Modules:
  0.0 1319.0 jit_solution(15667402002596627431)
XLA Ops:
  9.2 23.7 %all-gather = bf16[16,1,128]{2,1,0:T(2,128)(2,1)S(1)} all-gather(bf16[1,1,128]{2,1,0:T(2,128)(2,1)} %bitcast.161), channel_id=1, replica_groups=mesh['seq'=16,'tp'=2] {'seq'}, dimensions={0}, use_global_device_ids=true | all-gather | bytes 4352 | tf_op jit(solution)/shard_map/all_gather | solution.py:65
  35.2 2.1 fusion.16
  37.3 1.1 fusion.28
  38.5 74.9 %all-gather.7.cloned.1.call-done = bf16[2048,3,1024]{2,0,1:T(8,128)(2,1)} async-done(((bf16[128,3,1024]{2,0,1:T(8,128)(2,1)}), bf16[2048,3,1024]{2,0,1:T(8,128)(2,1)}) %all-gather.7.cloned.1.call-update) | async-done | bytes 12582928 | tf_op jit(solution)/shard_map/all_gather | solution.py:64
  113.4 10.4 convolution_convert_fusion.6
  123.8 2.5 collective-permute-start
  128.6 1.8 fusion.55
  130.4 1.4 fusion
  131.8 2.2 copy-done
  134.0 2.3 fusion.26
  136.3 31.3 %all-gather.9.cloned.1.call-done = bf16[1024,2048]{1,0:T(8,128)(2,1)} async-done(((bf16[1024,128]{1,0:T(8,128)(2,1)}), bf16[1024,2048]{1,0:T(8,128)(2,1)}) %all-gather.9.cloned.1.call-update) | async-done | bytes 4194320 | tf_op jit(solution)/shard_map/all_gather | solution.py:66
  167.5 5.9 convolution_convert_fusion.4
  174.6 19.1 %all-gather.1 = bf16[16,1,128]{2,1,0:T(2,128)(2,1)S(1)} all-gather(bf16[1,1,128]{2,1,0:T(2,128)(2,1)S(1)} %bitcast.162), channel_id=1, replica_groups=mesh['seq'=16,'tp'=2] {'seq'}, dimensions={0}, use_global_device_ids=true | all-gather | bytes 4352 | tf_op jit(solution)/shard_map/all_gather | solution.py:112
  193.7 41.0 %all-reduce.8.cloned.1.call-done = bf16[512,2048]{1,0:T(8,128)(2,1)} async-done(((bf16[512,2048]{1,0:T(8,128)(2,1)}), bf16[512,2048]{1,0:T(8,128)(2,1)}) %all-reduce.8.cloned.1.call-update) | async-done | bytes 2097168 | tf_op jit(solution)/shard_map/psum | solution.py:106
  234.7 2.3 multiply_reduce_fusion.1
  237.1 122.2 %all-gather.11.cloned.1.call-done = bf16[2048,2,2752]{0,2,1:T(8,128)(2,1)} async-done(((bf16[128,2,2752]{0,2,1:T(8,128)(2,1)}), bf16[2048,2,2752]{0,2,1:T(8,128)(2,1)}) %all-gather.11.cloned.1.call-update) | async-done | bytes 22544400 | tf_op jit(solution)/shard_map/all_gather | solution.py:111
  359.3 19.5 %fusion.51 = f32[512,2,2752]{0,2,1:T(8,128)} fusion(bf16[2048,2,2752]{0,2,1:T(8,128)(2,1)} %all-gather.11.cloned.1.call-done, bf16[512,2048]{1,0:T(8,128)(2,1)} %all-reduce.8.cloned.1.call-done, bf16[512,2048]{1,0:T(8,128)(2,1)S(1)} %copy-done.1, f32[2048]{0:T(1024)S(1)} %bitcast.153, f32[512]{0:T(512)S(1)} %fusion.45), kind=kOutput, calls=%fused_computation.112 | convolution fusion | flops 11549016064 | bytes 38021120 | tf_op jit(solution)/shard_map/td,dcf->tcf/dot_general | solution.py:117
  378.8 75.8 %all-gather.13.cloned.1.call-done = bf16[2752,2048]{1,0:T(8,128)(2,1)} async-done(((bf16[2752,128]{1,0:T(8,128)(2,1)}), bf16[2752,2048]{1,0:T(8,128)(2,1)}) %all-gather.13.cloned.1.call-update) | async-done | bytes 11272208 | tf_op jit(solution)/shard_map/all_gather | solution.py:113
  454.6 16.1 %fusion.20 = (bf16[512,1,2752]{0,2,1:T(8,128)(2,1)S(1)}, bf16[512,1,2752]{0,2,1:T(8,128)(2,1)S(1)}, bf16[512,2752]{0,1:T(8,128)(2,1)}) fusion(f32[512,2,2752]{0,2,1:T(8,128)} %fusion.51, bf16[512,2048]{1,0:T(8,128)(2,1)} %param.21, bf16[2752,2048]{1,0:T(8,128)(2,1)} %all-gather.13.cloned.1.call-done), kind=kOutput, calls=%fused_computation.56 | convolution fusion | flops 5796724736 | bytes 33095680 | tf_op jit(solution)/shard_map/td,fd->tf/dot_general | solution.py:138
  470.8 1.5 copy-done.25
  473.2 17.9 %bitcast_convert_fusion.1 = bf16[512,2048]{1,0:T(8,128)(2,1)} fusion(bf16[2048,2,2752]{0,2,1:T(8,128)(2,1)} %all-gather.11.cloned.1.call-done, bf16[512,1,2752]{0,2,1:T(8,128)(2,1)S(1)} %get-tuple-element.98, bf16[512,1,2752]{0,2,1:T(8,128)(2,1)S(1)} %get-tuple-element.97), kind=kOutput, calls=%fused_computation.46 | convolution fusion | flops 11546591232 | bytes 30277632 | tf_op jit(solution)/shard_map/tcf,dcf->td/dot_general | solution.py:144
  491.1 10.8 convolution_convert_fusion.5
  501.9 50.4 %all-reduce.10.cloned.1.call-done = bf16[512,2048]{1,0:T(8,128)(2,1)} async-done(((bf16[512,2048]{1,0:T(8,128)(2,1)}), bf16[512,2048]{1,0:T(8,128)(2,1)}) %all-reduce.10.cloned.1.call-update) | async-done | bytes 2097168 | tf_op jit(solution)/shard_map/psum | solution.py:143
  552.4 4.1 fusion.12
  556.5 6.6 fusion.27
  563.3 1.4 fusion.23
  565.4 1.1 slice.135
  566.6 4.8 multiply_reduce_fusion
  571.4 11.3 multiply_convert_fusion
  582.7 4.1 multiply_bitcast_fusion
  588.1 1.1 slice.130
  590.0 1.6 stack.51
  591.6 2.3 copy.80
  593.9 2.3 copy.82
  597.0 1.7 reshape.317
  599.8 1.6 pad_maximum_fusion.9
  601.4 1.3 collective-permute-start.1
  602.7 4.4 multiply_convert_fusion.4
  607.1 2.3 copy.83
  609.4 1.5 copy.74
  610.9 1.3 copy.79
  613.4 1.7 fusion.43
  615.1 11.6 bitcast_convert_fusion
  627.9 7.6 convolution_convert_fusion.3
  635.5 6.4 copy.87
  642.0 11.1 convolution_convert_fusion.1
  653.0 15.2 %copy.91 = bf16[2752,2048]{0,1:T(8,128)(2,1)} copy(bf16[2752,2048]{1,0:T(8,128)(2,1)} %convolution_convert_fusion.1) | data formatting | bytes 22544384
  668.3 1.1 copy-done.8
  669.5 11.3 convolution_convert_fusion.2
  681.0 18.1 %convolution_convert_fusion = bf16[2048,2,2752]{0,2,1:T(8,128)(2,1)} fusion(bf16[512,1,2752]{0,2,1:T(8,128)(2,1)} %copy-done.26, bf16[512,1,2752]{0,2,1:T(8,128)(2,1)} %copy-done.25, bf16[512,2048]{1,0:T(8,128)(2,1)} %all-reduce.8.cloned.1.call-done, bf16[512,2048]{1,0:T(8,128)(2,1)S(1)} %copy-done.1, f32[2048]{0:T(1024)S(1)} %bitcast.157, f32[512]{0:T(512)S(1)} %copy-done.16), kind=kOutput, calls=%fused_computation | convolution fusion | flops 11571560448 | bytes 32385024 | tf_op jit(solution)/shard_map/td,tcf->dcf/dot_general | solution.py:142
  699.1 28.8 %copy.93 = bf16[2048,5504]{1,0:T(8,128)(2,1)} copy(bf16[2048,5504]{0,1:T(8,128)(2,1)} %bitcast.135) | data formatting | bytes 45088768
  729.8 6.4 all-reduce.12.cloned.1.call-done
  736.3 3.3 fusion.13
  739.6 62.0 %all-reduce.2 = (f32[2048]{0:T(1024)S(1)}, f32[2048]{0:T(1024)S(1)}) all-reduce(f32[2048]{0:T(1024)S(1)} %get-tuple-element.91, f32[2048]{0:T(1024)S(1)} %get-tuple-element.89), channel_id=2, replica_groups=mesh['seq'=16,'tp'=2] {'seq'}, use_global_device_ids=true, to_apply=%region_14.15.clone | all-reduce | flops 4096 | bytes 32768
  802.8 7.9 fusion.15
  810.7 2.6 reduce-scatter.13.cloned.1.call-done
  815.2 128.3 %reduce-scatter.17.cloned.1.call-done = bf16[128,2752]{1,0:T(8,128)(2,1)} async-done(((bf16[2048,2752]{1,0:T(8,128)(2,1)}), bf16[128,2752]{1,0:T(8,128)(2,1)}) %reduce-scatter.17.cloned.1.call-update) | async-done | bytes 704528
  943.5 1.5 copy.92
  945.0 1.2 convert_element_type.143
  946.2 135.4 %reduce-scatter.11.cloned.1.call-done = bf16[128,3,1024]{2,0,1:T(8,128)(2,1)} async-done(((bf16[2048,3,1024]{2,0,1:T(8,128)(2,1)}), bf16[128,3,1024]{2,0,1:T(8,128)(2,1)}) %reduce-scatter.11.cloned.1.call-update) | async-done | bytes 786448 | tf_op jit(solution)/shard_map/reduce_scatter | solution.py:22
  1081.6 2.5 convert_element_type.137
  1084.1 224.3 %reduce-scatter.15.cloned.1.call-done = bf16[128,5504]{1,0:T(8,128)(2,1)} async-done(((bf16[2048,5504]{1,0:T(8,128)(2,1)}), bf16[128,5504]{1,0:T(8,128)(2,1)}) %reduce-scatter.15.cloned.1.call-update) | async-done | bytes 1409040
  1308.3 2.2 copy.94
  1310.6 1.7 convert_element_type.141
  (126 shorter events, 20.1 us)
Async XLA Ops:
  7.2 106.2 %all-gather.7.cloned.1.call-start = ((), (), s32[]{:S(2)}) async-start(), calls=%async_computation.4 | async-start | bytes 13369344 | tf_op jit(solution)/shard_map/all_gather | solution.py:64
  7.9 159.6 %all-gather.9.cloned.1.call-start = ((), (), s32[]{:S(2)}) async-start(), calls=%async_computation.5 | async-start | bytes 4456448 | tf_op jit(solution)/shard_map/all_gather | solution.py:66
  8.7 226.1 %all-reduce.8.cloned.1.call-start = ((), (), s32[]{:S(2)}) async-start(), calls=%async_computation.6 | async-start | bytes 4194304 | tf_op jit(solution)/shard_map/psum | solution.py:106
  32.9 80.5 %copy-start.11 = (f32[16,1,128]{2,1,0:T(1,128)}, f32[16,1,128]{2,1,0:T(1,128)S(1)}, u32[]{:S(2)}) copy-start(f32[16,1,128]{2,1,0:T(1,128)S(1)} %convert_element_type.144) | copy-start | bytes 24580
  37.3 76.1 %copy-start.17 = (f32[512]{0:T(512)}, f32[512]{0:T(512)S(1)}, u32[]{:S(2)}) copy-start(f32[512]{0:T(512)S(1)} %fusion.16) | copy-start | bytes 6148
  37.3 76.1 %copy-start.13 = (f32[512]{0:T(512)}, f32[512]{0:T(512)S(1)}, u32[]{:S(2)}) copy-start(f32[512]{0:T(512)S(1)} %fusion.44) | copy-start | bytes 6148
  123.8 4.0 collective-permute-start
  127.3 1.2 copy-start.4
  127.6 1.1 copy-start.7
  128.5 3.3 copy-start.5
  130.4 3.5 copy-start
  136.2 31.3 %copy-start.22 = (bf16[8,128,512]{2,1,0:T(8,128)(2,1)}, bf16[8,128,512]{2,1,0:T(8,128)(2,1)S(1)}, u32[]{:S(2)}) copy-start(bf16[8,128,512]{2,1,0:T(8,128)(2,1)S(1)} %fusion.26) | copy-start | bytes 3145732
  173.4 1.2 copy-start.21
  173.4 61.3 %copy-start.1 = (bf16[512,2048]{1,0:T(8,128)(2,1)S(1)}, bf16[512,2048]{1,0:T(8,128)(2,1)}, u32[]{:S(2)}) copy-start(bf16[512,2048]{1,0:T(8,128)(2,1)} %param.13) | copy-start | bytes 6291460
  173.4 185.9 %all-gather.11.cloned.1.call-start = ((), (), s32[]{:S(2)}) async-start(), calls=%async_computation.7 | async-start | bytes 23953408 | tf_op jit(solution)/shard_map/all_gather | solution.py:111
  174.0 280.6 %all-gather.13.cloned.1.call-start = ((), (), s32[]{:S(2)}) async-start(), calls=%async_computation.8 | async-start | bytes 11976704 | tf_op jit(solution)/shard_map/all_gather | solution.py:113
  174.6 377.8 %all-reduce.10.cloned.1.call-start = ((), (), s32[]{:S(2)}) async-start(), calls=%async_computation.9 | async-start | bytes 4194304 | tf_op jit(solution)/shard_map/psum | solution.py:143
  237.1 319.4 %copy-start.15 = (f32[512]{0:T(512)}, f32[512]{0:T(512)S(1)}, u32[]{:S(2)}) copy-start(f32[512]{0:T(512)S(1)} %fusion.45) | copy-start | bytes 6148
  470.8 1.5 copy-start.25
  470.8 2.4 copy-start.26
  491.1 245.2 %all-reduce.12.cloned.1.call-start = ((), (), s32[]{:S(2)}) async-start(), calls=%async_computation.14 | async-start | bytes 8388608 | tf_op jit(solution)/shard_map/psum | solution.py:121
  552.4 4.1 copy-start.2
  552.4 10.8 slice-start
  556.5 6.7 copy-start.19
  556.5 6.7 slice-start.1
  556.5 6.7 slice-start.2
  563.2 3.3 copy-start.6
  564.7 6.7 copy-start.3
  582.7 6.6 copy-start.10
  586.7 9.4 slice-start.3
  601.4 11.0 collective-permute-start.1
  607.1 5.1 copy-start.9
  626.7 0.7 copy-start.16
  626.7 0.7 copy-start.20
  626.7 1.2 copy-start.23
  626.7 186.5 %reduce-scatter.13.cloned.1.call-start = ((), (), s32[]{:S(2)}) async-start(), calls=%async_computation.11 | async-start | bytes 4456448
  641.9 301.6 %reduce-scatter.17.cloned.1.call-start = ((), (), s32[]{:S(2)}) async-start(), calls=%async_computation.13 | async-start | bytes 12255232
  668.2 1.2 copy-start.8
  668.2 1.2 copy-start.12
  668.3 1.2 copy-start.14
  668.3 413.3 %reduce-scatter.11.cloned.1.call-start = ((), (), s32[]{:S(2)}) async-start(), calls=%async_computation.10 | async-start | bytes 13369344 | tf_op jit(solution)/shard_map/reduce_scatter | solution.py:22
  680.8 627.6 %reduce-scatter.15.cloned.1.call-start = ((), (), s32[]{:S(2)}) async-start(), calls=%async_computation.12 | async-start | bytes 23953408
  728.0 0.7 copy-start.24
  728.0 74.8 %copy-start.18 = (f32[512]{0:T(512)S(1)}, f32[512]{0:T(512)}, u32[]{:S(2)}) copy-start(f32[512]{0:T(512)} %copy-done.17) | copy-start | bytes 6148
Sparse Core Ops, SparseCore 0:
  10.2 103.1 all-gather.6
  115.5 51.9 all-gather.8
  173.5 61.1 all-reduce.7
  236.1 123.1 all-gather.10
  361.3 93.3 all-gather.12
  491.2 61.1 all-reduce.9
  626.9 109.3 all-reduce.11
  740.1 73.0 reduce-scatter.12
  817.4 126.0 reduce-scatter.16
  947.4 134.1 reduce-scatter.10
  1085.8 222.4 reduce-scatter.14

commit v2 on v0

v2 whole, which is shorter than its diff:
```python
import jax
import jax.numpy as jnp
from jax import lax
from jax.sharding import PartitionSpec as P

HEAD_DIM = 128
WINDOW = 64


EPSILON = 1e-05
NEGATIVE = -1e30


def shifted(block, axis, distance):
    devices = range(lax.axis_size(axis))
    route = [(i - distance, i) for i in devices if i - distance in devices]
    return lax.ppermute(block, axis, route)


def chip_at(place, chips):
    place = place % chips
    return jnp.where(place < chips // 2, 2 * place, 2 * chips - 1 - 2 * place)


def ring_routes(chips):
    cycle = list(range(0, chips, 2)) + list(range(1, chips, 2))[::-1]
    ahead = []
    for place in range(chips):
        for core in range(2):
            ahead.append((2 * cycle[place] + core, 2 * cycle[(place + 1) % chips] + core))
    return ahead, [(target, source) for source, target in ahead]


def ring_scatter(terms, chips, place):
    routes = ring_routes(chips)
    steps = (1, -1)

    def part(direction, offset):
        chip = chip_at(place - steps[direction] * offset, chips)
        start = (chip, direction, 0, 0)
        return lax.dynamic_slice(terms, start, (1, 1) + terms.shape[2:])[0, 0]

    sums = [part(direction, 1) for direction in range(2)]
    for hop in range(2, chips + 1):
        for direction in range(2):
            arrived = lax.ppermute(sums[direction], "seq", routes[direction])
            total = arrived.astype(jnp.float32) + part(direction, hop).astype(jnp.float32)
            sums[direction] = total if hop == chips else total.astype(jnp.bfloat16)
    return jnp.concatenate(sums, axis=0)


def partner(block):
    size = lax.axis_size("seq")
    return lax.ppermute(block, "seq", [(i, i ^ 1) for i in range(size)])


def pair_rows(block):
    return jnp.concatenate([block, partner(block)], axis=0)


def pair_columns(block, chips, core):
    split = block.reshape(block.shape[0], chips, 2, -1)
    kept = lax.dynamic_index_in_dim(split, core, 2, keepdims=False)
    given = lax.dynamic_index_in_dim(split, 1 - core, 2, keepdims=False)
    both = jnp.concatenate([kept, partner(given)], axis=0)
    return both.reshape(both.shape[0], -1)


def pair_terms(left, right, chips):
    terms = jnp.einsum("td,tf->df", left, right, preferred_element_type=jnp.float32)
    rows = left.shape[1] // chips
    return terms.astype(jnp.bfloat16).reshape(chips, 2, rows // 2, right.shape[1])


def tp_sum(partial):
    sent = lax.optimization_barrier(partial.astype(jnp.bfloat16))
    other = lax.ppermute(sent, "tp", [(0, 1), (1, 0)])
    return sent.astype(jnp.float32) + other.astype(jnp.float32)


def gather_small(block):
    size = lax.axis_size("seq")
    index = lax.axis_index("seq")
    bit = 1
    while bit < size:
        other = lax.ppermute(block, "seq", [(i, i ^ bit) for i in range(size)])
        low_side = jnp.concatenate([block, other], axis=-1)
        high_side = jnp.concatenate([other, block], axis=-1)
        block = jnp.where(index & bit != 0, high_side, low_side)
        bit *= 2
    return block


def scatter_small(block):
    size = lax.axis_size("seq")
    index = lax.axis_index("seq")
    bit = size // 2
    while bit > 0:
        low_side, high_side = jnp.split(block, 2)
        upper = index & bit != 0
        given = jnp.where(upper, low_side, high_side)
        other = lax.ppermute(given, "seq", [(i, i ^ bit) for i in range(size)])
        block = jnp.where(upper, high_side, low_side) + other
        bit //= 2
    return block


def windows(rows, count, span):
    return jnp.stack([rows[i * span : (i + 1) * span + WINDOW] for i in range(count)])


def rms_scale(values_in, gain_vec):
    return (
        values_in
        * lax.rsqrt(jnp.mean(values_in * values_in, axis=-1, keepdims=True) + EPSILON)
        * gain_vec
    )


def gated(gate_part, up_part):
    return gate_part / (1.0 + jnp.exp(-gate_part)) * up_part


def doc_starts(lengths, positions):
    doc_ends = jnp.cumsum(lengths)
    return jnp.sum(jnp.where(doc_ends[None, :] <= positions[:, None], lengths[None, :], 0), axis=1)


def local(tokens, doc_lengths, gain_one, w_qkv, w_out, gain_two, w_gate_up, w_down, cotangent):
    token_count = tokens.shape[0]
    width = tokens.shape[1]
    local_width = w_qkv.shape[2]
    heads = local_width // HEAD_DIM
    score_scale = HEAD_DIM ** (-0.5)
    span = 128
    count = token_count // span
    device = lax.axis_index("seq")
    chips = lax.axis_size("seq") // 2
    core = device % 2
    chip = device // 2
    place = jnp.where(chip % 2 == 0, chip // 2, chips - (chip + 1) // 2)
    row_length = token_count * lax.axis_size("seq") // doc_lengths.shape[0]
    lengths = doc_lengths[0]
    positions = (device * token_count) % row_length + jnp.arange(token_count, dtype=jnp.int32)
    starts = doc_starts(lengths, positions)
    f32 = jnp.float32
    bf16 = jnp.bfloat16

    gains = gather_small(jnp.stack([gain_one, gain_two])).astype(f32)
    gain_a = gains[0]
    gain_b = gains[1]
    qkv_full = lax.all_gather(w_qkv, "seq", axis=0, tiled=True)
    out_full = lax.all_gather(w_out.T, "seq", axis=0, tiled=True)
    down_full = lax.all_gather(w_down.T, "seq", axis=0, tiled=True)
    gate_up_full = lax.all_gather(w_gate_up, "seq", axis=0, tiled=True)

    token_rows = tokens.astype(f32)
    normed = rms_scale(token_rows, gain_a).astype(bf16)
    proj_qkv = jnp.einsum("td,dcf->tcf", normed, qkv_full, preferred_element_type=f32).astype(bf16)
    queries = proj_qkv[:, 0]
    key_rows = proj_qkv[:, 1]
    values = proj_qkv[:, 2]
    key_rim = jnp.stack([key_rows[token_count - WINDOW :], values[token_count - WINDOW :]])
    before = shifted(key_rim, "seq", 1)
    query_blocks = queries.reshape(count, span, heads, HEAD_DIM)
    key_blocks = windows(jnp.concatenate([before[0], key_rows]), count, span)
    key_blocks = key_blocks.reshape(count, span + WINDOW, heads, HEAD_DIM)
    value_blocks = windows(jnp.concatenate([before[1], values]), count, span)
    value_blocks = value_blocks.reshape(count, span + WINDOW, heads, HEAD_DIM)
    query_pos = positions.reshape(count, span, 1)
    key_pos = query_pos[:, :1] - WINDOW + jnp.arange(span + WINDOW, dtype=jnp.int32)
    mask = (
        (key_pos >= starts.reshape(count, span, 1))
        & (key_pos <= query_pos)
        & (query_pos - key_pos < WINDOW)
    )
    scores = (
        jnp.einsum("bqhd,bkhd->bhqk", query_blocks, key_blocks, preferred_element_type=f32)
        * score_scale
    )
    scores = jnp.where(mask[:, None], scores, NEGATIVE)
    exponent = jnp.exp(scores - jnp.max(scores, axis=-1, keepdims=True))
    probabilities = exponent / jnp.sum(exponent, axis=-1, keepdims=True)
    probs_low = probabilities.astype(bf16)
    attn_mixed = (
        jnp.einsum("bhqk,bkhd->bqhd", probs_low, value_blocks, preferred_element_type=f32)
        .reshape(token_count, local_width)
        .astype(bf16)
    )
    attn_out = tp_sum(jnp.einsum("tf,df->td", attn_mixed, out_full, preferred_element_type=f32))
    middle = token_rows + attn_out
    normed_two = rms_scale(middle, gain_b).astype(bf16)
    gate_up = jnp.einsum("td,dcf->tcf", normed_two, gate_up_full, preferred_element_type=f32)
    gate_part = gate_up[:, 0]
    up_part = gate_up[:, 1]
    hidden = gated(gate_part, up_part).astype(bf16)
    cot_pair = pair_columns(cotangent, chips, core)
    down_terms = pair_terms(cot_pair, pair_rows(hidden), chips)
    grad_w_down = ring_scatter(down_terms, chips, place).T

    grad_hidden = jnp.einsum("td,df->tf", cotangent, down_full, preferred_element_type=f32)
    unused_value, gate_pull = jax.vjp(gated, gate_part, up_part)
    grad_gate, grad_up = gate_pull(grad_hidden)
    grad_gate = grad_gate.astype(bf16)
    grad_up = grad_up.astype(bf16)
    normed_pair = pair_columns(normed_two, chips, core)
    gate_terms = pair_terms(normed_pair, pair_rows(grad_gate), chips)
    up_terms = pair_terms(normed_pair, pair_rows(grad_up), chips)
    grad_w_gate = ring_scatter(gate_terms, chips, place)
    grad_w_up = ring_scatter(up_terms, chips, place)
    grad_w_gate_up = jnp.stack([grad_w_gate, grad_w_up], axis=1)
    grad_gate_up = jnp.stack([grad_gate, grad_up], axis=1)
    grad_normed_two = tp_sum(
        jnp.einsum("tcf,dcf->td", grad_gate_up, gate_up_full, preferred_element_type=f32)
    )
    branch = tp_sum(jnp.einsum("tf,df->td", hidden, down_full, preferred_element_type=f32))
    result = (middle + branch).astype(bf16)

    unused_norm, norm_pull = jax.vjp(rms_scale, middle, gain_b)
    grad_mid_norm, grad_gain_two = norm_pull(grad_normed_two)
    grad_middle = cotangent.astype(f32) + grad_mid_norm
    grad_gain_two = scatter_small(grad_gain_two)
    grad_attn = grad_middle.astype(bf16)
    grad_mixed = jnp.einsum("td,df->tf", grad_attn, out_full, preferred_element_type=f32).astype(
        bf16
    )
    out_terms = pair_terms(pair_columns(grad_attn, chips, core), pair_rows(attn_mixed), chips)
    grad_w_out = ring_scatter(out_terms, chips, place).T

    grad_blocks = grad_mixed.reshape(count, span, heads, HEAD_DIM)
    grad_probs = jnp.einsum("bqhd,bkhd->bhqk", grad_blocks, value_blocks, preferred_element_type=f32)
    grad_value_win = jnp.einsum(
        "bhqk,bqhd->bkhd", probs_low, grad_blocks, preferred_element_type=f32
    )
    row_inner = jnp.sum(probabilities * grad_probs, axis=-1, keepdims=True)
    grad_scores = (probabilities * (grad_probs - row_inner)).astype(bf16)
    grad_queries = (
        jnp.einsum("bhqk,bkhd->bqhd", grad_scores, key_blocks, preferred_element_type=f32)
        * score_scale
    )
    grad_key_win = (
        jnp.einsum("bhqk,bqhd->bkhd", grad_scores, query_blocks, preferred_element_type=f32)
        * score_scale
    )
    grad_key_win = grad_key_win.reshape(count, span + WINDOW, local_width)
    grad_value_win = grad_value_win.reshape(count, span + WINDOW, local_width)
    edge_grads = jnp.stack([grad_key_win[0, :WINDOW], grad_value_win[0, :WINDOW]])
    arrived = shifted(edge_grads.astype(bf16), "seq", -1).astype(f32)

    def joined(grad_win, edge):
        tails = jnp.concatenate([grad_win[1:, :WINDOW], edge[None]])
        own = grad_win[:, WINDOW:]
        own = jnp.concatenate([own[:, : span - WINDOW], own[:, span - WINDOW :] + tails], axis=1)
        return own.reshape(token_count, local_width)

    grad_keys = joined(grad_key_win, arrived[0])
    grad_values = joined(grad_value_win, arrived[1])
    grad_queries = grad_queries.reshape(token_count, local_width)
    grad_proj = jnp.concatenate([grad_queries, grad_keys, grad_values], axis=1).astype(bf16)
    qkv_terms = pair_terms(pair_columns(normed, chips, core), pair_rows(grad_proj), chips)
    grad_w_qkv = ring_scatter(qkv_terms, chips, place).reshape(-1, 3, local_width)
    grad_normed = tp_sum(
        jnp.einsum(
            "tf,df->td",
            grad_proj,
            qkv_full.reshape(width, 3 * local_width),
            preferred_element_type=f32,
        )
    )
    unused_first, first_pull = jax.vjp(rms_scale, token_rows, gain_a)
    grad_rows_norm, grad_gain_one = first_pull(grad_normed)
    grad_tokens = grad_middle + grad_rows_norm
    grad_gain_one = scatter_small(grad_gain_one)
    return (
        result,
        grad_tokens,
        grad_gain_one,
        grad_w_qkv,
        grad_w_out,
        grad_gain_two,
        grad_w_gate_up,
        grad_w_down,
    )


def solution(mesh):
    return jax.shard_map(
        local,
        mesh=mesh,
        in_specs=(
            P("seq", None),
            P(),
            P("seq"),
            P("seq", None, "tp"),
            P("tp", "seq"),
            P("seq"),
            P("seq", None, "tp"),
            P("tp", "seq"),
            P("seq", None),
        ),
        out_specs=(
            P("seq", None),
            P("seq", None),
            P("seq"),
            P("seq", None, "tp"),
            P("tp", "seq"),
            P("seq"),
            P("seq", None, "tp"),
            P("tp", "seq"),
        ),
        check_vma=False,
    )
```

time: 1920 us -> 987 us (0.51)
  waiting for transfers between devices: 1530 us -> 475 us
  local copies, waits for them, and re-layouts: 37.3 us -> 173 us
  blocking collectives: 106 us -> 0 us
  starting transfers between devices: 4.11 us -> 99.7 us
  matrix products: 173 us -> 153 us
    reduce_scatter x4 -> x0, waiting for transfers between devices: 936 us -> none  [the longest x1 428 us: local(): lax.psum_scatter(mlp_terms[0], 'seq', scatter_dimension=0, tiled=True)]
    psum x4 -> x0, waiting for transfers between devices: 291 us -> none  [the longest x1 95.3 us: local(): lax.psum(jnp.einsum('tcf,dcf->td', grad_gate_up, gate_up_back, preferred_...]
    ppermute x0 -> x95, waiting for transfers between devices: none -> 229 us  [the longest x70 188 us: ring_scatter(): arrived = lax.ppermute(sums[direction], 'seq', routes[direction])]
    ppermute x0 -> x95, starting transfers between devices: none -> 95.9 us  [the longest x70 73.6 us: ring_scatter(): arrived = lax.ppermute(sums[direction], 'seq', routes[direction])]
    unnamed x1 -> x0, blocking collectives: 63.3 us -> none
    all_gather x4, waiting for transfers between devices: 302 us -> 244 us  [the longest x1 87.3 us: local(): qkv_full = lax.all_gather(w_qkv, 'seq', axis=0, tiled=True)]
    unnamed x66 -> x174, local copies, waits for them, and re-layouts: 13.2 us -> 55.8 us
    all_gather x2 -> x0, blocking collectives: 42.4 us -> none  [the longest x1 23.7 us: local(): lax.all_gather(gain_one, 'seq', axis=0, tiled=True)]
  transfers between devices with their start and end apart: 14 -> 101, of which waited for: 12 -> 45; matrix products, arithmetic and copies ran while one was open for 8% -> 38% of each run, Pallas kernels for 0% -> 0%
where the time goes in v2:
time: 987 us; the launch traced here: 979 us
  waiting for transfers between devices  475 us (48%)
  local copies, waits for them, and re-layouts  173 us (18%)
  matrix products  153 us (16%)
  starting transfers between devices  99.7 us (10%)
  other arithmetic  62.6 us (6%)
  between operations  15.5 us (2%)
    ppermute x70, waiting for transfers between devices, ring_scatter(): arrived = lax.ppermute(sums[direction], 'seq', routes[direction])  188 us
    all_gather x1, waiting for transfers between devices, local(): qkv_full = lax.all_gather(w_qkv, 'seq', axis=0, tiled=True)  87.3 us
    all_gather x1, waiting for transfers between devices, local(): down_full = lax.all_gather(w_down.T, 'seq', axis=0, tiled=True)  76 us
    ppermute x70, starting transfers between devices, ring_scatter(): arrived = lax.ppermute(sums[direction], 'seq', routes[direction])  73.6 us
    unnamed x174, local copies, waits for them, and re-layouts  55.8 us
    all_gather x1, waiting for transfers between devices, local(): gate_up_full = lax.all_gather(w_gate_up, 'seq', axis=0, tiled=True)  51.1 us
    dot_general x5, matrix products, pair_terms(): jnp.einsum('td,tf->df', left, right, preferred_element_type=jnp.float32)  50.7 us
    all_gather x1, waiting for transfers between devices, local(): out_full = lax.all_gather(w_out.T, 'seq', axis=0, tiled=True)  29.8 us
  transfers between devices with their start and end apart: 101, of which 45 were waited for; matrix products, arithmetic and copies ran while one was open for 38% of the time, Pallas kernels for 0%

profile of v2, /device:TPU:0, one launch (start us, length us, event | category | flops | bytes accessed | tf_op | source)
XLA Modules:
  0.0 978.8 jit_solution(14678882577125087326)
XLA Ops:
  26.1 87.3 %all-gather.5.cloned.1.call-done = bf16[2048,3,1024]{2,0,1:T(8,128)(2,1)} async-done(((bf16[128,3,1024]{2,0,1:T(8,128)(2,1)}), bf16[2048,3,1024]{2,0,1:T(8,128)(2,1)}) %all-gather.5.cloned.1.call-update) | async-done | bytes 12582928 | tf_op jit(solution)/shard_map/all_gather | solution.py:152
  113.4 10.3 %convolution_convert_fusion.6 = bf16[512,3,1024]{2,0,1:T(8,128)(2,1)S(1)} fusion(bf16[2048,3,1024]{2,0,1:T(8,128)(2,1)} %all-gather.5.cloned.1.call-done, bf16[512,2048]{1,0:T(8,128)(2,1)} %fusion.27), kind=kOutput, calls=%fused_computation.71 | convolution fusion | flops 6444023808 | bytes 17825792 | tf_op jit(solution)/shard_map/td,dcf->tcf/dot_general | solution.py:159
  137.8 29.8 %all-gather.7.cloned.1.call-done = bf16[2048,1024]{0,1:T(8,128)(2,1)} async-done(((bf16[128,1024]{0,1:T(8,128)(2,1)}), bf16[2048,1024]{0,1:T(8,128)(2,1)}) %all-gather.7.cloned.1.call-update) | async-done | bytes 4194320 | tf_op jit(solution)/shard_map/all_gather | solution.py:153
  167.6 6.2 convolution_convert_fusion.4
  175.2 4.0 copy.328
  184.7 4.4 reshape.399
  189.1 7.9 constant_dynamic-slice_fusion.25
  198.6 23.2 %collective-permute-done.5 = bf16[512,2048]{1,0:T(8,128)(2,1)} collective-permute-done((bf16[512,2048]{1,0:T(8,128)(2,1)}, bf16[512,2048]{1,0:T(8,128)(2,1)}, u32[]{:S(2)}, u32[]{:S(2)}) %collective-permute-start.5) | collective-permute-done | bytes 2097184 | tf_op jit(solution)/shard_map/ppermute | solution.py:77
  228.8 3.6 reshape.405
  232.5 5.7 constant_dynamic-slice_fusion.3
  239.3 51.1 %all-gather.9.cloned.1.call-done = bf16[2048,2,2752]{0,2,1:T(8,128)(2,1)} async-done(((bf16[128,2,2752]{0,2,1:T(8,128)(2,1)}), bf16[2048,2,2752]{0,2,1:T(8,128)(2,1)}) %all-gather.9.cloned.1.call-update) | async-done | bytes 22544400 | tf_op jit(solution)/shard_map/all_gather | solution.py:155
  290.4 19.4 %fusion.51 = f32[512,2,2752]{0,2,1:T(8,128)} fusion(bf16[2048,2,2752]{0,2,1:T(8,128)(2,1)} %all-gather.9.cloned.1.call-done, bf16[512,2048]{1,0:T(8,128)(2,1)} %multiply_convert_fusion.2), kind=kOutput, calls=%fused_computation.86 | convolution fusion | flops 11542724608 | bytes 35913728 | tf_op jit(solution)/shard_map/td,dcf->tcf/dot_general | solution.py:193
  309.8 76.0 %all-gather.11.cloned.1.call-done = bf16[2048,2752]{0,1:T(8,128)(2,1)} async-done(((bf16[128,2752]{0,1:T(8,128)(2,1)}), bf16[2048,2752]{0,1:T(8,128)(2,1)}) %all-gather.11.cloned.1.call-update) | async-done | bytes 11272208 | tf_op jit(solution)/shard_map/all_gather | solution.py:154
  385.8 16.4 %add_convert_fusion = (bf16[512,2752]{0,1:T(8,128)(2,1)S(1)}, bf16[512,2752]{0,1:T(8,128)(2,1)S(1)}, bf16[512,2752]{0,1:T(8,128)(2,1)}) fusion(f32[512,2,2752]{0,2,1:T(8,128)} %fusion.51, bf16[512,2048]{1,0:T(8,128)(2,1)S(1)} %copy-done.5, bf16[2048,2752]{0,1:T(8,128)(2,1)} %all-gather.11.cloned.1.call-done), kind=kOutput, calls=%fused_computation.36 | convolution fusion | flops 5796724736 | bytes 33095680 | tf_op jit(solution)/shard_map/td,df->tf/dot_general | solution.py:201
  402.2 19.7 %bitcast_convert_fusion = bf16[512,2048]{1,0:T(8,128)(2,1)} fusion(bf16[2048,2,2752]{0,2,1:T(8,128)(2,1)} %all-gather.9.cloned.1.call-done, bf16[512,1,2752]{0,2,1:T(8,128)(2,1)S(1)} %bitcast.530, bf16[512,1,2752]{0,2,1:T(8,128)(2,1)S(1)} %bitcast.529), kind=kOutput, calls=%fused_computation.48 | convolution fusion | flops 11546591232 | bytes 30277632 | tf_op jit(solution)/shard_map/tcf,dcf->td/dot_general | solution.py:214
  423.5 5.8 copy.335
  434.2 16.9 %copy.296 = bf16[2048,3,1024]{0,2,1:T(8,128)(2,1)} copy(bf16[2048,3,1024]{2,0,1:T(8,128)(2,1)} %all-gather.5.cloned.1.call-done) | data formatting | bytes 25165824 | tf_op jit(solution)/shard_map/all_gather | solution.py:152
  453.6 5.8 copy.355
  462.4 11.4 %convolution_convert_fusion.5 = bf16[512,2048]{1,0:T(8,128)(2,1)} fusion(bf16[512,2752]{0,1:T(8,128)(2,1)} %get-tuple-element.48, bf16[2048,2752]{0,1:T(8,128)(2,1)} %all-gather.11.cloned.1.call-done), kind=kOutput, calls=%fused_computation.68 | convolution fusion | flops 5772410880 | bytes 16187392 | tf_op jit(solution)/shard_map/tf,df->td/dot_general | solution.py:216
  473.9 3.6 multiply_reduce_fusion
  477.5 3.8 fusion.156
  503.5 6.3 constant_dynamic-slice_fusion.21
  522.6 4.2 copy.339
  532.9 11.1 %convolution_convert_fusion.3 = bf16[512,2048]{1,0:T(8,128)(2,1)} fusion(bf16[2048,3072]{0,1:T(8,128)(2,1)} %bitcast.451, bf16[512,1024]{1,0:T(8,128)(2,1)S(1)} %bitcast.473, bf16[512,1024]{1,0:T(8,128)(2,1)S(1)} %bitcast.476, bf16[512,1024]{1,0:T(8,128)(2,1)S(1)} %bitcast.470), kind=kOutput, calls=%fused_computation.66 | convolution fusion | flops 6452936704 | bytes 17825792 | tf_op jit(solution)/shard_map/tf,df->td/dot_general | solution.py:263
  547.6 9.7 convolution_convert_fusion.1
  557.2 8.4 copy.327
  569.1 9.9 %convolution_convert_fusion.2 = bf16[1024,2752]{0,1:T(8,128)(2,1)} fusion(bf16[512,2752]{0,1:T(8,128)(2,1)} %collective-permute-done.51, bf16[512,2752]{0,1:T(8,128)(2,1)} %copy-done.55, bf16[512,1024]{0,1:T(8,128)(2,1)} %bitcast.500, bf16[512,1024]{0,1:T(8,128)(2,1)S(1)} %bitcast.495), kind=kOutput, calls=%fused_computation.19 | convolution fusion | flops 5789646848 | bytes 13369344 | tf_op jit(solution)/shard_map/td,tf->df/dot_general | solution.py:70
  580.1 10.1 %convolution_convert_fusion = bf16[1024,2752]{0,1:T(8,128)(2,1)} fusion(bf16[512,2752]{0,1:T(8,128)(2,1)} %collective-permute-done.82, bf16[512,2752]{0,1:T(8,128)(2,1)S(1)} %copy-done.54, bf16[512,1024]{0,1:T(8,128)(2,1)S(1)} %bitcast.499, bf16[512,1024]{0,1:T(8,128)(2,1)S(1)} %bitcast.492), kind=kOutput, calls=%fused_computation.17 | convolution fusion | flops 5789646848 | bytes 13369344 | tf_op jit(solution)/shard_map/td,tf->df/dot_general | solution.py:70
  590.2 8.2 copy.326
  598.4 8.3 copy.331
  615.3 4.2 fusion.54
  637.5 6.8 collective-permute-done.59
  647.8 4.3 collective-permute-done.90
  657.8 11.6 %collective-permute-done.40 = bf16[64,1024]{0,1:T(8,128)(2,1)S(1)} collective-permute-done((bf16[64,1024]{0,1:T(8,128)(2,1)S(1)}, bf16[64,1024]{0,1:T(8,128)(2,1)S(1)}, u32[]{:S(2)}, u32[]{:S(2)}) %collective-permute-start.40) | collective-permute-done | bytes 131104 | tf_op jit(solution)/shard_map/ppermute | solution.py:46
  671.3 6.0 collective-permute-done.33
  682.5 4.9 collective-permute-done.53
  697.9 3.8 collective-permute-done.41
  703.9 8.8 collective-permute-done.42
  713.7 5.4 collective-permute-done.35
  720.0 5.4 collective-permute-done.43
  726.4 5.4 collective-permute-done.36
  734.2 8.6 collective-permute-done.54
  745.1 7.8 collective-permute-done.85
  755.1 4.8 collective-permute-done.44
  762.2 5.2 collective-permute-done.45
  768.5 5.3 collective-permute-done.38
  776.9 5.5 collective-permute-done.77
  784.7 4.0 fusion.28
  795.3 3.7 collective-permute-done.10
  801.6 5.2 collective-permute-done.11
  807.0 3.5 collective-permute-done.12
  810.7 9.9 %fusion.30 = (f32[512,2048]{1,0:T(8,128)}, bf16[512,2048]{1,0:T(8,128)(2,1)}) fusion(bf16[512,2048]{1,0:T(8,128)(2,1)S(1)} %copy-done.4, bf16[512,2048]{1,0:T(8,128)(2,1)} %collective-permute-done.9, bf16[512,2048]{1,0:T(8,128)(2,1)} %convolution_convert_fusion.3, f32[512]{0:T(512)S(1)} %multiply_multiply_fusion, f32[2048]{0:T(1024)S(1)} %bitcast.515, ...), kind=kLoop, calls=%fused_computation.45 | loop fusion | flops 26214400 | bytes 27287552 | tf_op jit(solution)/shard_map/add | solution.py:272
  825.5 6.4 collective-permute-done.63
  835.0 4.6 collective-permute-done.94
  842.7 4.6 collective-permute-done.79
  850.6 16.9 %fusion.9 = bf16[1024,3072]{1,0:T(8,128)(2,1)S(1)} fusion(bf16[512,3072]{1,0:T(8,128)(2,1)} %collective-permute-done.15, bf16[512,1024]{1,0:T(8,128)(2,1)S(1)} %bitcast.475, bf16[512,1024]{1,0:T(8,128)(2,1)} %bitcast.478, bf16[512,1024]{1,0:T(8,128)(2,1)S(1)} %bitcast.472, bf16[512,1024]{0,1:T(8,128)(2,1)} %bitcast.497, bf16[512,1024]{0,1:T(8,128)(2,1)} %bitcast.493), kind=kOutput, calls=%fused_computation.16 | convolution fusion | flops 6474956800 | bytes 14680064 | tf_op jit(solution)/shard_map/td,tf->df/dot_general | solution.py:70
  871.7 6.7 collective-permute-done.16
  884.3 12.0 %collective-permute-done.17 = bf16[64,3072]{1,0:T(8,128)(2,1)S(1)} collective-permute-done((bf16[64,3072]{1,0:T(8,128)(2,1)S(1)}, bf16[64,3072]{1,0:T(8,128)(2,1)S(1)}, u32[]{:S(2)}, u32[]{:S(2)}) %collective-permute-start.17) | collective-permute-done | bytes 393248 | tf_op jit(solution)/shard_map/ppermute | solution.py:46
  901.9 12.4 %collective-permute-done.18 = bf16[64,3072]{1,0:T(8,128)(2,1)S(1)} collective-permute-done((bf16[64,3072]{1,0:T(8,128)(2,1)S(1)}, bf16[64,3072]{1,0:T(8,128)(2,1)S(1)}, u32[]{:S(2)}, u32[]{:S(2)}) %collective-permute-start.18) | collective-permute-done | bytes 393248 | tf_op jit(solution)/shard_map/ppermute | solution.py:46
  916.8 5.6 collective-permute-done.19
  922.4 6.5 collective-permute-done.26
  932.6 6.7 collective-permute-done.20
  942.3 5.5 collective-permute-done.21
  947.7 6.1 collective-permute-done.28
  (484 shorter events, 250.7 us)
Async XLA Ops:
  7.2 106.2 %all-gather.5.cloned.1.call-start = ((), (), s32[]{:S(2)}) async-start(), calls=%async_computation | async-start | bytes 13369344 | tf_op jit(solution)/shard_map/all_gather | solution.py:152
  7.9 159.6 %all-gather.7.cloned.1.call-start = ((), (), s32[]{:S(2)}) async-start(), calls=%async_computation.1 | async-start | bytes 4456448 | tf_op jit(solution)/shard_map/all_gather | solution.py:153
  8.7 281.8 %all-gather.9.cloned.1.call-start = ((), (), s32[]{:S(2)}) async-start(), calls=%async_computation.2 | async-start | bytes 23953408 | tf_op jit(solution)/shard_map/all_gather | solution.py:155
  9.4 376.4 %all-gather.11.cloned.1.call-start = ((), (), s32[]{:S(2)}) async-start(), calls=%async_computation.3 | async-start | bytes 11976704 | tf_op jit(solution)/shard_map/all_gather | solution.py:154
  173.7 48.1 %collective-permute-start.5 = (bf16[512,2048]{1,0:T(8,128)(2,1)}, bf16[512,2048]{1,0:T(8,128)(2,1)}, u32[]{:S(2)}, u32[]{:S(2)}) collective-permute-start(bf16[512,2048]{1,0:T(8,128)(2,1)} %convolution_convert_fusion.4), channel_id=1, source_target_pairs={{0,1},{1,0},{2,3},{3,2},{4,5},{5,4},{6,7},{7,6},{8,9},{9,8},{10,11... | collective-permute-start | bytes 6291464 | tf_op jit(solution)/shard_map/ppermute | solution.py:77
  184.7 244.6 %collective-permute-start.81 = (bf16[512,8,128]{2,1,0:T(8,128)(2,1)}, bf16[512,8,128]{2,1,0:T(8,128)(2,1)}, u32[]{:S(2)}, u32[]{:S(2)}) collective-permute-start(bf16[512,8,128]{2,1,0:T(8,128)(2,1)} %bitcast.498), channel_id=1, source_target_pairs={{0,2},{2,0},{4,6},{6,4},{8,10},{10,8},{12,14},{14,12},{16,18},{18,... | collective-permute-start | bytes 3145736 | tf_op jit(solution)/shard_map/ppermute | solution.py:54
  198.1 233.6 %collective-permute-start.14 = (bf16[512,8,128]{2,1,0:T(8,128)(2,1)}, bf16[512,8,128]{2,1,0:T(8,128)(2,1)}, u32[]{:S(2)}, u32[]{:S(2)}) collective-permute-start(bf16[512,8,128]{2,1,0:T(8,128)(2,1)} %bitcast.418), channel_id=1, source_target_pairs={{0,2},{2,0},{4,6},{6,4},{8,10},{10,8},{12,14},{14,12},{16,18},{18,... | collective-permute-start | bytes 3145736 | tf_op jit(solution)/shard_map/ppermute | solution.py:54
  239.3 220.1 %collective-permute-start.50 = (bf16[512,8,128]{2,1,0:T(8,128)(2,1)}, bf16[512,8,128]{2,1,0:T(8,128)(2,1)}, u32[]{:S(2)}, u32[]{:S(2)}) collective-permute-start(bf16[512,8,128]{2,1,0:T(8,128)(2,1)} %bitcast.416), channel_id=1, source_target_pairs={{0,2},{2,0},{4,6},{6,4},{8,10},{10,8},{12,14},{14,12},{16,18},{18,... | collective-permute-start | bytes 3145736 | tf_op jit(solution)/shard_map/ppermute | solution.py:54
  422.0 51.9 %collective-permute-start.7 = (bf16[512,2048]{1,0:T(8,128)(2,1)}, bf16[512,2048]{1,0:T(8,128)(2,1)}, u32[]{:S(2)}, u32[]{:S(2)}) collective-permute-start(bf16[512,2048]{1,0:T(8,128)(2,1)} %bitcast_convert_fusion), channel_id=1, source_target_pairs={{0,1},{1,0},{2,3},{3,2},{4,5},{5,4},{6,7},{7,6},{8,9},{9,8},{10,11... | collective-permute-start | bytes 6291464 | tf_op jit(solution)/shard_map/ppermute | solution.py:77
  453.6 160.6 %collective-permute-start.31 = (bf16[512,1024]{1,0:T(8,128)(2,1)}, bf16[512,1024]{1,0:T(8,128)(2,1)}, u32[]{:S(2)}, u32[]{:S(2)}) collective-permute-start(bf16[512,1024]{1,0:T(8,128)(2,1)} %bitcast.415), channel_id=1, source_target_pairs={{0,2},{2,0},{4,6},{6,4},{8,10},{10,8},{12,14},{14,12},{16,18},{18,... | collective-permute-start | bytes 3145736 | tf_op jit(solution)/shard_map/ppermute | solution.py:54
  461.9 83.8 %collective-permute-start.66 = (bf16[512,2752]{0,1:T(8,128)(2,1)}, bf16[512,2752]{0,1:T(8,128)(2,1)}, u32[]{:S(2)}, u32[]{:S(2)}) collective-permute-start(bf16[512,2752]{0,1:T(8,128)(2,1)} %copy-done.56), channel_id=1, source_target_pairs={{0,2},{2,0},{4,6},{6,4},{8,10},{10,8},{12,14},{14,12},{16,18},{18,... | collective-permute-start | bytes 8454152 | tf_op jit(solution)/shard_map/ppermute | solution.py:54
  462.4 105.2 %collective-permute-start.51 = (bf16[512,2752]{0,1:T(8,128)(2,1)}, bf16[512,2752]{0,1:T(8,128)(2,1)}, u32[]{:S(2)}, u32[]{:S(2)}) collective-permute-start(bf16[512,2752]{0,1:T(8,128)(2,1)} %copy-done.55), channel_id=1, source_target_pairs={{0,2},{2,0},{4,6},{6,4},{8,10},{10,8},{12,14},{14,12},{16,18},{18,... | collective-permute-start | bytes 8454152 | tf_op jit(solution)/shard_map/ppermute | solution.py:54
  488.9 12.0 %collective-permute-start.46 = (f32[1024]{0:T(1024)S(1)}, f32[1024]{0:T(1024)S(1)}, u32[]{:S(2)}, u32[]{:S(2)}) collective-permute-start(f32[1024]{0:T(1024)S(1)} %slice_select_fusion), channel_id=1, source_target_pairs={{0,16},{2,18},{4,20},{6,22},{8,24},{10,26},{12,28},{14,30},{16,0},... | collective-permute-start | bytes 12296 | tf_op jit(solution)/shard_map/ppermute | solution.py:102
  499.4 28.3 %collective-permute-start.8 = (bf16[2,64,1024]{2,1,0:T(8,128)(2,1)}, bf16[2,64,1024]{2,1,0:T(8,128)(2,1)}, u32[]{:S(2)}, u32[]{:S(2)}) collective-permute-start(bf16[2,64,1024]{2,1,0:T(8,128)(2,1)} %pad_maximum_fusion.11), channel_id=1, source_target_pairs={{2,0},{4,2},{6,4},{8,6},{10,8},{12,10},{14,12},{16,14},{18,16},{20... | collective-permute-start | bytes 786440 | tf_op jit(solution)/shard_map/ppermute | solution.py:17
  513.5 13.3 %collective-permute-start.49 = (f32[128]{0:T(128)S(1)}, f32[128]{0:T(128)S(1)}, u32[]{:S(2)}, u32[]{:S(2)}) collective-permute-start(f32[128]{0:T(128)S(1)} %broadcast_select_fusion.6), channel_id=1, source_target_pairs={{0,2},{2,0},{4,6},{6,4},{8,10},{10,8},{12,14},{14,12},{16,18},{18,... | collective-permute-start | bytes 1544 | tf_op jit(solution)/shard_map/ppermute | solution.py:102
  526.8 52.3 %collective-permute-start.82 = (bf16[512,2752]{0,1:T(8,128)(2,1)}, bf16[512,2752]{0,1:T(8,128)(2,1)}, u32[]{:S(2)}, u32[]{:S(2)}) collective-permute-start(bf16[512,2752]{0,1:T(8,128)(2,1)} %get-tuple-element.48), channel_id=1, source_target_pairs={{0,2},{2,0},{4,6},{6,4},{8,10},{10,8},{12,14},{14,12},{16,18},{18,... | collective-permute-start | bytes 8454152 | tf_op jit(solution)/shard_map/ppermute | solution.py:54
  527.8 282.8 %collective-permute-start.6 = (bf16[512,2048]{1,0:T(8,128)(2,1)}, bf16[512,2048]{1,0:T(8,128)(2,1)}, u32[]{:S(2)}, u32[]{:S(2)}) collective-permute-start(bf16[512,2048]{1,0:T(8,128)(2,1)} %convolution_convert_fusion.5), channel_id=1, source_target_pairs={{0,1},{1,0},{2,3},{3,2},{4,5},{5,4},{6,7},{7,6},{8,9},{9,8},{10,11... | collective-permute-start | bytes 6291464 | tf_op jit(solution)/shard_map/ppermute | solution.py:77
  545.8 65.1 %collective-permute-start.30 = (bf16[512,8,128]{2,1,0:T(8,128)(2,1)}, bf16[512,8,128]{2,1,0:T(8,128)(2,1)}, u32[]{:S(2)}, u32[]{:S(2)}) collective-permute-start(bf16[512,8,128]{2,1,0:T(8,128)(2,1)} %bitcast.417), channel_id=1, source_target_pairs={{0,2},{2,0},{4,6},{6,4},{8,10},{10,8},{12,14},{14,12},{16,18},{18,... | collective-permute-start | bytes 3145736 | tf_op jit(solution)/shard_map/ppermute | solution.py:54
  567.6 216.0 %collective-permute-start.9 = (bf16[512,2048]{1,0:T(8,128)(2,1)}, bf16[512,2048]{1,0:T(8,128)(2,1)}, u32[]{:S(2)}, u32[]{:S(2)}) collective-permute-start(bf16[512,2048]{1,0:T(8,128)(2,1)} %convolution_convert_fusion.3), channel_id=1, source_target_pairs={{0,1},{1,0},{2,3},{3,2},{4,5},{5,4},{6,7},{7,6},{8,9},{9,8},{10,11... | collective-permute-start | bytes 6291464 | tf_op jit(solution)/shard_map/ppermute | solution.py:77
  579.0 53.8 %collective-permute-start.67 = (bf16[64,2752]{1,0:T(8,128)(2,1)}, bf16[64,2752]{1,0:T(8,128)(2,1)}, u32[]{:S(2)}, u32[]{:S(2)}) collective-permute-start(bf16[64,2752]{1,0:T(8,128)(2,1)} %get-tuple-element.111), channel_id=1, source_target_pairs={{0,8},{2,10},{8,16},{10,18},{16,24},{18,26},{24,28},{26,30},{28,20... | collective-permute-start | bytes 1056776 | tf_op jit(solution)/shard_map/ppermute | solution.py:46
  610.9 22.9 %collective-permute-start.74 = (bf16[64,2752]{1,0:T(8,128)(2,1)}, bf16[64,2752]{1,0:T(8,128)(2,1)}, u32[]{:S(2)}, u32[]{:S(2)}) collective-permute-start(bf16[64,2752]{1,0:T(8,128)(2,1)} %get-tuple-element.112), channel_id=1, source_target_pairs={{8,0},{10,2},{16,8},{18,10},{24,16},{26,18},{28,24},{30,26},{20,28... | collective-permute-start | bytes 1056776 | tf_op jit(solution)/shard_map/ppermute | solution.py:46
  614.2 22.3 %collective-permute-start.52 = (bf16[64,2752]{1,0:T(8,128)(2,1)}, bf16[64,2752]{1,0:T(8,128)(2,1)}, u32[]{:S(2)}, u32[]{:S(2)}) collective-permute-start(bf16[64,2752]{1,0:T(8,128)(2,1)} %get-tuple-element.95), channel_id=1, source_target_pairs={{0,8},{2,10},{8,16},{10,18},{16,24},{18,26},{24,28},{26,30},{28,20... | collective-permute-start | bytes 1056776 | tf_op jit(solution)/shard_map/ppermute | solution.py:46
  632.9 11.5 %collective-permute-start.59 = (bf16[64,2752]{1,0:T(8,128)(2,1)}, bf16[64,2752]{1,0:T(8,128)(2,1)S(1)}, u32[]{:S(2)}, u32[]{:S(2)}) collective-permute-start(bf16[64,2752]{1,0:T(8,128)(2,1)} %get-tuple-element.96), channel_id=1, source_target_pairs={{8,0},{10,2},{16,8},{18,10},{24,16},{26,18},{28,24},{30,26},{20,28... | collective-permute-start | bytes 1056776 | tf_op jit(solution)/shard_map/ppermute | solution.py:46
  633.8 12.9 %collective-permute-start.83 = (bf16[64,2752]{1,0:T(8,128)(2,1)}, bf16[64,2752]{1,0:T(8,128)(2,1)S(1)}, u32[]{:S(2)}, u32[]{:S(2)}) collective-permute-start(bf16[64,2752]{1,0:T(8,128)(2,1)} %get-tuple-element.79), channel_id=1, source_target_pairs={{0,8},{2,10},{8,16},{10,18},{16,24},{18,26},{24,28},{26,30},{28,20... | collective-permute-start | bytes 1056776 | tf_op jit(solution)/shard_map/ppermute | solution.py:46
  636.5 15.5 %collective-permute-start.90 = (bf16[64,2752]{1,0:T(8,128)(2,1)}, bf16[64,2752]{1,0:T(8,128)(2,1)S(1)}, u32[]{:S(2)}, u32[]{:S(2)}) collective-permute-start(bf16[64,2752]{1,0:T(8,128)(2,1)} %get-tuple-element.80), channel_id=1, source_target_pairs={{8,0},{10,2},{16,8},{18,10},{24,16},{26,18},{28,24},{30,26},{20,28... | collective-permute-start | bytes 1056776 | tf_op jit(solution)/shard_map/ppermute | solution.py:46
  644.4 11.2 %collective-permute-start.39 = (bf16[64,1024]{0,1:T(8,128)(2,1)}, bf16[64,1024]{0,1:T(8,128)(2,1)S(1)}, u32[]{:S(2)}, u32[]{:S(2)}) collective-permute-start(bf16[64,1024]{0,1:T(8,128)(2,1)} %bitcast.506), channel_id=1, source_target_pairs={{8,0},{10,2},{16,8},{18,10},{24,16},{26,18},{28,24},{30,26},{20,28... | collective-permute-start | bytes 393224 | tf_op jit(solution)/shard_map/ppermute | solution.py:46
  652.1 27.0 %collective-permute-start.68 = (bf16[64,2752]{1,0:T(8,128)(2,1)S(1)}, bf16[64,2752]{1,0:T(8,128)(2,1)S(1)}, u32[]{:S(2)}, u32[]{:S(2)}) collective-permute-start(bf16[64,2752]{1,0:T(8,128)(2,1)S(1)} %get-tuple-element.109), channel_id=1, source_target_pairs={{0,8},{2,10},{8,16},{10,18},{16,24},{18,26},{24,28},{26,30},{28,20... | collective-permute-start | bytes 1056776 | tf_op jit(solution)/shard_map/ppermute | solution.py:46
  655.6 23.9 %collective-permute-start.75 = (bf16[64,2752]{1,0:T(8,128)(2,1)S(1)}, bf16[64,2752]{1,0:T(8,128)(2,1)S(1)}, u32[]{:S(2)}, u32[]{:S(2)}) collective-permute-start(bf16[64,2752]{1,0:T(8,128)(2,1)S(1)} %get-tuple-element.110), channel_id=1, source_target_pairs={{8,0},{10,2},{16,8},{18,10},{24,16},{26,18},{28,24},{30,26},{20,28... | collective-permute-start | bytes 1056776 | tf_op jit(solution)/shard_map/ppermute | solution.py:46
  656.6 12.9 %collective-permute-start.40 = (bf16[64,1024]{0,1:T(8,128)(2,1)S(1)}, bf16[64,1024]{0,1:T(8,128)(2,1)S(1)}, u32[]{:S(2)}, u32[]{:S(2)}) collective-permute-start(bf16[64,1024]{0,1:T(8,128)(2,1)S(1)} %fusion.128), channel_id=1, source_target_pairs={{8,0},{10,2},{16,8},{18,10},{24,16},{26,18},{28,24},{30,26},{20,28... | collective-permute-start | bytes 393224 | tf_op jit(solution)/shard_map/ppermute | solution.py:46
  679.1 11.3 %collective-permute-start.60 = (bf16[64,2752]{1,0:T(8,128)(2,1)S(1)}, bf16[64,2752]{1,0:T(8,128)(2,1)S(1)}, u32[]{:S(2)}, u32[]{:S(2)}) collective-permute-start(bf16[64,2752]{1,0:T(8,128)(2,1)S(1)} %get-tuple-element.94), channel_id=1, source_target_pairs={{8,0},{10,2},{16,8},{18,10},{24,16},{26,18},{28,24},{30,26},{20,28... | collective-permute-start | bytes 1056776 | tf_op jit(solution)/shard_map/ppermute | solution.py:46
  679.5 14.1 %collective-permute-start.84 = (bf16[64,2752]{1,0:T(8,128)(2,1)S(1)}, bf16[64,2752]{1,0:T(8,128)(2,1)S(1)}, u32[]{:S(2)}, u32[]{:S(2)}) collective-permute-start(bf16[64,2752]{1,0:T(8,128)(2,1)S(1)} %get-tuple-element.77), channel_id=1, source_target_pairs={{0,8},{2,10},{8,16},{10,18},{16,24},{18,26},{24,28},{26,30},{28,20... | collective-permute-start | bytes 1056776 | tf_op jit(solution)/shard_map/ppermute | solution.py:46
  690.4 11.2 %collective-permute-start.41 = (bf16[64,1024]{0,1:T(8,128)(2,1)S(1)}, bf16[64,1024]{0,1:T(8,128)(2,1)S(1)}, u32[]{:S(2)}, u32[]{:S(2)}) collective-permute-start(bf16[64,1024]{0,1:T(8,128)(2,1)S(1)} %fusion.127), channel_id=1, source_target_pairs={{8,0},{10,2},{16,8},{18,10},{24,16},{26,18},{28,24},{30,26},{20,28... | collective-permute-start | bytes 393224 | tf_op jit(solution)/shard_map/ppermute | solution.py:46
  696.5 35.4 %collective-permute-start.69 = (bf16[64,2752]{1,0:T(8,128)(2,1)S(1)}, bf16[64,2752]{1,0:T(8,128)(2,1)S(1)}, u32[]{:S(2)}, u32[]{:S(2)}) collective-permute-start(bf16[64,2752]{1,0:T(8,128)(2,1)S(1)} %get-tuple-element.107), channel_id=1, source_target_pairs={{0,8},{2,10},{8,16},{10,18},{16,24},{18,26},{24,28},{26,30},{28,20... | collective-permute-start | bytes 1056776 | tf_op jit(solution)/shard_map/ppermute | solution.py:46
  701.6 31.2 %collective-permute-start.76 = (bf16[64,2752]{1,0:T(8,128)(2,1)S(1)}, bf16[64,2752]{1,0:T(8,128)(2,1)S(1)}, u32[]{:S(2)}, u32[]{:S(2)}) collective-permute-start(bf16[64,2752]{1,0:T(8,128)(2,1)S(1)} %get-tuple-element.108), channel_id=1, source_target_pairs={{8,0},{10,2},{16,8},{18,10},{24,16},{26,18},{28,24},{30,26},{20,28... | collective-permute-start | bytes 1056776 | tf_op jit(solution)/shard_map/ppermute | solution.py:46
  731.8 118.6 %collective-permute-start.15 = (bf16[512,3072]{1,0:T(8,128)(2,1)}, bf16[512,3072]{1,0:T(8,128)(2,1)}, u32[]{:S(2)}, u32[]{:S(2)}) collective-permute-start(bf16[512,3072]{1,0:T(8,128)(2,1)} %pad_maximum_fusion), channel_id=1, source_target_pairs={{0,2},{2,0},{4,6},{6,4},{8,10},{10,8},{12,14},{14,12},{16,18},{18,... | collective-permute-start | bytes 9437192 | tf_op jit(solution)/shard_map/ppermute | solution.py:54
  732.8 11.0 %collective-permute-start.61 = (bf16[64,2752]{1,0:T(8,128)(2,1)S(1)}, bf16[64,2752]{1,0:T(8,128)(2,1)S(1)}, u32[]{:S(2)}, u32[]{:S(2)}) collective-permute-start(bf16[64,2752]{1,0:T(8,128)(2,1)S(1)} %get-tuple-element.92), channel_id=1, source_target_pairs={{8,0},{10,2},{16,8},{18,10},{24,16},{26,18},{28,24},{30,26},{20,28... | collective-permute-start | bytes 1056776 | tf_op jit(solution)/shard_map/ppermute | solution.py:46
  759.9 16.0 %collective-permute-start.70 = (bf16[64,2752]{1,0:T(8,128)(2,1)S(1)}, bf16[64,2752]{1,0:T(8,128)(2,1)S(1)}, u32[]{:S(2)}, u32[]{:S(2)}) collective-permute-start(bf16[64,2752]{1,0:T(8,128)(2,1)S(1)} %get-tuple-element.105), channel_id=1, source_target_pairs={{0,8},{2,10},{8,16},{10,18},{16,24},{18,26},{24,28},{26,30},{28,20... | collective-permute-start | bytes 1056776 | tf_op jit(solution)/shard_map/ppermute | solution.py:46
  775.9 12.8 %collective-permute-start.55 = (bf16[64,2752]{1,0:T(8,128)(2,1)S(1)}, bf16[64,2752]{1,0:T(8,128)(2,1)S(1)}, u32[]{:S(2)}, u32[]{:S(2)}) collective-permute-start(bf16[64,2752]{1,0:T(8,128)(2,1)S(1)} %get-tuple-element.89), channel_id=1, source_target_pairs={{0,8},{2,10},{8,16},{10,18},{16,24},{18,26},{24,28},{26,30},{28,20... | collective-permute-start | bytes 1056776 | tf_op jit(solution)/shard_map/ppermute | solution.py:46
  783.6 15.7 %collective-permute-start.86 = (bf16[64,2752]{1,0:T(8,128)(2,1)S(1)}, bf16[64,2752]{1,0:T(8,128)(2,1)S(1)}, u32[]{:S(2)}, u32[]{:S(2)}) collective-permute-start(bf16[64,2752]{1,0:T(8,128)(2,1)S(1)} %get-tuple-element.73), channel_id=1, source_target_pairs={{0,8},{2,10},{8,16},{10,18},{16,24},{18,26},{24,28},{26,30},{28,20... | collective-permute-start | bytes 1056776 | tf_op jit(solution)/shard_map/ppermute | solution.py:46
  788.7 12.3 %collective-permute-start.93 = (bf16[64,2752]{1,0:T(8,128)(2,1)S(1)}, bf16[64,2752]{1,0:T(8,128)(2,1)S(1)}, u32[]{:S(2)}, u32[]{:S(2)}) collective-permute-start(bf16[64,2752]{1,0:T(8,128)(2,1)S(1)} %get-tuple-element.74), channel_id=1, source_target_pairs={{8,0},{10,2},{16,8},{18,10},{24,16},{26,18},{28,24},{30,26},{20,28... | collective-permute-start | bytes 1056776 | tf_op jit(solution)/shard_map/ppermute | solution.py:46
  799.0 24.2 %collective-permute-start.71 = (bf16[64,2752]{1,0:T(8,128)(2,1)S(1)}, bf16[64,2752]{1,0:T(8,128)(2,1)S(1)}, u32[]{:S(2)}, u32[]{:S(2)}) collective-permute-start(bf16[64,2752]{1,0:T(8,128)(2,1)S(1)} %get-tuple-element.103), channel_id=1, source_target_pairs={{0,8},{2,10},{8,16},{10,18},{16,24},{18,26},{24,28},{26,30},{28,20... | collective-permute-start | bytes 1056776 | tf_op jit(solution)/shard_map/ppermute | solution.py:46
  799.4 23.8 %collective-permute-start.78 = (bf16[64,2752]{1,0:T(8,128)(2,1)S(1)}, bf16[64,2752]{1,0:T(8,128)(2,1)S(1)}, u32[]{:S(2)}, u32[]{:S(2)}) collective-permute-start(bf16[64,2752]{1,0:T(8,128)(2,1)S(1)} %get-tuple-element.104), channel_id=1, source_target_pairs={{8,0},{10,2},{16,8},{18,10},{24,16},{26,18},{28,24},{30,26},{20,28... | collective-permute-start | bytes 1056776 | tf_op jit(solution)/shard_map/ppermute | solution.py:46
  810.5 14.8 %collective-permute-start.56 = (bf16[64,2752]{1,0:T(8,128)(2,1)S(1)}, bf16[64,2752]{1,0:T(8,128)(2,1)S(1)}, u32[]{:S(2)}, u32[]{:S(2)}) collective-permute-start(bf16[64,2752]{1,0:T(8,128)(2,1)S(1)} %get-tuple-element.87), channel_id=1, source_target_pairs={{0,8},{2,10},{8,16},{10,18},{16,24},{18,26},{24,28},{26,30},{28,20... | collective-permute-start | bytes 1056776 | tf_op jit(solution)/shard_map/ppermute | solution.py:46
  820.5 11.3 %collective-permute-start.63 = (bf16[64,2752]{1,0:T(8,128)(2,1)S(1)}, bf16[64,2752]{1,0:T(8,128)(2,1)S(1)}, u32[]{:S(2)}, u32[]{:S(2)}) collective-permute-start(bf16[64,2752]{1,0:T(8,128)(2,1)S(1)} %get-tuple-element.88), channel_id=1, source_target_pairs={{8,0},{10,2},{16,8},{18,10},{24,16},{26,18},{28,24},{30,26},{20,28... | collective-permute-start | bytes 1056776 | tf_op jit(solution)/shard_map/ppermute | solution.py:46
  823.1 11.8 %collective-permute-start.87 = (bf16[64,2752]{1,0:T(8,128)(2,1)S(1)}, bf16[64,2752]{1,0:T(8,128)(2,1)S(1)}, u32[]{:S(2)}, u32[]{:S(2)}) collective-permute-start(bf16[64,2752]{1,0:T(8,128)(2,1)S(1)} %get-tuple-element.71), channel_id=1, source_target_pairs={{0,8},{2,10},{8,16},{10,18},{16,24},{18,26},{24,28},{26,30},{28,20... | collective-permute-start | bytes 1056776 | tf_op jit(solution)/shard_map/ppermute | solution.py:46
  823.2 16.5 %collective-permute-start.94 = (bf16[64,2752]{1,0:T(8,128)(2,1)S(1)}, bf16[64,2752]{1,0:T(8,128)(2,1)S(1)}, u32[]{:S(2)}, u32[]{:S(2)}) collective-permute-start(bf16[64,2752]{1,0:T(8,128)(2,1)S(1)} %get-tuple-element.72), channel_id=1, source_target_pairs={{8,0},{10,2},{16,8},{18,10},{24,16},{26,18},{28,24},{30,26},{20,28... | collective-permute-start | bytes 1056776 | tf_op jit(solution)/shard_map/ppermute | solution.py:46
  825.3 17.3 %collective-permute-start.72 = (bf16[64,2752]{1,0:T(8,128)(2,1)S(1)}, bf16[64,2752]{1,0:T(8,128)(2,1)S(1)}, u32[]{:S(2)}, u32[]{:S(2)}) collective-permute-start(bf16[64,2752]{1,0:T(8,128)(2,1)S(1)} %get-tuple-element.101), channel_id=1, source_target_pairs={{0,8},{2,10},{8,16},{10,18},{16,24},{18,26},{24,28},{26,30},{28,20... | collective-permute-start | bytes 1056776 | tf_op jit(solution)/shard_map/ppermute | solution.py:46
  831.9 15.4 %collective-permute-start.79 = (bf16[64,2752]{1,0:T(8,128)(2,1)S(1)}, bf16[64,2752]{1,0:T(8,128)(2,1)S(1)}, u32[]{:S(2)}, u32[]{:S(2)}) collective-permute-start(bf16[64,2752]{1,0:T(8,128)(2,1)S(1)} %get-tuple-element.102), channel_id=1, source_target_pairs={{8,0},{10,2},{16,8},{18,10},{24,16},{26,18},{28,24},{30,26},{20,28... | collective-permute-start | bytes 1056776 | tf_op jit(solution)/shard_map/ppermute | solution.py:46
  835.0 33.4 %collective-permute-start.57 = (bf16[64,2752]{1,0:T(8,128)(2,1)}, bf16[64,2752]{1,0:T(8,128)(2,1)}, u32[]{:S(2)}, u32[]{:S(2)}) collective-permute-start(bf16[64,2752]{1,0:T(8,128)(2,1)} %get-tuple-element.85), channel_id=1, source_target_pairs={{0,8},{2,10},{8,16},{10,18},{16,24},{18,26},{24,28},{26,30},{28,20... | collective-permute-start | bytes 1056776 | tf_op jit(solution)/shard_map/ppermute | solution.py:46
  839.6 30.1 %collective-permute-start.64 = (bf16[64,2752]{1,0:T(8,128)(2,1)}, bf16[64,2752]{1,0:T(8,128)(2,1)}, u32[]{:S(2)}, u32[]{:S(2)}) collective-permute-start(bf16[64,2752]{1,0:T(8,128)(2,1)} %get-tuple-element.86), channel_id=1, source_target_pairs={{8,0},{10,2},{16,8},{18,10},{24,16},{26,18},{28,24},{30,26},{20,28... | collective-permute-start | bytes 1056776 | tf_op jit(solution)/shard_map/ppermute | solution.py:46
  842.7 38.2 %collective-permute-start.88 = (bf16[64,2752]{1,0:T(8,128)(2,1)}, bf16[64,2752]{1,0:T(8,128)(2,1)}, u32[]{:S(2)}, u32[]{:S(2)}) collective-permute-start(bf16[64,2752]{1,0:T(8,128)(2,1)} %get-tuple-element.69), channel_id=1, source_target_pairs={{0,8},{2,10},{8,16},{10,18},{16,24},{18,26},{24,28},{26,30},{28,20... | collective-permute-start | bytes 1056776 | tf_op jit(solution)/shard_map/ppermute | solution.py:46
  847.3 34.9 %collective-permute-start.95 = (bf16[64,2752]{1,0:T(8,128)(2,1)}, bf16[64,2752]{1,0:T(8,128)(2,1)}, u32[]{:S(2)}, u32[]{:S(2)}) collective-permute-start(bf16[64,2752]{1,0:T(8,128)(2,1)} %get-tuple-element.70), channel_id=1, source_target_pairs={{8,0},{10,2},{16,8},{18,10},{24,16},{26,18},{28,24},{30,26},{20,28... | collective-permute-start | bytes 1056776 | tf_op jit(solution)/shard_map/ppermute | solution.py:46
  850.4 48.2 %collective-permute-start.73 = (bf16[64,2752]{1,0:T(8,128)(2,1)}, bf16[64,2752]{1,0:T(8,128)(2,1)S(1)}, u32[]{:S(2)}, u32[]{:S(2)}) collective-permute-start(bf16[64,2752]{1,0:T(8,128)(2,1)} %get-tuple-element.99), channel_id=1, source_target_pairs={{0,8},{2,10},{8,16},{10,18},{16,24},{18,26},{24,28},{26,30},{28,20... | collective-permute-start | bytes 1056776 | tf_op jit(solution)/shard_map/ppermute | solution.py:46
  878.4 21.0 %collective-permute-start.80 = (bf16[64,2752]{1,0:T(8,128)(2,1)S(1)}, bf16[64,2752]{1,0:T(8,128)(2,1)S(1)}, u32[]{:S(2)}, u32[]{:S(2)}) collective-permute-start(bf16[64,2752]{1,0:T(8,128)(2,1)S(1)} %copy-done.40), channel_id=1, source_target_pairs={{8,0},{10,2},{16,8},{18,10},{24,16},{26,18},{28,24},{30,26},{20,28... | collective-permute-start | bytes 1056776 | tf_op jit(solution)/shard_map/ppermute | solution.py:46
  880.1 36.6 %collective-permute-start.58 = (bf16[64,2752]{1,0:T(8,128)(2,1)S(1)}, bf16[64,2752]{1,0:T(8,128)(2,1)S(1)}, u32[]{:S(2)}, u32[]{:S(2)}) collective-permute-start(bf16[64,2752]{1,0:T(8,128)(2,1)S(1)} %get-tuple-element.83), channel_id=1, source_target_pairs={{0,8},{2,10},{8,16},{10,18},{16,24},{18,26},{24,28},{26,30},{28,20... | collective-permute-start | bytes 1056776 | tf_op jit(solution)/shard_map/ppermute | solution.py:46
  880.9 15.4 %collective-permute-start.17 = (bf16[64,3072]{1,0:T(8,128)(2,1)S(1)}, bf16[64,3072]{1,0:T(8,128)(2,1)S(1)}, u32[]{:S(2)}, u32[]{:S(2)}) collective-permute-start(bf16[64,3072]{1,0:T(8,128)(2,1)S(1)} %get-tuple-element.63), channel_id=1, source_target_pairs={{0,8},{2,10},{8,16},{10,18},{16,24},{18,26},{24,28},{26,30},{28,20... | collective-permute-start | bytes 1179656 | tf_op jit(solution)/shard_map/ppermute | solution.py:46
  882.2 15.4 %collective-permute-start.24 = (bf16[64,3072]{1,0:T(8,128)(2,1)S(1)}, bf16[64,3072]{1,0:T(8,128)(2,1)S(1)}, u32[]{:S(2)}, u32[]{:S(2)}) collective-permute-start(bf16[64,3072]{1,0:T(8,128)(2,1)S(1)} %get-tuple-element.64), channel_id=1, source_target_pairs={{8,0},{10,2},{16,8},{18,10},{24,16},{26,18},{28,24},{30,26},{20,28... | collective-permute-start | bytes 1179656 | tf_op jit(solution)/shard_map/ppermute | solution.py:46
  896.3 20.3 %collective-permute-start.65 = (bf16[64,2752]{1,0:T(8,128)(2,1)S(1)}, bf16[64,2752]{1,0:T(8,128)(2,1)S(1)}, u32[]{:S(2)}, u32[]{:S(2)}) collective-permute-start(bf16[64,2752]{1,0:T(8,128)(2,1)S(1)} %get-tuple-element.84), channel_id=1, source_target_pairs={{8,0},{10,2},{16,8},{18,10},{24,16},{26,18},{28,24},{30,26},{20,28... | collective-permute-start | bytes 1056776 | tf_op jit(solution)/shard_map/ppermute | solution.py:46
  897.6 33.7 %collective-permute-start.89 = (bf16[64,2752]{1,0:T(8,128)(2,1)S(1)}, bf16[64,2752]{1,0:T(8,128)(2,1)S(1)}, u32[]{:S(2)}, u32[]{:S(2)}) collective-permute-start(bf16[64,2752]{1,0:T(8,128)(2,1)S(1)} %get-tuple-element.67), channel_id=1, source_target_pairs={{0,8},{2,10},{8,16},{10,18},{16,24},{18,26},{24,28},{26,30},{28,20... | collective-permute-start | bytes 1056776 | tf_op jit(solution)/shard_map/ppermute | solution.py:46
  898.5 15.8 %collective-permute-start.18 = (bf16[64,3072]{1,0:T(8,128)(2,1)S(1)}, bf16[64,3072]{1,0:T(8,128)(2,1)S(1)}, u32[]{:S(2)}, u32[]{:S(2)}) collective-permute-start(bf16[64,3072]{1,0:T(8,128)(2,1)S(1)} %get-tuple-element.61), channel_id=1, source_target_pairs={{0,8},{2,10},{8,16},{10,18},{16,24},{18,26},{24,28},{26,30},{28,20... | collective-permute-start | bytes 1179656 | tf_op jit(solution)/shard_map/ppermute | solution.py:46
  899.3 15.0 %collective-permute-start.25 = (bf16[64,3072]{1,0:T(8,128)(2,1)S(1)}, bf16[64,3072]{1,0:T(8,128)(2,1)S(1)}, u32[]{:S(2)}, u32[]{:S(2)}) collective-permute-start(bf16[64,3072]{1,0:T(8,128)(2,1)S(1)} %get-tuple-element.62), channel_id=1, source_target_pairs={{8,0},{10,2},{16,8},{18,10},{24,16},{26,18},{28,24},{30,26},{20,28... | collective-permute-start | bytes 1179656 | tf_op jit(solution)/shard_map/ppermute | solution.py:46
  914.3 17.0 %collective-permute-start.96 = (bf16[64,2752]{1,0:T(8,128)(2,1)S(1)}, bf16[64,2752]{1,0:T(8,128)(2,1)S(1)}, u32[]{:S(2)}, u32[]{:S(2)}) collective-permute-start(bf16[64,2752]{1,0:T(8,128)(2,1)S(1)} %get-tuple-element.68), channel_id=1, source_target_pairs={{8,0},{10,2},{16,8},{18,10},{24,16},{26,18},{28,24},{30,26},{20,28... | collective-permute-start | bytes 1056776 | tf_op jit(solution)/shard_map/ppermute | solution.py:46
  916.6 12.2 %collective-permute-start.26 = (bf16[64,3072]{1,0:T(8,128)(2,1)S(1)}, bf16[64,3072]{1,0:T(8,128)(2,1)S(1)}, u32[]{:S(2)}, u32[]{:S(2)}) collective-permute-start(bf16[64,3072]{1,0:T(8,128)(2,1)S(1)} %get-tuple-element.60), channel_id=1, source_target_pairs={{8,0},{10,2},{16,8},{18,10},{24,16},{26,18},{28,24},{30,26},{20,28... | collective-permute-start | bytes 1179656 | tf_op jit(solution)/shard_map/ppermute | solution.py:46
  941.6 12.3 %collective-permute-start.28 = (bf16[64,3072]{1,0:T(8,128)(2,1)S(1)}, bf16[64,3072]{1,0:T(8,128)(2,1)S(1)}, u32[]{:S(2)}, u32[]{:S(2)}) collective-permute-start(bf16[64,3072]{1,0:T(8,128)(2,1)S(1)} %get-tuple-element.56), channel_id=1, source_target_pairs={{8,0},{10,2},{16,8},{18,10},{24,16},{26,18},{28,24},{30,26},{20,28... | collective-permute-start | bytes 1179656 | tf_op jit(solution)/shard_map/ppermute | solution.py:46
  (101 other events, 1729.4 us)
Sparse Core Ops, SparseCore 0:
  10.2 103.1 all-gather.4
  115.6 51.9 all-gather.6
  169.1 121.3 all-gather.8
  292.5 93.3 all-gather.10

commit v3 on v2

v3 whole, which is shorter than its diff:
```python
import jax
import jax.numpy as jnp
from jax import lax
from jax.experimental import pallas as pl
from jax.experimental.pallas import tpu as pltpu
from jax.sharding import PartitionSpec as P

HEAD_DIM = 128
WINDOW = 64


EPSILON = 1e-05
NEGATIVE = -1e30


def shifted(block, axis, distance):
    devices = range(lax.axis_size(axis))
    route = [(i - distance, i) for i in devices if i - distance in devices]
    return lax.ppermute(block, axis, route)


def chip_at(place, chips):
    place = place % chips
    return jnp.where(place < chips // 2, 2 * place, 2 * chips - 1 - 2 * place)


def ring_routes(chips):
    cycle = list(range(0, chips, 2)) + list(range(1, chips, 2))[::-1]
    ahead = []
    for place in range(chips):
        for core in range(2):
            ahead.append((2 * cycle[place] + core, 2 * cycle[(place + 1) % chips] + core))
    return ahead, [(target, source) for source, target in ahead]


def ring_scatter(terms, chips, place):
    routes = ring_routes(chips)
    steps = (1, -1)

    def part(direction, offset):
        chip = chip_at(place - steps[direction] * offset, chips)
        start = (chip, direction, 0, 0, 0)
        return lax.dynamic_slice(terms, start, (1, 1) + terms.shape[2:])[0, 0]

    sums = [part(direction, 1) for direction in range(2)]
    for hop in range(2, chips + 1):
        for direction in range(2):
            arrived = lax.ppermute(sums[direction], "seq", routes[direction])
            total = arrived.astype(jnp.float32) + part(direction, hop).astype(jnp.float32)
            sums[direction] = total if hop == chips else total.astype(jnp.bfloat16)
    return jnp.concatenate(sums, axis=1)


def partner(block):
    size = lax.axis_size("seq")
    return lax.ppermute(block, "seq", [(i, i ^ 1) for i in range(size)])


def select_kernel(core_ref, own_ref, other_ref, kept_ref, given_ref):
    kept_ref[...] = own_ref[...]
    given_ref[...] = other_ref[...]


def pair_columns(block, chips, core):
    tokens, width = block.shape
    rows = width // (2 * chips)
    half = jax.ShapeDtypeStruct((tokens, width // 2), block.dtype)
    if rows % 128 == 0:
        kept, given = pl.pallas_call(
            select_kernel,
            grid_spec=pltpu.PrefetchScalarGridSpec(
                num_scalar_prefetch=1,
                grid=(chips,),
                in_specs=[
                    pl.BlockSpec((tokens, rows), lambda q, c: (0, 2 * q + c[0])),
                    pl.BlockSpec((tokens, rows), lambda q, c: (0, 2 * q + 1 - c[0])),
                ],
                out_specs=[pl.BlockSpec((tokens, rows), lambda q, c: (0, q))] * 2,
            ),
            out_shape=[half, half],
            name="select_columns",
        )(core.reshape(1), block, block)
    else:
        split = block.reshape(tokens, chips, 2, rows)
        kept = lax.dynamic_index_in_dim(split, core, 2, keepdims=False).reshape(half.shape)
        given = lax.dynamic_index_in_dim(split, 1 - core, 2, keepdims=False).reshape(half.shape)
    return kept, partner(given)


def pair_kernel(left_ref, left_two_ref, right_ref, right_two_ref, terms_ref):
    def product(left, right):
        return lax.dot_general(
            left, right, (((0,), (0,)), ((), ())), preferred_element_type=jnp.float32
        )

    total = product(left_ref[...], right_ref[0]) + product(left_two_ref[...], right_two_ref[0])
    terms_ref[...] = total.astype(jnp.bfloat16).reshape(terms_ref.shape)


def pair_terms(left, right, chips):
    planes, tokens, columns = right.shape
    rows = left[0].shape[1] // chips
    group = max(1, 256 // rows)
    left_spec = pl.BlockSpec((tokens, group * rows), lambda p, m: (0, m))
    right_spec = pl.BlockSpec((1, tokens, columns), lambda p, m: (p, 0, 0))
    return pl.pallas_call(
        pair_kernel,
        grid=(planes, chips // group),
        in_specs=[left_spec, left_spec, right_spec, right_spec],
        out_specs=pl.BlockSpec(
            (group, 2, 1, rows // 2, columns), lambda p, m: (m, 0, p, 0, 0)
        ),
        out_shape=jax.ShapeDtypeStruct((chips, 2, planes, rows // 2, columns), jnp.bfloat16),
        cost_estimate=pl.CostEstimate(
            flops=4 * planes * tokens * chips * rows * columns,
            bytes_accessed=2 * planes * columns * (2 * tokens + chips * rows),
            transcendentals=0,
        ),
        name="pair_terms",
    )(left[0], left[1], right, partner(right))


SPAN = 128


def block_scores(queries, keys, starts_ref, block):
    rows = pl.ds(block * SPAN, SPAN)
    scores = lax.dot_general(
        queries, keys, (((1,), (1,)), ((), ())), preferred_element_type=jnp.float32
    ) * (HEAD_DIM ** (-0.5))
    query_pos = block * SPAN + lax.broadcasted_iota(jnp.int32, scores.shape, 0)
    key_pos = block * SPAN - WINDOW + lax.broadcasted_iota(jnp.int32, scores.shape, 1)
    mask = (
        (key_pos >= starts_ref[rows, :])
        & (key_pos <= query_pos)
        & (query_pos - key_pos < WINDOW)
    )
    scores = jnp.where(mask, scores, NEGATIVE)
    exponent = jnp.exp(scores - jnp.max(scores, axis=-1, keepdims=True))
    return exponent / jnp.sum(exponent, axis=-1, keepdims=True)


def attend_kernel(starts_ref, proj_ref, before_ref, mixed_ref):
    count = proj_ref.shape[1] // SPAN
    keys = jnp.concatenate([before_ref[0], proj_ref[1]], axis=0)
    values = jnp.concatenate([before_ref[1], proj_ref[2]], axis=0)
    for block in range(count):
        rows = slice(block * SPAN, (block + 1) * SPAN)
        seen = slice(block * SPAN, (block + 1) * SPAN + WINDOW)
        probs = block_scores(proj_ref[0, rows], keys[seen], starts_ref, block)
        mixed = jnp.dot(
            probs.astype(jnp.bfloat16), values[seen], preferred_element_type=jnp.float32
        )
        mixed_ref[rows, :] = mixed.astype(jnp.bfloat16)


def attend_back_kernel(
    starts_ref, proj_ref, before_ref, grad_ref, out_ref, rim_ref, tail_ref, keys_ref, values_ref
):
    count = proj_ref.shape[1] // SPAN
    scale = HEAD_DIM ** (-0.5)
    keys = jnp.concatenate([before_ref[0], proj_ref[1]], axis=0)
    values = jnp.concatenate([before_ref[1], proj_ref[2]], axis=0)
    keys_ref[...] = jnp.zeros_like(keys_ref)
    values_ref[...] = jnp.zeros_like(values_ref)

    def crossed(left, right):
        return lax.dot_general(
            left, right, (((0,), (0,)), ((), ())), preferred_element_type=jnp.float32
        )

    for block in range(count):
        rows = slice(block * SPAN, (block + 1) * SPAN)
        seen = slice(block * SPAN, (block + 1) * SPAN + WINDOW)
        queries = proj_ref[0, rows]
        grads = grad_ref[rows, :]
        probs = block_scores(queries, keys[seen], starts_ref, block)
        grad_probs = lax.dot_general(
            grads, values[seen], (((1,), (1,)), ((), ())), preferred_element_type=jnp.float32
        )
        inner = jnp.sum(probs * grad_probs, axis=-1, keepdims=True)
        grad_scores = (probs * (grad_probs - inner)).astype(jnp.bfloat16)
        grad_queries = jnp.dot(grad_scores, keys[seen], preferred_element_type=jnp.float32)
        out_ref[0, rows] = (grad_queries * scale).astype(jnp.bfloat16)
        keys_ref[seen, :] += crossed(grad_scores, queries) * scale
        values_ref[seen, :] += crossed(probs.astype(jnp.bfloat16), grads)
    tokens = count * SPAN
    for plane, total_ref in enumerate((keys_ref, values_ref)):
        rim_ref[plane] = total_ref[:WINDOW, :].astype(jnp.bfloat16)
        out_ref[1 + plane] = total_ref[WINDOW:, :].astype(jnp.bfloat16)
        tail_ref[plane] = total_ref[tokens:, :]


def attend(starts, proj, before):
    planes, tokens, width = proj.shape
    return pl.pallas_call(
        attend_kernel,
        grid=(width // HEAD_DIM,),
        in_specs=[
            pl.BlockSpec((tokens, 1), lambda h: (0, 0)),
            pl.BlockSpec((planes, tokens, HEAD_DIM), lambda h: (0, 0, h)),
            pl.BlockSpec((2, WINDOW, HEAD_DIM), lambda h: (0, 0, h)),
        ],
        out_specs=pl.BlockSpec((tokens, HEAD_DIM), lambda h: (0, h)),
        out_shape=jax.ShapeDtypeStruct((tokens, width), jnp.bfloat16),
        name="attend",
    )(starts, proj, before)


def attend_back(starts, proj, before, grad_mixed):
    planes, tokens, width = proj.shape
    rim_spec = pl.BlockSpec((2, WINDOW, HEAD_DIM), lambda h: (0, 0, h))
    proj_spec = pl.BlockSpec((planes, tokens, HEAD_DIM), lambda h: (0, 0, h))
    return pl.pallas_call(
        attend_back_kernel,
        grid=(width // HEAD_DIM,),
        in_specs=[
            pl.BlockSpec((tokens, 1), lambda h: (0, 0)),
            proj_spec,
            rim_spec,
            pl.BlockSpec((tokens, HEAD_DIM), lambda h: (0, h)),
        ],
        out_specs=[proj_spec, rim_spec, rim_spec],
        out_shape=[
            jax.ShapeDtypeStruct(proj.shape, jnp.bfloat16),
            jax.ShapeDtypeStruct((2, WINDOW, width), jnp.bfloat16),
            jax.ShapeDtypeStruct((2, WINDOW, width), jnp.float32),
        ],
        scratch_shapes=[pltpu.VMEM((tokens + WINDOW, HEAD_DIM), jnp.float32)] * 2,
        name="attend_back",
    )(starts, proj, before, grad_mixed)


def tp_sum(partial):
    sent = lax.optimization_barrier(partial.astype(jnp.bfloat16))
    other = lax.ppermute(sent, "tp", [(0, 1), (1, 0)])
    return sent.astype(jnp.float32) + other.astype(jnp.float32)


def gather_small(block):
    size = lax.axis_size("seq")
    index = lax.axis_index("seq")
    bit = 1
    while bit < size:
        other = lax.ppermute(block, "seq", [(i, i ^ bit) for i in range(size)])
        low_side = jnp.concatenate([block, other], axis=-1)
        high_side = jnp.concatenate([other, block], axis=-1)
        block = jnp.where(index & bit != 0, high_side, low_side)
        bit *= 2
    return block


def scatter_small(block):
    size = lax.axis_size("seq")
    index = lax.axis_index("seq")
    bit = size // 2
    while bit > 0:
        low_side, high_side = jnp.split(block, 2)
        upper = index & bit != 0
        given = jnp.where(upper, low_side, high_side)
        other = lax.ppermute(given, "seq", [(i, i ^ bit) for i in range(size)])
        block = jnp.where(upper, high_side, low_side) + other
        bit //= 2
    return block


def rms_scale(values_in, gain_vec):
    return (
        values_in
        * lax.rsqrt(jnp.mean(values_in * values_in, axis=-1, keepdims=True) + EPSILON)
        * gain_vec
    )


def gated(gate_part, up_part):
    return gate_part / (1.0 + jnp.exp(-gate_part)) * up_part


def doc_starts(lengths, positions):
    doc_ends = jnp.cumsum(lengths)
    return jnp.sum(jnp.where(doc_ends[None, :] <= positions[:, None], lengths[None, :], 0), axis=1)


def local(tokens, doc_lengths, gain_one, w_qkv, w_out, gain_two, w_gate_up, w_down, cotangent):
    token_count = tokens.shape[0]
    device = lax.axis_index("seq")
    chips = lax.axis_size("seq") // 2
    core = device % 2
    chip = device // 2
    place = jnp.where(chip % 2 == 0, chip // 2, chips - (chip + 1) // 2)
    row_length = token_count * lax.axis_size("seq") // doc_lengths.shape[0]
    first = (device * token_count) % row_length
    positions = first + jnp.arange(token_count, dtype=jnp.int32)
    starts = (doc_starts(doc_lengths[0], positions) - first).reshape(token_count, 1)
    f32 = jnp.float32
    bf16 = jnp.bfloat16

    gains = gather_small(jnp.stack([gain_one, gain_two])).astype(f32)
    gain_a = gains[0]
    gain_b = gains[1]
    first_weights = lax.all_gather(
        jnp.concatenate([w_qkv, w_out.T[:, None]], axis=1), "seq", axis=0, tiled=True
    )
    second_weights = lax.all_gather(
        jnp.concatenate([w_gate_up, w_down.T[:, None]], axis=1), "seq", axis=0, tiled=True
    )
    qkv_full = first_weights[:, :3]
    out_full = first_weights[:, 3]
    gate_up_full = second_weights[:, :2]
    down_full = second_weights[:, 2]

    token_rows = tokens.astype(f32)
    normed = rms_scale(token_rows, gain_a).astype(bf16)
    proj = jnp.einsum("td,dcf->ctf", normed, qkv_full, preferred_element_type=f32).astype(bf16)
    before = shifted(proj[1:, token_count - WINDOW :], "seq", 1)
    attn_mixed = attend(starts, proj, before)
    attn_out = tp_sum(jnp.einsum("tf,df->td", attn_mixed, out_full, preferred_element_type=f32))
    middle = token_rows + attn_out
    normed_two = rms_scale(middle, gain_b).astype(bf16)
    gate_up = jnp.einsum("td,dcf->ctf", normed_two, gate_up_full, preferred_element_type=f32)
    gate_part = gate_up[0]
    up_part = gate_up[1]
    hidden = gated(gate_part, up_part).astype(bf16)
    down_terms = pair_terms(pair_columns(cotangent, chips, core), hidden[None], chips)
    grad_w_down = ring_scatter(down_terms, chips, place)[0].T

    grad_hidden = jnp.einsum("td,df->tf", cotangent, down_full, preferred_element_type=f32)
    unused_value, gate_pull = jax.vjp(gated, gate_part, up_part)
    grad_gate_up = jnp.stack(gate_pull(grad_hidden)).astype(bf16)
    gate_up_terms = pair_terms(pair_columns(normed_two, chips, core), grad_gate_up, chips)
    grad_w_gate_up = ring_scatter(gate_up_terms, chips, place).transpose(1, 0, 2)
    grad_normed_two = tp_sum(
        jnp.einsum("ctf,dcf->td", grad_gate_up, gate_up_full, preferred_element_type=f32)
    )
    branch = tp_sum(jnp.einsum("tf,df->td", hidden, down_full, preferred_element_type=f32))
    result = (middle + branch).astype(bf16)

    unused_norm, norm_pull = jax.vjp(rms_scale, middle, gain_b)
    grad_mid_norm, grad_gain_two = norm_pull(grad_normed_two)
    grad_middle = cotangent.astype(f32) + grad_mid_norm
    grad_gain_two = scatter_small(grad_gain_two)
    grad_attn = grad_middle.astype(bf16)
    grad_mixed = jnp.einsum("td,df->tf", grad_attn, out_full, preferred_element_type=f32).astype(
        bf16
    )
    out_terms = pair_terms(pair_columns(grad_attn, chips, core), attn_mixed[None], chips)
    grad_w_out = ring_scatter(out_terms, chips, place)[0].T

    grad_proj, rim, tail = attend_back(starts, proj, before, grad_mixed)
    arrived = shifted(rim, "seq", -1).astype(f32)
    grad_proj = grad_proj.at[1:, token_count - WINDOW :].set((tail + arrived).astype(bf16))
    qkv_terms = pair_terms(pair_columns(normed, chips, core), grad_proj, chips)
    grad_w_qkv = ring_scatter(qkv_terms, chips, place).transpose(1, 0, 2)
    grad_normed = tp_sum(
        jnp.einsum("ctf,dcf->td", grad_proj, qkv_full, preferred_element_type=f32)
    )
    unused_first, first_pull = jax.vjp(rms_scale, token_rows, gain_a)
    grad_rows_norm, grad_gain_one = first_pull(grad_normed)
    grad_tokens = grad_middle + grad_rows_norm
    grad_gain_one = scatter_small(grad_gain_one)
    return (
        result,
        grad_tokens,
        grad_gain_one,
        grad_w_qkv,
        grad_w_out,
        grad_gain_two,
        grad_w_gate_up,
        grad_w_down,
    )


def solution(mesh):
    return jax.shard_map(
        local,
        mesh=mesh,
        in_specs=(
            P("seq", None),
            P(),
            P("seq"),
            P("seq", None, "tp"),
            P("tp", "seq"),
            P("seq"),
            P("seq", None, "tp"),
            P("tp", "seq"),
            P("seq", None),
        ),
        out_specs=(
            P("seq", None),
            P("seq", None),
            P("seq"),
            P("seq", None, "tp"),
            P("tp", "seq"),
            P("seq"),
            P("seq", None, "tp"),
            P("tp", "seq"),
        ),
        check_vma=False,
    )
```

time: 987 us -> 847 us (0.86)
  local copies, waits for them, and re-layouts: 173 us -> 44.5 us
  Pallas kernels: 0 us -> 106 us
  matrix products: 153 us -> 91.5 us
  waiting for transfers between devices: 475 us -> 417 us
  other arithmetic: 62.6 us -> 82.4 us
  starting transfers between devices: 99.7 us -> 84.6 us
    pallas_call x0 -> x10, Pallas kernels: none -> 106 us  [the longest x4 52.5 us: pair_terms(): pl.pallas_call(pair_kernel, grid=(planes, chips // group), in_specs=[left...]
    dot_general x15 -> x4, matrix products: 117 us -> 58.2 us  [the longest x1 19 us: local(): jnp.einsum('ctf,dcf->td', grad_gate_up, gate_up_full, preferred_element_t...]
    all_gather x4 -> x2, waiting for transfers between devices: 244 us -> 200 us  [the longest x1 109 us: local(): lax.all_gather(jnp.concatenate([w_qkv, w_out.T[:, None]], axis=1), 'seq',...]
    unnamed x174 -> x64, local copies, waits for them, and re-layouts: 55.8 us -> 12.9 us
    ppermute x70 -> x56, waiting for transfers between devices: 188 us -> 151 us  [ring_scatter(): arrived = lax.ppermute(sums[direction], 'seq', routes[direction])]
    dynamic_slice x9 -> x0, local copies, waits for them, and re-layouts: 29 us -> none  [the longest x4 23 us: pair_columns(): kept = lax.dynamic_index_in_dim(split, core, 2, keepdims=False)]
    ppermute x4, waiting for transfers between devices: 23.2 us -> 51.9 us  [tp_sum(): other = lax.ppermute(sent, 'tp', [(0, 1), (1, 0)])]
    convert_element_type x4 -> x1, local copies, waits for them, and re-layouts: 27.3 us -> 4.52 us  [local(): hidden = gated(gate_part, up_part).astype(bf16)]
  transfers between devices with their start and end apart: 101 -> 84, of which waited for: 45 -> 48; matrix products, arithmetic and copies ran while one was open for 38% -> 24% of each run, Pallas kernels for 0% -> 13%
where the time goes in v3:
time: 847 us; the launch traced here: 841 us
  waiting for transfers between devices  417 us (49%)
  Pallas kernels  106 us (13%)
  matrix products  91.5 us (11%)
  starting transfers between devices  84.6 us (10%)
  other arithmetic  82.4 us (10%)
  local copies, waits for them, and re-layouts  44.5 us (5%)
  between operations  15.1 us (2%)
    ppermute x56, waiting for transfers between devices, ring_scatter(): arrived = lax.ppermute(sums[direction], 'seq', routes[direction])  151 us
    all_gather x1, waiting for transfers between devices, local(): lax.all_gather(jnp.concatenate([w_qkv, w_out.T[:, None]], axis=1), 'seq',...  109 us
    all_gather x1, waiting for transfers between devices, local(): lax.all_gather(jnp.concatenate([w_gate_up, w_down.T[:, None]], axis=1), '...  91.1 us
    ppermute x56, starting transfers between devices, ring_scatter(): arrived = lax.ppermute(sums[direction], 'seq', routes[direction])  55 us
    pallas_call x4, Pallas kernels, pair_terms(): pl.pallas_call(pair_kernel, grid=(planes, chips // group), in_specs=[left...  52.5 us
    ppermute x4, waiting for transfers between devices, tp_sum(): other = lax.ppermute(sent, 'tp', [(0, 1), (1, 0)])  51.9 us
    convert_element_type x24, other arithmetic, ring_scatter(): sums[direction] = total if hop == chips else total.astype(jnp.bfloat16)  25.3 us
    pallas_call x4, Pallas kernels, pair_columns(): pl.pallas_call(select_kernel, grid_spec=pltpu.PrefetchScalarGridSpec(num_...  23.6 us
  transfers between devices with their start and end apart: 84, of which 48 were waited for; matrix products, arithmetic and copies ran while one was open for 24% of the time, Pallas kernels for 13%

profile of v3, /device:TPU:0, one launch (start us, length us, event | category | flops | bytes accessed | tf_op | source)
XLA Modules:
  0.0 841.2 jit_solution(7333748003834342349)
XLA Ops:
  23.0 3.1 collective-permute-start.3
  30.8 109.2 %all-gather.3.cloned.1.call-done = bf16[2048,4,1024]{2,0,1:T(8,128)(2,1)} async-done(((bf16[128,4,1024]{2,0,1:T(8,128)(2,1)}), bf16[2048,4,1024]{2,0,1:T(8,128)(2,1)}) %all-gather.3.cloned.1.call-update) | async-done | bytes 16777232 | tf_op jit(solution)/shard_map/all_gather | solution.py:301
  140.0 10.3 %convert_bitcast_fusion.proj_ref = bf16[3,512,1024]{2,1,0:T(8,128)(2,1)S(1)} fusion(bf16[2048,4,1024]{2,0,1:T(8,128)(2,1)} %all-gather.3.cloned.1.call-done, bf16[512,2048]{1,0:T(8,128)(2,1)} %fusion.18.own_ref.other_ref), kind=kOutput, calls=%fused_computation.53 | convolution fusion | flops 6444023808 | bytes 17825792 | tf_op jit(solution)/shard_map/td,dcf->ctf/dot_general | solution.py:314
  156.1 12.3 %attend.1 = bf16[512,1024]{1,0:T(8,128)(2,1)} custom-call(s32[512,1]{1,0:T(8,128)} %copy.51.starts_ref, bf16[3,512,1024]{2,1,0:T(8,128)(2,1)} %copy-done.7, bf16[2,64,1024]{2,1,0:T(8,128)(2,1)} %copy-done.12), custom_call_target="tpu_custom_call" | custom-call | tf_op jit(solution)/shard_map/attend/pallas_call | solution.py:196
  168.4 6.2 fusion.33
  176.1 6.0 select_columns.7
  182.1 8.0 collective-permute-start.66
  190.1 5.8 select_columns.4
  196.2 19.8 %collective-permute-done.5 = bf16[512,2048]{1,0:T(8,128)(2,1)} collective-permute-done((bf16[512,2048]{1,0:T(8,128)(2,1)}, bf16[512,2048]{1,0:T(8,128)(2,1)}, u32[]{:S(2)}, u32[]{:S(2)}) %collective-permute-start.5) | collective-permute-done | bytes 2097184 | tf_op jit(solution)/shard_map/ppermute | solution.py:236
  216.1 3.2 multiply_reduce_fusion.2
  223.0 5.9 select_columns.6
  228.9 91.1 %all-gather.5.cloned.1.call-done = bf16[2048,3,2752]{0,2,1:T(8,128)(2,1)} async-done(((bf16[128,3,2752]{0,2,1:T(8,128)(2,1)}), bf16[2048,3,2752]{0,2,1:T(8,128)(2,1)}) %all-gather.5.cloned.1.call-update) | async-done | bytes 33816592 | tf_op jit(solution)/shard_map/all_gather | solution.py:304
  320.1 17.1 %convolution_bitcast_fusion = f32[2,512,2752]{2,1,0:T(8,128)S(1)} fusion(bf16[2048,3,2752]{0,2,1:T(8,128)(2,1)} %all-gather.5.cloned.1.call-done, bf16[512,2048]{1,0:T(8,128)(2,1)} %multiply_convert_fusion.1.own_ref.other_ref), kind=kOutput, calls=%fused_computation.14 | convolution fusion | flops 11542724608 | bytes 47185920 | tf_op jit(solution)/shard_map/td,dcf->ctf/dot_general | solution.py:320
  340.1 9.9 %fusion.6 = f32[2752,512]{0,1:T(8,128)S(1)} fusion(bf16[512,2048]{1,0:T(8,128)(2,1)S(1)} %copy-done.4, bf16[2048,3,2752]{0,2,1:T(8,128)(2,1)} %all-gather.5.cloned.1.call-done), kind=kOutput, calls=%fused_computation.7 | convolution fusion | flops 5771362304 | bytes 19005440 | tf_op jit(solution)/shard_map/td,df->tf/dot_general | solution.py:327
  350.1 5.3 fusion.36
  355.3 19.0 %bitcast_convert_fusion.1 = bf16[512,2048]{1,0:T(8,128)(2,1)} fusion(bf16[2048,3,2752]{0,2,1:T(8,128)(2,1)} %all-gather.5.cloned.1.call-done, bf16[1,512,2752]{2,1,0:T(8,128)(2,1)} %get-tuple-element.81, bf16[1,512,2752]{2,1,0:T(8,128)(2,1)} %get-tuple-element.80), kind=kOutput, calls=%fused_computation.41 | convolution fusion | flops 11546591232 | bytes 30408704 | tf_op jit(solution)/shard_map/ctf,dcf->td/dot_general | solution.py:333
  375.9 4.5 copy.58
  380.4 11.0 %fusion.32 = bf16[512,2048]{1,0:T(8,128)(2,1)} fusion(bf16[2048,3,2752]{0,2,1:T(8,128)(2,1)} %all-gather.5.cloned.1.call-done, bf16[1,512,2752]{2,1,0:T(8,128)(2,1)} %multiply_convert_fusion.right_ref), kind=kOutput, calls=%fused_computation.54 | convolution fusion | flops 5772410880 | bytes 16252928 | tf_op jit(solution)/shard_map/tf,df->td/dot_general | solution.py:335
  391.4 3.0 pad_maximum_fusion.right_ref
  394.4 8.4 %copy.56 = bf16[2,512,2752]{1,2,0:T(8,128)(2,1)} copy(bf16[2,512,2752]{2,1,0:T(8,128)(2,1)} %pad_maximum_fusion.right_ref) | data formatting | bytes 11272192 | tf_op jit(solution)/shard_map/stack | solution.py:329
  402.8 19.7 %collective-permute-done.7 = bf16[512,2048]{1,0:T(8,128)(2,1)} collective-permute-done((bf16[512,2048]{1,0:T(8,128)(2,1)}, bf16[512,2048]{1,0:T(8,128)(2,1)}, u32[]{:S(2)}, u32[]{:S(2)}) %collective-permute-start.7) | collective-permute-done | bytes 2097184 | tf_op jit(solution)/shard_map/ppermute | solution.py:236
  422.5 4.8 multiply_reduce_fusion
  428.0 3.9 collective-permute-done.46
  432.5 5.1 fusion.96.own_ref.other_ref
  437.6 5.9 select_columns.5
  444.2 6.1 fusion.41.grad_ref
  450.3 17.6 %attend_back.1 = (bf16[3,512,1024]{2,1,0:T(8,128)(2,1)}, bf16[2,64,1024]{2,1,0:T(8,128)(2,1)}, f32[2,64,1024]{2,1,0:T(8,128)}) custom-call(s32[512,1]{1,0:T(8,128)} %copy.51.starts_ref, bf16[3,512,1024]{2,1,0:T(8,128)(2,1)} %copy-done.7, bf16[2,64,1024]{2,1,0:T(8,128)(2,1)} %copy-done.12, bf16[512,1024]{1,0:T(8,128)(2,1)} %fusion.41.grad_ref), custom_call_target="tpu_custom_call" | custom-call | tf_op jit(solution)/shard_map/attend_back/pallas_call | solution.py:214
  469.5 4.6 copy.59.right_two_ref
  474.1 6.0 pair_terms.5
  481.1 3.4 collective-permute-start.32
  484.6 10.9 %pair_terms.7 = bf16[8,2,1,64,2752]{4,3,2,1,0:T(8,128)(2,1)} custom-call(bf16[512,1024]{1,0:T(8,128)(2,1)} %get-tuple-element.40.left_ref, bf16[512,1024]{1,0:T(8,128)(2,1)} %collective-permute-done.66.left_two_ref, bf16[1,512,2752]{2,1,0:T(8,128)(2,1)} %multiply_convert_fusion.right_ref, bf16[1,512,2752]{2,1,0:T(8,128)(2,1)} %copy.59.right_two_ref), custom_call_target="tpu_custom_call" | custom-call | flops 5771362304 | bytes 11272192 | tf_op jit(solution)/shard_map/pair_terms/pallas_call | solution.py:106
  508.3 3.8 collective-permute-done.34
  524.4 11.8 %bitcast_convert_fusion = bf16[512,2048]{1,0:T(8,128)(2,1)} fusion(bf16[3,512,1024]{2,1,0:T(8,128)(2,1)} %fusion.78.right_ref, bf16[2048,4,1024]{2,0,1:T(8,128)(2,1)} %all-gather.3.cloned.1.call-done), kind=kOutput, calls=%fused_computation.40 | convolution fusion | flops 6443499520 | bytes 17825792 | tf_op jit(solution)/shard_map/ctf,dcf->td/dot_general | solution.py:355
  544.8 7.8 collective-permute-done.44
  561.8 7.1 collective-permute-done.71
  572.1 12.4 %collective-permute-done.9 = bf16[512,2048]{1,0:T(8,128)(2,1)} collective-permute-done((bf16[512,2048]{1,0:T(8,128)(2,1)}, bf16[512,2048]{1,0:T(8,128)(2,1)}, u32[]{:S(2)}, u32[]{:S(2)}) %collective-permute-start.9) | collective-permute-done | bytes 2097184 | tf_op jit(solution)/shard_map/ppermute | solution.py:236
  584.5 3.9 fusion.19
  588.6 4.5 collective-permute-done.10
  595.5 15.7 %pair_terms.4 = bf16[8,2,3,64,1024]{4,3,2,1,0:T(8,128)(2,1)} custom-call(bf16[512,1024]{1,0:T(8,128)(2,1)} %get-tuple-element.34.left_ref, bf16[512,1024]{1,0:T(8,128)(2,1)} %copy-done.24, bf16[3,512,1024]{2,1,0:T(8,128)(2,1)} %fusion.78.right_ref, bf16[3,512,1024]{2,1,0:T(8,128)(2,1)} %collective-permute-done.15.right_two_ref), custom_call_target="tpu_custom_call" | custom-call | flops 6442450944 | bytes 12582912 | tf_op jit(solution)/shard_map/pair_terms/pallas_call | solution.py:106
  614.4 8.4 copy.57.right_two_ref
  622.8 19.9 %pair_terms.6 = bf16[8,2,2,64,2752]{4,3,2,1,0:T(8,128)(2,1)} custom-call(bf16[512,1024]{1,0:T(8,128)(2,1)} %get-tuple-element.38.left_ref, bf16[512,1024]{1,0:T(8,128)(2,1)} %collective-permute-done.50.left_two_ref, bf16[2,512,2752]{2,1,0:T(8,128)(2,1)} %pad_maximum_fusion.right_ref, bf16[2,512,2752]{2,1,0:T(8,128)(2,1)} %copy.57.right_two_ref), custom_call_target="tpu_custom_call" | custom-call | flops 11542724608 | bytes 22544384 | tf_op jit(solution)/shard_map/pair_terms/pallas_call | solution.py:106
  649.5 13.7 %collective-permute-done.52 = bf16[2,64,2752]{2,1,0:T(8,128)(2,1)S(1)} collective-permute-done((bf16[2,64,2752]{2,1,0:T(8,128)(2,1)S(1)}, bf16[2,64,2752]{2,1,0:T(8,128)(2,1)S(1)}, u32[]{:S(2)}, u32[]{:S(2)}) %collective-permute-start.52) | collective-permute-done | bytes 704544 | tf_op jit(solution)/shard_map/ppermute | solution.py:48
  667.5 4.2 collective-permute-done.17
  671.7 3.5 collective-permute-done.24
  678.7 8.5 %collective-permute-done.53 = bf16[2,64,2752]{2,1,0:T(8,128)(2,1)S(1)} collective-permute-done((bf16[2,64,2752]{2,1,0:T(8,128)(2,1)S(1)}, bf16[2,64,2752]{2,1,0:T(8,128)(2,1)S(1)}, u32[]{:S(2)}, u32[]{:S(2)}) %collective-permute-start.53) | collective-permute-done | bytes 704544 | tf_op jit(solution)/shard_map/ppermute | solution.py:48
  692.5 9.8 %fusion.21 = (f32[512,2048]{1,0:T(8,128)}, bf16[512,2048]{1,0:T(8,128)(2,1)}) fusion(bf16[512,2048]{1,0:T(8,128)(2,1)S(1)} %copy-done.3, bf16[512,2048]{1,0:T(8,128)(2,1)} %collective-permute-done.9, bf16[512,2048]{1,0:T(8,128)(2,1)} %bitcast_convert_fusion, f32[512]{0:T(512)S(1)} %multiply_multiply_fusion, f32[2048]{0:T(1024)S(1)} %bitcast.312, ...), kind=kLoop, calls=%fused_computation.36 | loop fusion | flops 26214400 | bytes 27287552 | tf_op jit(solution)/shard_map/add | solution.py:359
  708.0 3.0 collective-permute-done.54
  711.4 3.6 collective-permute-done.61
  719.2 3.6 collective-permute-done.79
  727.6 3.6 collective-permute-done.26
  732.6 10.0 %collective-permute-done.55 = bf16[2,64,2752]{2,1,0:T(8,128)(2,1)S(1)} collective-permute-done((bf16[2,64,2752]{2,1,0:T(8,128)(2,1)S(1)}, bf16[2,64,2752]{2,1,0:T(8,128)(2,1)S(1)}, u32[]{:S(2)}, u32[]{:S(2)}) %collective-permute-start.55) | collective-permute-done | bytes 704544 | tf_op jit(solution)/shard_map/ppermute | solution.py:48
  743.0 3.6 collective-permute-done.62
  750.8 3.6 collective-permute-done.80
  759.2 3.6 collective-permute-done.27
  764.2 10.0 %collective-permute-done.56 = bf16[2,64,2752]{2,1,0:T(8,128)(2,1)S(1)} collective-permute-done((bf16[2,64,2752]{2,1,0:T(8,128)(2,1)S(1)}, bf16[2,64,2752]{2,1,0:T(8,128)(2,1)S(1)}, u32[]{:S(2)}, u32[]{:S(2)}) %collective-permute-start.56) | collective-permute-done | bytes 704544 | tf_op jit(solution)/shard_map/ppermute | solution.py:48
  774.6 3.6 collective-permute-done.63
  782.4 3.6 collective-permute-done.81
  787.2 3.2 collective-permute-done.21
  790.4 4.0 collective-permute-done.28
  797.6 8.2 collective-permute-done.57
  805.8 4.0 collective-permute-done.64
  814.7 3.7 collective-permute-done.29
  821.2 5.1 collective-permute-done.58
  830.6 3.4 copy.61
  (280 shorter events, 160.8 us)
Async XLA Ops:
  7.2 132.9 %all-gather.3.cloned.1.call-start = ((), (), s32[]{:S(2)}) async-start(), calls=%async_computation | async-start | bytes 17825792 | tf_op jit(solution)/shard_map/all_gather | solution.py:301
  10.6 309.4 %all-gather.5.cloned.1.call-start = ((), (), s32[]{:S(2)}) async-start(), calls=%async_computation.1 | async-start | bytes 35930112 | tf_op jit(solution)/shard_map/all_gather | solution.py:304
  174.6 41.4 %collective-permute-start.5 = (bf16[512,2048]{1,0:T(8,128)(2,1)}, bf16[512,2048]{1,0:T(8,128)(2,1)}, u32[]{:S(2)}, u32[]{:S(2)}) collective-permute-start(bf16[512,2048]{1,0:T(8,128)(2,1)} %fusion.33), channel_id=1, source_target_pairs={{0,1},{1,0},{2,3},{3,2},{4,5},{5,4},{6,7},{7,6},{8,9},{9,8},{10,11... | collective-permute-start | bytes 6291464 | tf_op jit(solution)/shard_map/ppermute | solution.py:236
  182.1 302.5 %collective-permute-start.66 = (bf16[512,1024]{1,0:T(8,128)(2,1)}, bf16[512,1024]{1,0:T(8,128)(2,1)}, u32[]{:S(2)}, u32[]{:S(2)}) collective-permute-start(bf16[512,1024]{1,0:T(8,128)(2,1)} %get-tuple-element.41), channel_id=1, source_target_pairs={{0,2},{2,0},{4,6},{6,4},{8,10},{10,8},{12,14},{14,12},{16,18},{18,... | collective-permute-start | bytes 3145736 | tf_op jit(solution)/shard_map/ppermute | solution.py:56
  196.0 278.2 %collective-permute-start.31 = (bf16[1,512,1024]{2,1,0:T(8,128)(2,1)S(1)}, bf16[1,512,1024]{2,1,0:T(8,128)(2,1)}, u32[]{:S(2)}, u32[]{:S(2)}) collective-permute-start(bf16[1,512,1024]{2,1,0:T(8,128)(2,1)S(1)} %bitcast.303), channel_id=1, source_target_pairs={{0,2},{2,0},{4,6},{6,4},{8,10},{10,8},{12,14},{14,12},{16,18},{18,... | collective-permute-start | bytes 3145736 | tf_op jit(solution)/shard_map/ppermute | solution.py:56
  374.4 48.1 %collective-permute-start.7 = (bf16[512,2048]{1,0:T(8,128)(2,1)}, bf16[512,2048]{1,0:T(8,128)(2,1)}, u32[]{:S(2)}, u32[]{:S(2)}) collective-permute-start(bf16[512,2048]{1,0:T(8,128)(2,1)} %bitcast_convert_fusion.1), channel_id=1, source_target_pairs={{0,1},{1,0},{2,3},{3,2},{4,5},{5,4},{6,7},{7,6},{8,9},{9,8},{10,11... | collective-permute-start | bytes 6291464 | tf_op jit(solution)/shard_map/ppermute | solution.py:236
  391.4 76.9 %collective-permute-start.67 = (bf16[1,512,2752]{1,2,0:T(8,128)(2,1)}, bf16[1,512,2752]{1,2,0:T(8,128)(2,1)}, u32[]{:S(2)}, u32[]{:S(2)}) collective-permute-start(bf16[1,512,2752]{1,2,0:T(8,128)(2,1)} %copy.58), channel_id=1, source_target_pairs={{0,2},{2,0},{4,6},{6,4},{8,10},{10,8},{12,14},{14,12},{16,18},{18,... | collective-permute-start | bytes 8454152 | tf_op jit(solution)/shard_map/ppermute | solution.py:56
  431.9 11.5 %collective-permute-start.47 = (f32[512]{0:T(512)S(1)}, f32[512]{0:T(512)S(1)}, u32[]{:S(2)}, u32[]{:S(2)}) collective-permute-start(f32[512]{0:T(512)S(1)} %slice_select_fusion.2), channel_id=1, source_target_pairs={{0,8},{2,10},{4,12},{6,14},{8,0},{10,2},{12,4},{14,6},{16,24},{18,... | collective-permute-start | bytes 6152 | tf_op jit(solution)/shard_map/ppermute | solution.py:261
  443.5 30.7 %collective-permute-start.30 = (bf16[512,1024]{1,0:T(8,128)(2,1)}, bf16[512,1024]{1,0:T(8,128)(2,1)}, u32[]{:S(2)}, u32[]{:S(2)}) collective-permute-start(bf16[512,1024]{1,0:T(8,128)(2,1)} %get-tuple-element.37), channel_id=1, source_target_pairs={{0,2},{2,0},{4,6},{6,4},{8,10},{10,8},{12,14},{14,12},{16,18},{18,... | collective-permute-start | bytes 3145736 | tf_op jit(solution)/shard_map/ppermute | solution.py:56
  443.5 24.5 %collective-permute-start.48 = (f32[256]{0:T(256)S(1)}, f32[256]{0:T(256)S(1)}, u32[]{:S(2)}, u32[]{:S(2)}) collective-permute-start(f32[256]{0:T(256)S(1)} %broadcast_select_fusion.4), channel_id=1, source_target_pairs={{0,4},{2,6},{4,0},{6,2},{8,12},{10,14},{12,8},{14,10},{16,20},{18,... | collective-permute-start | bytes 3080 | tf_op jit(solution)/shard_map/ppermute | solution.py:261
  467.9 145.6 %collective-permute-start.51 = (bf16[2,512,2752]{1,2,0:T(8,128)(2,1)}, bf16[2,512,2752]{1,2,0:T(8,128)(2,1)}, u32[]{:S(2)}, u32[]{:S(2)}) collective-permute-start(bf16[2,512,2752]{1,2,0:T(8,128)(2,1)} %copy.56), channel_id=1, source_target_pairs={{0,2},{2,0},{4,6},{6,4},{8,10},{10,8},{12,14},{14,12},{16,18},{18,... | collective-permute-start | bytes 16908296 | tf_op jit(solution)/shard_map/ppermute | solution.py:56
  468.2 38.9 %collective-permute-start.8 = (bf16[2,64,1024]{2,1,0:T(8,128)(2,1)}, bf16[2,64,1024]{2,1,0:T(8,128)(2,1)S(1)}, u32[]{:S(2)}, u32[]{:S(2)}) collective-permute-start(bf16[2,64,1024]{2,1,0:T(8,128)(2,1)} %get-tuple-element.33), channel_id=1, source_target_pairs={{2,0},{4,2},{6,4},{8,6},{10,8},{12,10},{14,12},{16,14},{18,16},{20... | collective-permute-start | bytes 786440 | tf_op jit(solution)/shard_map/ppermute | solution.py:19
  481.1 14.3 %collective-permute-start.32 = (bf16[1,64,1024]{2,1,0:T(8,128)(2,1)S(1)}, bf16[1,64,1024]{2,1,0:T(8,128)(2,1)S(1)}, u32[]{:S(2)}, u32[]{:S(2)}) collective-permute-start(bf16[1,64,1024]{2,1,0:T(8,128)(2,1)S(1)} %get-tuple-element.146), channel_id=1, source_target_pairs={{0,8},{2,10},{8,16},{10,18},{16,24},{18,26},{24,28},{26,30},{28,20... | collective-permute-start | bytes 393224 | tf_op jit(solution)/shard_map/ppermute | solution.py:48
  484.5 10.9 %collective-permute-start.39 = (bf16[1,64,1024]{2,1,0:T(8,128)(2,1)S(1)}, bf16[1,64,1024]{2,1,0:T(8,128)(2,1)S(1)}, u32[]{:S(2)}, u32[]{:S(2)}) collective-permute-start(bf16[1,64,1024]{2,1,0:T(8,128)(2,1)S(1)} %get-tuple-element.147), channel_id=1, source_target_pairs={{8,0},{10,2},{16,8},{18,10},{24,16},{26,18},{28,24},{30,26},{20,28... | collective-permute-start | bytes 393224 | tf_op jit(solution)/shard_map/ppermute | solution.py:48
  499.8 16.5 %collective-permute-start.68 = (bf16[1,64,2752]{2,1,0:T(8,128)(2,1)S(1)}, bf16[1,64,2752]{2,1,0:T(8,128)(2,1)S(1)}, u32[]{:S(2)}, u32[]{:S(2)}) collective-permute-start(bf16[1,64,2752]{2,1,0:T(8,128)(2,1)S(1)} %get-tuple-element.128), channel_id=1, source_target_pairs={{0,8},{2,10},{8,16},{10,18},{16,24},{18,26},{24,28},{26,30},{28,20... | collective-permute-start | bytes 1056776 | tf_op jit(solution)/shard_map/ppermute | solution.py:48
  501.9 14.4 %collective-permute-start.75 = (bf16[1,64,2752]{2,1,0:T(8,128)(2,1)S(1)}, bf16[1,64,2752]{2,1,0:T(8,128)(2,1)S(1)}, u32[]{:S(2)}, u32[]{:S(2)}) collective-permute-start(bf16[1,64,2752]{2,1,0:T(8,128)(2,1)S(1)} %get-tuple-element.129), channel_id=1, source_target_pairs={{8,0},{10,2},{16,8},{18,10},{24,16},{26,18},{28,24},{30,26},{20,28... | collective-permute-start | bytes 1056776 | tf_op jit(solution)/shard_map/ppermute | solution.py:48
  517.6 20.2 %collective-permute-start.69 = (bf16[1,64,2752]{2,1,0:T(8,128)(2,1)S(1)}, bf16[1,64,2752]{2,1,0:T(8,128)(2,1)S(1)}, u32[]{:S(2)}, u32[]{:S(2)}) collective-permute-start(bf16[1,64,2752]{2,1,0:T(8,128)(2,1)S(1)} %get-tuple-element.126), channel_id=1, source_target_pairs={{0,8},{2,10},{8,16},{10,18},{16,24},{18,26},{24,28},{26,30},{28,20... | collective-permute-start | bytes 1056776 | tf_op jit(solution)/shard_map/ppermute | solution.py:48
  519.2 18.7 %collective-permute-start.76 = (bf16[1,64,2752]{2,1,0:T(8,128)(2,1)S(1)}, bf16[1,64,2752]{2,1,0:T(8,128)(2,1)S(1)}, u32[]{:S(2)}, u32[]{:S(2)}) collective-permute-start(bf16[1,64,2752]{2,1,0:T(8,128)(2,1)S(1)} %get-tuple-element.127), channel_id=1, source_target_pairs={{8,0},{10,2},{16,8},{18,10},{24,16},{26,18},{28,24},{30,26},{20,28... | collective-permute-start | bytes 1056776 | tf_op jit(solution)/shard_map/ppermute | solution.py:48
  522.3 13.9 %collective-permute-start.36 = (bf16[1,64,1024]{2,1,0:T(8,128)(2,1)S(1)}, bf16[1,64,1024]{2,1,0:T(8,128)(2,1)S(1)}, u32[]{:S(2)}, u32[]{:S(2)}) collective-permute-start(bf16[1,64,1024]{2,1,0:T(8,128)(2,1)S(1)} %get-tuple-element.138), channel_id=1, source_target_pairs={{0,8},{2,10},{8,16},{10,18},{16,24},{18,26},{24,28},{26,30},{28,20... | collective-permute-start | bytes 393224 | tf_op jit(solution)/shard_map/ppermute | solution.py:48
  522.4 13.8 %collective-permute-start.43 = (bf16[1,64,1024]{2,1,0:T(8,128)(2,1)S(1)}, bf16[1,64,1024]{2,1,0:T(8,128)(2,1)S(1)}, u32[]{:S(2)}, u32[]{:S(2)}) collective-permute-start(bf16[1,64,1024]{2,1,0:T(8,128)(2,1)S(1)} %get-tuple-element.139), channel_id=1, source_target_pairs={{8,0},{10,2},{16,8},{18,10},{24,16},{26,18},{28,24},{30,26},{20,28... | collective-permute-start | bytes 393224 | tf_op jit(solution)/shard_map/ppermute | solution.py:48
  536.2 48.3 %collective-permute-start.9 = (bf16[512,2048]{1,0:T(8,128)(2,1)}, bf16[512,2048]{1,0:T(8,128)(2,1)}, u32[]{:S(2)}, u32[]{:S(2)}) collective-permute-start(bf16[512,2048]{1,0:T(8,128)(2,1)} %bitcast_convert_fusion), channel_id=1, source_target_pairs={{0,1},{1,0},{2,3},{3,2},{4,5},{5,4},{6,7},{7,6},{8,9},{9,8},{10,11... | collective-permute-start | bytes 6291464 | tf_op jit(solution)/shard_map/ppermute | solution.py:236
  539.2 13.4 %collective-permute-start.70 = (bf16[1,64,2752]{2,1,0:T(8,128)(2,1)S(1)}, bf16[1,64,2752]{2,1,0:T(8,128)(2,1)S(1)}, u32[]{:S(2)}, u32[]{:S(2)}) collective-permute-start(bf16[1,64,2752]{2,1,0:T(8,128)(2,1)S(1)} %get-tuple-element.124), channel_id=1, source_target_pairs={{0,8},{2,10},{8,16},{10,18},{16,24},{18,26},{24,28},{26,30},{28,20... | collective-permute-start | bytes 1056776 | tf_op jit(solution)/shard_map/ppermute | solution.py:48
  539.4 14.6 %collective-permute-start.77 = (bf16[1,64,2752]{2,1,0:T(8,128)(2,1)S(1)}, bf16[1,64,2752]{2,1,0:T(8,128)(2,1)S(1)}, u32[]{:S(2)}, u32[]{:S(2)}) collective-permute-start(bf16[1,64,2752]{2,1,0:T(8,128)(2,1)S(1)} %get-tuple-element.125), channel_id=1, source_target_pairs={{8,0},{10,2},{16,8},{18,10},{24,16},{26,18},{28,24},{30,26},{20,28... | collective-permute-start | bytes 1056776 | tf_op jit(solution)/shard_map/ppermute | solution.py:48
  552.6 42.9 %collective-permute-start.15 = (bf16[3,512,1024]{2,1,0:T(8,128)(2,1)}, bf16[3,512,1024]{2,1,0:T(8,128)(2,1)}, u32[]{:S(2)}, u32[]{:S(2)}) collective-permute-start(bf16[3,512,1024]{2,1,0:T(8,128)(2,1)} %fusion.78.right_ref), channel_id=1, source_target_pairs={{0,2},{2,0},{4,6},{6,4},{8,10},{10,8},{12,14},{14,12},{16,18},{18,... | collective-permute-start | bytes 9437192 | tf_op jit(solution)/shard_map/ppermute | solution.py:56
  568.9 25.6 %collective-permute-start.14 = (bf16[512,1024]{1,0:T(8,128)(2,1)}, bf16[512,1024]{1,0:T(8,128)(2,1)S(1)}, u32[]{:S(2)}, u32[]{:S(2)}) collective-permute-start(bf16[512,1024]{1,0:T(8,128)(2,1)} %get-tuple-element.35), channel_id=1, source_target_pairs={{0,2},{2,0},{4,6},{6,4},{8,10},{10,8},{12,14},{14,12},{16,18},{18,... | collective-permute-start | bytes 3145736 | tf_op jit(solution)/shard_map/ppermute | solution.py:56
  569.8 53.0 %collective-permute-start.50 = (bf16[512,1024]{1,0:T(8,128)(2,1)}, bf16[512,1024]{1,0:T(8,128)(2,1)}, u32[]{:S(2)}, u32[]{:S(2)}) collective-permute-start(bf16[512,1024]{1,0:T(8,128)(2,1)} %get-tuple-element.39), channel_id=1, source_target_pairs={{0,2},{2,0},{4,6},{6,4},{8,10},{10,8},{12,14},{14,12},{16,18},{18,... | collective-permute-start | bytes 3145736 | tf_op jit(solution)/shard_map/ppermute | solution.py:56
  593.0 98.9 %collective-permute-start.6 = (bf16[512,2048]{1,0:T(8,128)(2,1)}, bf16[512,2048]{1,0:T(8,128)(2,1)}, u32[]{:S(2)}, u32[]{:S(2)}) collective-permute-start(bf16[512,2048]{1,0:T(8,128)(2,1)} %fusion.32), channel_id=1, source_target_pairs={{0,1},{1,0},{2,3},{3,2},{4,5},{5,4},{6,7},{7,6},{8,9},{9,8},{10,11... | collective-permute-start | bytes 6291464 | tf_op jit(solution)/shard_map/ppermute | solution.py:236
  594.5 50.8 %collective-permute-start.11 = (f32[512]{0:T(512)S(1)}, f32[512]{0:T(512)S(1)}, u32[]{:S(2)}, u32[]{:S(2)}) collective-permute-start(f32[512]{0:T(512)S(1)} %slice_select_fusion.3), channel_id=1, source_target_pairs={{0,8},{2,10},{4,12},{6,14},{8,0},{10,2},{12,4},{14,6},{16,24},{18,... | collective-permute-start | bytes 6152 | tf_op jit(solution)/shard_map/ppermute | solution.py:261
  612.3 33.9 %collective-permute-start.16 = (bf16[3,64,1024]{2,1,0:T(8,128)(2,1)S(1)}, bf16[3,64,1024]{2,1,0:T(8,128)(2,1)S(1)}, u32[]{:S(2)}, u32[]{:S(2)}) collective-permute-start(bf16[3,64,1024]{2,1,0:T(8,128)(2,1)S(1)} %get-tuple-element.112), channel_id=1, source_target_pairs={{0,8},{2,10},{8,16},{10,18},{16,24},{18,26},{24,28},{26,30},{28,20... | collective-permute-start | bytes 1179656 | tf_op jit(solution)/shard_map/ppermute | solution.py:48
  613.5 33.3 %collective-permute-start.23 = (bf16[3,64,1024]{2,1,0:T(8,128)(2,1)S(1)}, bf16[3,64,1024]{2,1,0:T(8,128)(2,1)}, u32[]{:S(2)}, u32[]{:S(2)}) collective-permute-start(bf16[3,64,1024]{2,1,0:T(8,128)(2,1)S(1)} %get-tuple-element.113), channel_id=1, source_target_pairs={{8,0},{10,2},{16,8},{18,10},{24,16},{26,18},{28,24},{30,26},{20,28... | collective-permute-start | bytes 1179656 | tf_op jit(solution)/shard_map/ppermute | solution.py:48
  644.2 19.1 %collective-permute-start.52 = (bf16[2,64,2752]{2,1,0:T(8,128)(2,1)S(1)}, bf16[2,64,2752]{2,1,0:T(8,128)(2,1)S(1)}, u32[]{:S(2)}, u32[]{:S(2)}) collective-permute-start(bf16[2,64,2752]{2,1,0:T(8,128)(2,1)S(1)} %get-tuple-element.96), channel_id=1, source_target_pairs={{0,8},{2,10},{8,16},{10,18},{16,24},{18,26},{24,28},{26,30},{28,20... | collective-permute-start | bytes 2113544 | tf_op jit(solution)/shard_map/ppermute | solution.py:48
  645.4 18.3 %collective-permute-start.59 = (bf16[2,64,2752]{2,1,0:T(8,128)(2,1)S(1)}, bf16[2,64,2752]{2,1,0:T(8,128)(2,1)S(1)}, u32[]{:S(2)}, u32[]{:S(2)}) collective-permute-start(bf16[2,64,2752]{2,1,0:T(8,128)(2,1)S(1)} %get-tuple-element.97), channel_id=1, source_target_pairs={{8,0},{10,2},{16,8},{18,10},{24,16},{26,18},{28,24},{30,26},{20,28... | collective-permute-start | bytes 2113544 | tf_op jit(solution)/shard_map/ppermute | solution.py:48
  646.3 20.8 %collective-permute-start.12 = (f32[256]{0:T(256)S(1)}, f32[256]{0:T(256)S(1)}, u32[]{:S(2)}, u32[]{:S(2)}) collective-permute-start(f32[256]{0:T(256)S(1)} %broadcast_select_fusion.5), channel_id=1, source_target_pairs={{0,4},{2,6},{4,0},{6,2},{8,12},{10,14},{12,8},{14,10},{16,20},{18,... | collective-permute-start | bytes 3080 | tf_op jit(solution)/shard_map/ppermute | solution.py:261
  648.3 23.3 %collective-permute-start.17 = (bf16[3,64,1024]{2,1,0:T(8,128)(2,1)S(1)}, bf16[3,64,1024]{2,1,0:T(8,128)(2,1)S(1)}, u32[]{:S(2)}, u32[]{:S(2)}) collective-permute-start(bf16[3,64,1024]{2,1,0:T(8,128)(2,1)S(1)} %get-tuple-element.110), channel_id=1, source_target_pairs={{0,8},{2,10},{8,16},{10,18},{16,24},{18,26},{24,28},{26,30},{28,20... | collective-permute-start | bytes 1179656 | tf_op jit(solution)/shard_map/ppermute | solution.py:48
  663.2 12.0 %collective-permute-start.24 = (bf16[3,64,1024]{2,1,0:T(8,128)(2,1)S(1)}, bf16[3,64,1024]{2,1,0:T(8,128)(2,1)S(1)}, u32[]{:S(2)}, u32[]{:S(2)}) collective-permute-start(bf16[3,64,1024]{2,1,0:T(8,128)(2,1)S(1)} %get-tuple-element.111), channel_id=1, source_target_pairs={{8,0},{10,2},{16,8},{18,10},{24,16},{26,18},{28,24},{30,26},{20,28... | collective-permute-start | bytes 1179656 | tf_op jit(solution)/shard_map/ppermute | solution.py:48
  665.4 21.7 %collective-permute-start.53 = (bf16[2,64,2752]{2,1,0:T(8,128)(2,1)S(1)}, bf16[2,64,2752]{2,1,0:T(8,128)(2,1)S(1)}, u32[]{:S(2)}, u32[]{:S(2)}) collective-permute-start(bf16[2,64,2752]{2,1,0:T(8,128)(2,1)S(1)} %get-tuple-element.94), channel_id=1, source_target_pairs={{0,8},{2,10},{8,16},{10,18},{16,24},{18,26},{24,28},{26,30},{28,20... | collective-permute-start | bytes 2113544 | tf_op jit(solution)/shard_map/ppermute | solution.py:48
  667.0 20.8 %collective-permute-start.60 = (bf16[2,64,2752]{2,1,0:T(8,128)(2,1)S(1)}, bf16[2,64,2752]{2,1,0:T(8,128)(2,1)S(1)}, u32[]{:S(2)}, u32[]{:S(2)}) collective-permute-start(bf16[2,64,2752]{2,1,0:T(8,128)(2,1)S(1)} %get-tuple-element.95), channel_id=1, source_target_pairs={{8,0},{10,2},{16,8},{18,10},{24,16},{26,18},{28,24},{30,26},{20,28... | collective-permute-start | bytes 2113544 | tf_op jit(solution)/shard_map/ppermute | solution.py:48
  671.7 30.6 %collective-permute-start.13 = (f32[128]{0:T(128)S(1)}, f32[128]{0:T(128)S(1)}, u32[]{:S(2)}, u32[]{:S(2)}) collective-permute-start(f32[128]{0:T(128)S(1)} %broadcast_select_fusion.8), channel_id=1, source_target_pairs={{0,2},{2,0},{4,6},{6,4},{8,10},{10,8},{12,14},{14,12},{16,18},{18,... | collective-permute-start | bytes 1544 | tf_op jit(solution)/shard_map/ppermute | solution.py:261
  677.5 27.1 %collective-permute-start.18 = (bf16[3,64,1024]{2,1,0:T(8,128)(2,1)}, bf16[3,64,1024]{2,1,0:T(8,128)(2,1)S(1)}, u32[]{:S(2)}, u32[]{:S(2)}) collective-permute-start(bf16[3,64,1024]{2,1,0:T(8,128)(2,1)} %get-tuple-element.108), channel_id=1, source_target_pairs={{0,8},{2,10},{8,16},{10,18},{16,24},{18,26},{24,28},{26,30},{28,20... | collective-permute-start | bytes 1179656 | tf_op jit(solution)/shard_map/ppermute | solution.py:48
  687.1 17.7 %collective-permute-start.25 = (bf16[3,64,1024]{2,1,0:T(8,128)(2,1)}, bf16[3,64,1024]{2,1,0:T(8,128)(2,1)}, u32[]{:S(2)}, u32[]{:S(2)}) collective-permute-start(bf16[3,64,1024]{2,1,0:T(8,128)(2,1)} %get-tuple-element.109), channel_id=1, source_target_pairs={{8,0},{10,2},{16,8},{18,10},{24,16},{26,18},{28,24},{30,26},{20,28... | collective-permute-start | bytes 1179656 | tf_op jit(solution)/shard_map/ppermute | solution.py:48
  690.3 20.7 %collective-permute-start.54 = (bf16[2,64,2752]{2,1,0:T(8,128)(2,1)}, bf16[2,64,2752]{2,1,0:T(8,128)(2,1)S(1)}, u32[]{:S(2)}, u32[]{:S(2)}) collective-permute-start(bf16[2,64,2752]{2,1,0:T(8,128)(2,1)} %get-tuple-element.92), channel_id=1, source_target_pairs={{0,8},{2,10},{8,16},{10,18},{16,24},{18,26},{24,28},{26,30},{28,20... | collective-permute-start | bytes 2113544 | tf_op jit(solution)/shard_map/ppermute | solution.py:48
  692.0 23.0 %collective-permute-start.61 = (bf16[2,64,2752]{2,1,0:T(8,128)(2,1)S(1)}, bf16[2,64,2752]{2,1,0:T(8,128)(2,1)S(1)}, u32[]{:S(2)}, u32[]{:S(2)}) collective-permute-start(bf16[2,64,2752]{2,1,0:T(8,128)(2,1)S(1)} %get-tuple-element.93), channel_id=1, source_target_pairs={{8,0},{10,2},{16,8},{18,10},{24,16},{26,18},{28,24},{30,26},{20,28... | collective-permute-start | bytes 2113544 | tf_op jit(solution)/shard_map/ppermute | solution.py:48
  702.2 16.5 %collective-permute-start.72 = (bf16[1,64,2752]{2,1,0:T(8,128)(2,1)}, bf16[1,64,2752]{2,1,0:T(8,128)(2,1)S(1)}, u32[]{:S(2)}, u32[]{:S(2)}) collective-permute-start(bf16[1,64,2752]{2,1,0:T(8,128)(2,1)} %get-tuple-element.120), channel_id=1, source_target_pairs={{0,8},{2,10},{8,16},{10,18},{16,24},{18,26},{24,28},{26,30},{28,20... | collective-permute-start | bytes 1056776 | tf_op jit(solution)/shard_map/ppermute | solution.py:48
  704.6 18.1 %collective-permute-start.79 = (bf16[1,64,2752]{2,1,0:T(8,128)(2,1)}, bf16[1,64,2752]{2,1,0:T(8,128)(2,1)S(1)}, u32[]{:S(2)}, u32[]{:S(2)}) collective-permute-start(bf16[1,64,2752]{2,1,0:T(8,128)(2,1)} %get-tuple-element.121), channel_id=1, source_target_pairs={{8,0},{10,2},{16,8},{18,10},{24,16},{26,18},{28,24},{30,26},{20,28... | collective-permute-start | bytes 1056776 | tf_op jit(solution)/shard_map/ppermute | solution.py:48
  706.2 21.0 %collective-permute-start.19 = (bf16[3,64,1024]{2,1,0:T(8,128)(2,1)S(1)}, bf16[3,64,1024]{2,1,0:T(8,128)(2,1)S(1)}, u32[]{:S(2)}, u32[]{:S(2)}) collective-permute-start(bf16[3,64,1024]{2,1,0:T(8,128)(2,1)S(1)} %get-tuple-element.106), channel_id=1, source_target_pairs={{0,8},{2,10},{8,16},{10,18},{16,24},{18,26},{24,28},{26,30},{28,20... | collective-permute-start | bytes 1179656 | tf_op jit(solution)/shard_map/ppermute | solution.py:48
  711.0 20.2 %collective-permute-start.26 = (bf16[3,64,1024]{2,1,0:T(8,128)(2,1)S(1)}, bf16[3,64,1024]{2,1,0:T(8,128)(2,1)S(1)}, u32[]{:S(2)}, u32[]{:S(2)}) collective-permute-start(bf16[3,64,1024]{2,1,0:T(8,128)(2,1)S(1)} %get-tuple-element.107), channel_id=1, source_target_pairs={{8,0},{10,2},{16,8},{18,10},{24,16},{26,18},{28,24},{30,26},{20,28... | collective-permute-start | bytes 1179656 | tf_op jit(solution)/shard_map/ppermute | solution.py:48
  715.4 27.2 %collective-permute-start.55 = (bf16[2,64,2752]{2,1,0:T(8,128)(2,1)S(1)}, bf16[2,64,2752]{2,1,0:T(8,128)(2,1)S(1)}, u32[]{:S(2)}, u32[]{:S(2)}) collective-permute-start(bf16[2,64,2752]{2,1,0:T(8,128)(2,1)S(1)} %get-tuple-element.90), channel_id=1, source_target_pairs={{0,8},{2,10},{8,16},{10,18},{16,24},{18,26},{24,28},{26,30},{28,20... | collective-permute-start | bytes 2113544 | tf_op jit(solution)/shard_map/ppermute | solution.py:48
  718.7 27.9 %collective-permute-start.62 = (bf16[2,64,2752]{2,1,0:T(8,128)(2,1)S(1)}, bf16[2,64,2752]{2,1,0:T(8,128)(2,1)S(1)}, u32[]{:S(2)}, u32[]{:S(2)}) collective-permute-start(bf16[2,64,2752]{2,1,0:T(8,128)(2,1)S(1)} %get-tuple-element.91), channel_id=1, source_target_pairs={{8,0},{10,2},{16,8},{18,10},{24,16},{26,18},{28,24},{30,26},{20,28... | collective-permute-start | bytes 2113544 | tf_op jit(solution)/shard_map/ppermute | solution.py:48
  724.0 26.3 %collective-permute-start.73 = (bf16[1,64,2752]{2,1,0:T(8,128)(2,1)S(1)}, bf16[1,64,2752]{2,1,0:T(8,128)(2,1)S(1)}, u32[]{:S(2)}, u32[]{:S(2)}) collective-permute-start(bf16[1,64,2752]{2,1,0:T(8,128)(2,1)S(1)} %get-tuple-element.118), channel_id=1, source_target_pairs={{0,8},{2,10},{8,16},{10,18},{16,24},{18,26},{24,28},{26,30},{28,20... | collective-permute-start | bytes 1056776 | tf_op jit(solution)/shard_map/ppermute | solution.py:48
  727.2 27.2 %collective-permute-start.80 = (bf16[1,64,2752]{2,1,0:T(8,128)(2,1)S(1)}, bf16[1,64,2752]{2,1,0:T(8,128)(2,1)S(1)}, u32[]{:S(2)}, u32[]{:S(2)}) collective-permute-start(bf16[1,64,2752]{2,1,0:T(8,128)(2,1)S(1)} %get-tuple-element.119), channel_id=1, source_target_pairs={{8,0},{10,2},{16,8},{18,10},{24,16},{26,18},{28,24},{30,26},{20,28... | collective-permute-start | bytes 1056776 | tf_op jit(solution)/shard_map/ppermute | solution.py:48
  731.5 27.3 %collective-permute-start.20 = (bf16[3,64,1024]{2,1,0:T(8,128)(2,1)S(1)}, bf16[3,64,1024]{2,1,0:T(8,128)(2,1)S(1)}, u32[]{:S(2)}, u32[]{:S(2)}) collective-permute-start(bf16[3,64,1024]{2,1,0:T(8,128)(2,1)S(1)} %get-tuple-element.104), channel_id=1, source_target_pairs={{0,8},{2,10},{8,16},{10,18},{16,24},{18,26},{24,28},{26,30},{28,20... | collective-permute-start | bytes 1179656 | tf_op jit(solution)/shard_map/ppermute | solution.py:48
  742.6 20.2 %collective-permute-start.27 = (bf16[3,64,1024]{2,1,0:T(8,128)(2,1)S(1)}, bf16[3,64,1024]{2,1,0:T(8,128)(2,1)S(1)}, u32[]{:S(2)}, u32[]{:S(2)}) collective-permute-start(bf16[3,64,1024]{2,1,0:T(8,128)(2,1)S(1)} %get-tuple-element.105), channel_id=1, source_target_pairs={{8,0},{10,2},{16,8},{18,10},{24,16},{26,18},{28,24},{30,26},{20,28... | collective-permute-start | bytes 1179656 | tf_op jit(solution)/shard_map/ppermute | solution.py:48
  747.0 27.2 %collective-permute-start.56 = (bf16[2,64,2752]{2,1,0:T(8,128)(2,1)S(1)}, bf16[2,64,2752]{2,1,0:T(8,128)(2,1)S(1)}, u32[]{:S(2)}, u32[]{:S(2)}) collective-permute-start(bf16[2,64,2752]{2,1,0:T(8,128)(2,1)S(1)} %get-tuple-element.88), channel_id=1, source_target_pairs={{0,8},{2,10},{8,16},{10,18},{16,24},{18,26},{24,28},{26,30},{28,20... | collective-permute-start | bytes 2113544 | tf_op jit(solution)/shard_map/ppermute | solution.py:48
  750.3 27.9 %collective-permute-start.63 = (bf16[2,64,2752]{2,1,0:T(8,128)(2,1)S(1)}, bf16[2,64,2752]{2,1,0:T(8,128)(2,1)S(1)}, u32[]{:S(2)}, u32[]{:S(2)}) collective-permute-start(bf16[2,64,2752]{2,1,0:T(8,128)(2,1)S(1)} %get-tuple-element.89), channel_id=1, source_target_pairs={{8,0},{10,2},{16,8},{18,10},{24,16},{26,18},{28,24},{30,26},{20,28... | collective-permute-start | bytes 2113544 | tf_op jit(solution)/shard_map/ppermute | solution.py:48
  755.6 26.3 %collective-permute-start.74 = (bf16[1,64,2752]{2,1,0:T(8,128)(2,1)S(1)}, bf16[1,64,2752]{2,1,0:T(8,128)(2,1)S(1)}, u32[]{:S(2)}, u32[]{:S(2)}) collective-permute-start(bf16[1,64,2752]{2,1,0:T(8,128)(2,1)S(1)} %get-tuple-element.116), channel_id=1, source_target_pairs={{0,8},{2,10},{8,16},{10,18},{16,24},{18,26},{24,28},{26,30},{28,20... | collective-permute-start | bytes 1056776 | tf_op jit(solution)/shard_map/ppermute | solution.py:48
  758.8 27.2 %collective-permute-start.81 = (bf16[1,64,2752]{2,1,0:T(8,128)(2,1)S(1)}, bf16[1,64,2752]{2,1,0:T(8,128)(2,1)S(1)}, u32[]{:S(2)}, u32[]{:S(2)}) collective-permute-start(bf16[1,64,2752]{2,1,0:T(8,128)(2,1)S(1)} %get-tuple-element.117), channel_id=1, source_target_pairs={{8,0},{10,2},{16,8},{18,10},{24,16},{26,18},{28,24},{30,26},{20,28... | collective-permute-start | bytes 1056776 | tf_op jit(solution)/shard_map/ppermute | solution.py:48
  763.1 27.3 %collective-permute-start.21 = (bf16[3,64,1024]{2,1,0:T(8,128)(2,1)S(1)}, bf16[3,64,1024]{2,1,0:T(8,128)(2,1)S(1)}, u32[]{:S(2)}, u32[]{:S(2)}) collective-permute-start(bf16[3,64,1024]{2,1,0:T(8,128)(2,1)S(1)} %get-tuple-element.102), channel_id=1, source_target_pairs={{0,8},{2,10},{8,16},{10,18},{16,24},{18,26},{24,28},{26,30},{28,20... | collective-permute-start | bytes 1179656 | tf_op jit(solution)/shard_map/ppermute | solution.py:48
  774.2 20.2 %collective-permute-start.28 = (bf16[3,64,1024]{2,1,0:T(8,128)(2,1)S(1)}, bf16[3,64,1024]{2,1,0:T(8,128)(2,1)S(1)}, u32[]{:S(2)}, u32[]{:S(2)}) collective-permute-start(bf16[3,64,1024]{2,1,0:T(8,128)(2,1)S(1)} %get-tuple-element.103), channel_id=1, source_target_pairs={{8,0},{10,2},{16,8},{18,10},{24,16},{26,18},{28,24},{30,26},{20,28... | collective-permute-start | bytes 1179656 | tf_op jit(solution)/shard_map/ppermute | solution.py:48
  778.6 27.2 %collective-permute-start.57 = (bf16[2,64,2752]{2,1,0:T(8,128)(2,1)S(1)}, bf16[2,64,2752]{2,1,0:T(8,128)(2,1)S(1)}, u32[]{:S(2)}, u32[]{:S(2)}) collective-permute-start(bf16[2,64,2752]{2,1,0:T(8,128)(2,1)S(1)} %get-tuple-element.86), channel_id=1, source_target_pairs={{0,8},{2,10},{8,16},{10,18},{16,24},{18,26},{24,28},{26,30},{28,20... | collective-permute-start | bytes 2113544 | tf_op jit(solution)/shard_map/ppermute | solution.py:48
  781.9 27.9 %collective-permute-start.64 = (bf16[2,64,2752]{2,1,0:T(8,128)(2,1)S(1)}, bf16[2,64,2752]{2,1,0:T(8,128)(2,1)S(1)}, u32[]{:S(2)}, u32[]{:S(2)}) collective-permute-start(bf16[2,64,2752]{2,1,0:T(8,128)(2,1)S(1)} %get-tuple-element.87), channel_id=1, source_target_pairs={{8,0},{10,2},{16,8},{18,10},{24,16},{26,18},{28,24},{30,26},{20,28... | collective-permute-start | bytes 2113544 | tf_op jit(solution)/shard_map/ppermute | solution.py:48
  795.5 19.1 %collective-permute-start.22 = (bf16[3,64,1024]{2,1,0:T(8,128)(2,1)}, bf16[3,64,1024]{2,1,0:T(8,128)(2,1)S(1)}, u32[]{:S(2)}, u32[]{:S(2)}) collective-permute-start(bf16[3,64,1024]{2,1,0:T(8,128)(2,1)} %get-tuple-element.100), channel_id=1, source_target_pairs={{0,8},{2,10},{8,16},{10,18},{16,24},{18,26},{24,28},{26,30},{28,20... | collective-permute-start | bytes 1179656 | tf_op jit(solution)/shard_map/ppermute | solution.py:48
  796.7 21.7 %collective-permute-start.29 = (bf16[3,64,1024]{2,1,0:T(8,128)(2,1)}, bf16[3,64,1024]{2,1,0:T(8,128)(2,1)}, u32[]{:S(2)}, u32[]{:S(2)}) collective-permute-start(bf16[3,64,1024]{2,1,0:T(8,128)(2,1)} %get-tuple-element.101), channel_id=1, source_target_pairs={{8,0},{10,2},{16,8},{18,10},{24,16},{26,18},{28,24},{30,26},{20,28... | collective-permute-start | bytes 1179656 | tf_op jit(solution)/shard_map/ppermute | solution.py:48
  811.0 15.3 %collective-permute-start.58 = (bf16[2,64,2752]{2,1,0:T(8,128)(2,1)}, bf16[2,64,2752]{2,1,0:T(8,128)(2,1)S(1)}, u32[]{:S(2)}, u32[]{:S(2)}) collective-permute-start(bf16[2,64,2752]{2,1,0:T(8,128)(2,1)} %get-tuple-element.84), channel_id=1, source_target_pairs={{0,8},{2,10},{8,16},{10,18},{16,24},{18,26},{24,28},{26,30},{28,20... | collective-permute-start | bytes 2113544 | tf_op jit(solution)/shard_map/ppermute | solution.py:48
  812.2 14.8 %collective-permute-start.65 = (bf16[2,64,2752]{2,1,0:T(8,128)(2,1)S(1)}, bf16[2,64,2752]{2,1,0:T(8,128)(2,1)}, u32[]{:S(2)}, u32[]{:S(2)}) collective-permute-start(bf16[2,64,2752]{2,1,0:T(8,128)(2,1)S(1)} %get-tuple-element.85), channel_id=1, source_target_pairs={{8,0},{10,2},{16,8},{18,10},{24,16},{26,18},{28,24},{30,26},{20,28... | collective-permute-start | bytes 2113544 | tf_op jit(solution)/shard_map/ppermute | solution.py:48
  (50 other events, 693.9 us)
Sparse Core Ops, SparseCore 0:
  10.8 129.2 all-gather.2
  142.1 177.9 all-gather.4

commit v4 on v3

--- a/solution.py
+++ b/solution.py
@@ -33,22 +33,50 @@
     return ahead, [(target, source) for source, target in ahead]
 
 
-def ring_scatter(terms, chips, place):
-    routes = ring_routes(chips)
-    steps = (1, -1)
-
-    def part(direction, offset):
-        chip = chip_at(place - steps[direction] * offset, chips)
+class Ring:
+    def __init__(self, terms, chips, place):
+        self.terms = terms
+        self.chips = chips
+        self.place = place
+        self.hop = 1
+        self.routes = ring_routes(chips)
+        self.sums = [self.part(direction) for direction in range(2)]
+
+    def part(self, direction):
+        chip = chip_at(self.place - (1, -1)[direction] * self.hop, self.chips)
         start = (chip, direction, 0, 0, 0)
-        return lax.dynamic_slice(terms, start, (1, 1) + terms.shape[2:])[0, 0]
-
-    sums = [part(direction, 1) for direction in range(2)]
-    for hop in range(2, chips + 1):
+        return lax.dynamic_slice(self.terms, start, (1, 1) + self.terms.shape[2:])[0, 0]
+
+    def open(self):
+        return self.hop < self.chips
+
+    def send(self):
+        return [lax.ppermute(self.sums[d], "seq", self.routes[d]) for d in range(2)]
+
+    def take(self, arrived):
+        self.hop += 1
         for direction in range(2):
-            arrived = lax.ppermute(sums[direction], "seq", routes[direction])
-            total = arrived.astype(jnp.float32) + part(direction, hop).astype(jnp.float32)
-            sums[direction] = total if hop == chips else total.astype(jnp.bfloat16)
-    return jnp.concatenate(sums, axis=1)
+            total = arrived[direction].astype(jnp.float32)
+            total = total + self.part(direction).astype(jnp.float32)
+            self.sums[direction] = total if not self.open() else total.astype(jnp.bfloat16)
+
+    def result(self):
+        while self.open():
+            self.take(self.send())
+        return jnp.concatenate(self.sums, axis=1)
+
+
+def beside(rings, work, *given):
+    rings = [ring for ring in rings if ring.open()]
+    sums, given = lax.optimization_barrier(([ring.sums for ring in rings], given))
+    for ring, held in zip(rings, sums):
+        ring.sums = held
+    arrived = [ring.send() for ring in rings]
+    made = work(*given)
+    arrived, made = lax.optimization_barrier((arrived, made))
+    for ring, blocks in zip(rings, arrived):
+        ring.take(blocks)
+    return made
 
 
 def partner(block):
@@ -56,30 +84,33 @@
     return lax.ppermute(block, "seq", [(i, i ^ 1) for i in range(size)])
 
 
-def select_kernel(core_ref, own_ref, other_ref, kept_ref, given_ref):
-    kept_ref[...] = own_ref[...]
-    given_ref[...] = other_ref[...]
+def select_kernel(core_ref, block_ref, kept_ref, given_ref):
+    rows = 128
+    for chip in range(kept_ref.shape[1] // rows):
+        even = block_ref[:, 2 * chip * rows : (2 * chip + 1) * rows]
+        odd = block_ref[:, (2 * chip + 1) * rows : (2 * chip + 2) * rows]
+        first = core_ref[0] == 0
+        kept_ref[:, chip * rows : (chip + 1) * rows] = jnp.where(first, even, odd)
+        given_ref[:, chip * rows : (chip + 1) * rows] = jnp.where(first, odd, even)
 
 
 def pair_columns(block, chips, core):
     tokens, width = block.shape
     rows = width // (2 * chips)
     half = jax.ShapeDtypeStruct((tokens, width // 2), block.dtype)
-    if rows % 128 == 0:
+    if rows == 128:
+        group = 128
         kept, given = pl.pallas_call(
             select_kernel,
             grid_spec=pltpu.PrefetchScalarGridSpec(
                 num_scalar_prefetch=1,
-                grid=(chips,),
-                in_specs=[
-                    pl.BlockSpec((tokens, rows), lambda q, c: (0, 2 * q + c[0])),
-                    pl.BlockSpec((tokens, rows), lambda q, c: (0, 2 * q + 1 - c[0])),
-                ],
-                out_specs=[pl.BlockSpec((tokens, rows), lambda q, c: (0, q))] * 2,
+                grid=(tokens // group,),
+                in_specs=[pl.BlockSpec((group, width), lambda t, c: (t, 0))],
+                out_specs=[pl.BlockSpec((group, width // 2), lambda t, c: (t, 0))] * 2,
             ),
             out_shape=[half, half],
             name="select_columns",
-        )(core.reshape(1), block, block)
+        )(core.reshape(1), block)
     else:
         split = block.reshape(tokens, chips, 2, rows)
         kept = lax.dynamic_index_in_dim(split, core, 2, keepdims=False).reshape(half.shape)
@@ -97,7 +128,7 @@
     terms_ref[...] = total.astype(jnp.bfloat16).reshape(terms_ref.shape)
 
 
-def pair_terms(left, right, chips):
+def pair_terms(left, right, right_two, chips):
     planes, tokens, columns = right.shape
     rows = left[0].shape[1] // chips
     group = max(1, 256 // rows)
@@ -117,7 +148,7 @@
             transcendentals=0,
         ),
         name="pair_terms",
-    )(left[0], left[1], right, partner(right))
+    )(left[0], left[1], right, right_two)
 
 
 SPAN = 128
@@ -231,10 +262,12 @@
     )(starts, proj, before, grad_mixed)
 
 
+def tp_send(sent):
+    return sent.astype(jnp.float32) + lax.ppermute(sent, "tp", [(0, 1), (1, 0)]).astype(jnp.float32)
+
+
 def tp_sum(partial):
-    sent = lax.optimization_barrier(partial.astype(jnp.bfloat16))
-    other = lax.ppermute(sent, "tp", [(0, 1), (1, 0)])
-    return sent.astype(jnp.float32) + other.astype(jnp.float32)
+    return tp_send(lax.optimization_barrier(partial.astype(jnp.bfloat16)))
 
 
 def gather_small(block):
@@ -295,15 +328,15 @@
     f32 = jnp.float32
     bf16 = jnp.bfloat16
 
-    gains = gather_small(jnp.stack([gain_one, gain_two])).astype(f32)
+    first_own = jnp.concatenate([w_qkv, w_out.T[:, None]], axis=1)
+    second_own = jnp.concatenate([w_gate_up, w_down.T[:, None]], axis=1)
+    gains = jnp.stack([gain_one, gain_two])
+    first_own, second_own, gains = lax.optimization_barrier((first_own, second_own, gains))
+    first_weights = lax.all_gather(first_own, "seq", axis=0, tiled=True)
+    second_weights = lax.all_gather(second_own, "seq", axis=0, tiled=True)
+    gains = gather_small(gains).astype(f32)
     gain_a = gains[0]
     gain_b = gains[1]
-    first_weights = lax.all_gather(
-        jnp.concatenate([w_qkv, w_out.T[:, None]], axis=1), "seq", axis=0, tiled=True
-    )
-    second_weights = lax.all_gather(
-        jnp.concatenate([w_gate_up, w_down.T[:, None]], axis=1), "seq", axis=0, tiled=True
-    )
     qkv_full = first_weights[:, :3]
     out_full = first_weights[:, 3]
     gate_up_full = second_weights[:, :2]
@@ -318,46 +351,101 @@
     middle = token_rows + attn_out
     normed_two = rms_scale(middle, gain_b).astype(bf16)
     gate_up = jnp.einsum("td,dcf->ctf", normed_two, gate_up_full, preferred_element_type=f32)
-    gate_part = gate_up[0]
-    up_part = gate_up[1]
-    hidden = gated(gate_part, up_part).astype(bf16)
-    down_terms = pair_terms(pair_columns(cotangent, chips, core), hidden[None], chips)
-    grad_w_down = ring_scatter(down_terms, chips, place)[0].T
-
-    grad_hidden = jnp.einsum("td,df->tf", cotangent, down_full, preferred_element_type=f32)
-    unused_value, gate_pull = jax.vjp(gated, gate_part, up_part)
-    grad_gate_up = jnp.stack(gate_pull(grad_hidden)).astype(bf16)
-    gate_up_terms = pair_terms(pair_columns(normed_two, chips, core), grad_gate_up, chips)
-    grad_w_gate_up = ring_scatter(gate_up_terms, chips, place).transpose(1, 0, 2)
-    grad_normed_two = tp_sum(
-        jnp.einsum("ctf,dcf->td", grad_gate_up, gate_up_full, preferred_element_type=f32)
-    )
-    branch = tp_sum(jnp.einsum("tf,df->td", hidden, down_full, preferred_element_type=f32))
-    result = (middle + branch).astype(bf16)
-
-    unused_norm, norm_pull = jax.vjp(rms_scale, middle, gain_b)
-    grad_mid_norm, grad_gain_two = norm_pull(grad_normed_two)
-    grad_middle = cotangent.astype(f32) + grad_mid_norm
+    hidden = gated(gate_up[0], gate_up[1]).astype(bf16)
+    cot_pair = pair_columns(cotangent, chips, core)
+    normed_two_pair = pair_columns(normed_two, chips, core)
+    normed_pair = pair_columns(normed, chips, core)
+    hidden, cot_held = lax.optimization_barrier((hidden, cotangent))
+    hidden_two = partner(hidden[None])
+    grad_hidden = jnp.einsum("td,df->tf", cot_held, down_full, preferred_element_type=f32)
+    down_terms = pair_terms(cot_pair, hidden[None], hidden_two, chips)
+    down = Ring(down_terms, chips, place)
+
+    def through_gate(grad_hidden, gate_up):
+        unused_value, gate_pull = jax.vjp(gated, gate_up[0], gate_up[1])
+        return jnp.stack(gate_pull(grad_hidden)).astype(bf16)
+
+    grad_gate_up = beside([down], through_gate, grad_hidden, gate_up)
+    grad_gate_up_two = partner(grad_gate_up)
+
+    def through_gate_up(grad_gate_up):
+        return jnp.einsum(
+            "ctf,dcf->td", grad_gate_up, gate_up_full, preferred_element_type=f32
+        ).astype(bf16)
+
+    sent_two = beside([down], through_gate_up, grad_gate_up)
+    grad_normed_two = tp_send(sent_two)
+
+    def gate_up_product(grad_gate_up):
+        return pair_terms(normed_two_pair, grad_gate_up, grad_gate_up_two, chips)
+
+    gate_up_ring = Ring(beside([down], gate_up_product, grad_gate_up), chips, place)
+
+    def through_down(hidden):
+        return jnp.einsum("tf,df->td", hidden, down_full, preferred_element_type=f32).astype(bf16)
+
+    rings = [down, gate_up_ring]
+    branch = tp_send(beside(rings, through_down, hidden))
+
+    def through_norm_two(middle):
+        unused_norm, norm_pull = jax.vjp(rms_scale, middle, gain_b)
+        grad_mid_norm, grad_gain_two = norm_pull(grad_normed_two)
+        grad_middle = cotangent.astype(f32) + grad_mid_norm
+        grad_attn = grad_middle.astype(bf16)
+        grad_mixed = jnp.einsum("td,df->tf", grad_attn, out_full, preferred_element_type=f32)
+        return grad_middle, grad_gain_two, grad_attn, grad_mixed.astype(bf16)
+
+    grad_middle, grad_gain_two, grad_attn, grad_mixed = beside(rings, through_norm_two, middle)
     grad_gain_two = scatter_small(grad_gain_two)
-    grad_attn = grad_middle.astype(bf16)
-    grad_mixed = jnp.einsum("td,df->tf", grad_attn, out_full, preferred_element_type=f32).astype(
-        bf16
-    )
-    out_terms = pair_terms(pair_columns(grad_attn, chips, core), attn_mixed[None], chips)
-    grad_w_out = ring_scatter(out_terms, chips, place)[0].T
-
-    grad_proj, rim, tail = attend_back(starts, proj, before, grad_mixed)
+    mixed_two = partner(attn_mixed[None])
+    grad_attn_pair = pair_columns(grad_attn, chips, core)
+
+    def through_attention(grad_mixed):
+        return attend_back(starts, proj, before, grad_mixed)
+
+    grad_proj, rim, tail = beside(rings, through_attention, grad_mixed)
     arrived = shifted(rim, "seq", -1).astype(f32)
-    grad_proj = grad_proj.at[1:, token_count - WINDOW :].set((tail + arrived).astype(bf16))
-    qkv_terms = pair_terms(pair_columns(normed, chips, core), grad_proj, chips)
-    grad_w_qkv = ring_scatter(qkv_terms, chips, place).transpose(1, 0, 2)
-    grad_normed = tp_sum(
-        jnp.einsum("ctf,dcf->td", grad_proj, qkv_full, preferred_element_type=f32)
-    )
-    unused_first, first_pull = jax.vjp(rms_scale, token_rows, gain_a)
-    grad_rows_norm, grad_gain_one = first_pull(grad_normed)
-    grad_tokens = grad_middle + grad_rows_norm
+
+    def out_product(grad_proj):
+        out_terms = pair_terms(grad_attn_pair, attn_mixed[None], mixed_two, chips)
+        edge = (tail + arrived).astype(bf16)
+        return out_terms, grad_proj.at[1:, token_count - WINDOW :].set(edge)
+
+    out_terms, grad_proj = beside(rings, out_product, grad_proj)
+    rings.append(Ring(out_terms, chips, place))
+    grad_proj_two = partner(grad_proj)
+
+    def through_qkv(grad_proj):
+        return jnp.einsum(
+            "ctf,dcf->td", grad_proj, qkv_full, preferred_element_type=f32
+        ).astype(bf16)
+
+    grad_normed = tp_send(beside(rings, through_qkv, grad_proj))
+
+    def qkv_product(grad_proj):
+        return pair_terms(normed_pair, grad_proj, grad_proj_two, chips)
+
+    rings.append(Ring(beside(rings, qkv_product, grad_proj), chips, place))
+
+    def finish(middle):
+        return (middle + branch).astype(bf16), down.result()[0].T
+
+    result, grad_w_down = beside(rings, finish, middle)
+
+    def finish_gate_up(whole):
+        return whole.transpose(1, 0, 2)
+
+    grad_w_gate_up = beside(rings, finish_gate_up, gate_up_ring.result())
+
+    def through_norm(token_rows):
+        unused_first, first_pull = jax.vjp(rms_scale, token_rows, gain_a)
+        grad_rows_norm, grad_gain_one = first_pull(grad_normed)
+        return grad_middle + grad_rows_norm, grad_gain_one
+
+    grad_tokens, grad_gain_one = beside(rings, through_norm, token_rows)
     grad_gain_one = scatter_small(grad_gain_one)
+    grad_w_out = rings[2].result()[0].T
+    grad_w_qkv = rings[3].result().transpose(1, 0, 2)
     return (
         result,
         grad_tokens,

time: 847 us -> 818 us (0.966)
  waiting for transfers between devices: 417 us -> 357 us
  starting transfers between devices: 84.6 us -> 104 us
  other arithmetic: 82.4 us -> 95.1 us
    ppermute x60, waiting for transfers between devices: 203 us -> 138 us  [the longest x4 72.8 us: tp_send(): lax.ppermute(sent, 'tp', [(0, 1), (1, 0)]).astype(jnp.float32)]
    ppermute x60, starting transfers between devices: 61 us -> 84.7 us  [the longest x56 79.6 us: send(): return [lax.ppermute(self.sums[d], 'seq', self.routes[d]) for d in range(2)]]
    convert_element_type x27 -> x29, other arithmetic: 33.2 us -> 52.6 us  [the longest x24 39.5 us: take(): total.astype(jnp.bfloat16)]
    optimization_barrier x0 -> x2, local copies, waits for them, and re-layouts: none -> 14.5 us  [the longest x1 8.27 us: beside(): arrived, made = lax.optimization_barrier((arrived, made))]
    all_gather x2, waiting for transfers between devices: 200 us -> 214 us  [the longest x1 112 us: local(): first_weights = lax.all_gather(first_own, 'seq', axis=0, tiled=True)]
  transfers between devices with their start and end apart: 84 -> 84, of which waited for: 48 -> 28; matrix products, arithmetic and copies ran while one was open for 24% -> 23% of each run, Pallas kernels for 13% -> 11%
where the time goes in v4:
time: 818 us; the launch traced here: 812 us
  waiting for transfers between devices  357 us (44%)
  starting transfers between devices  104 us (13%)
  Pallas kernels  98.5 us (12%)
  other arithmetic  95.1 us (12%)
  matrix products  90.1 us (11%)
  local copies, waits for them, and re-layouts  52.1 us (6%)
  between operations  15 us (2%)
    all_gather x1, waiting for transfers between devices, local(): first_weights = lax.all_gather(first_own, 'seq', axis=0, tiled=True)  112 us
    all_gather x1, waiting for transfers between devices, local(): second_weights = lax.all_gather(second_own, 'seq', axis=0, tiled=True)  102 us
    ppermute x56, starting transfers between devices, send(): return [lax.ppermute(self.sums[d], 'seq', self.routes[d]) for d in range(2)]  79.6 us
    ppermute x4, waiting for transfers between devices, tp_send(): lax.ppermute(sent, 'tp', [(0, 1), (1, 0)]).astype(jnp.float32)  72.8 us
    ppermute x56, waiting for transfers between devices, send(): return [lax.ppermute(self.sums[d], 'seq', self.routes[d]) for d in range(2)]  64.9 us
    pallas_call x4, Pallas kernels, pair_terms(): pl.pallas_call(pair_kernel, grid=(planes, chips // group), in_specs=[left...  52.5 us
    convert_element_type x24, other arithmetic, take(): total.astype(jnp.bfloat16)  39.5 us
    dot_general x1, matrix products, through_gate_up(): jnp.einsum('ctf,dcf->td', grad_gate_up, gate_up_full, preferred_element_t...  18.5 us
  transfers between devices with their start and end apart: 84, of which 28 were waited for; matrix products, arithmetic and copies ran while one was open for 23% of the time, Pallas kernels for 11%

profile of v4, /device:TPU:0, one launch (start us, length us, event | category | flops | bytes accessed | tf_op | source)
XLA Modules:
  0.0 812.1 jit_solution(3763978275770978190)
XLA Ops:
  8.3 2.2 pad_maximum_fusion.3
  10.5 3.2 pad_maximum_fusion.2
  15.9 2.8 collective-permute-start.2
  24.0 3.1 collective-permute-start.4
  31.3 111.8 %all-gather.5.cloned.1.call-done = bf16[2048,4,1024]{2,0,1:T(8,128)(2,1)} async-done(((bf16[128,4,1024]{2,0,1:T(8,128)(2,1)}), bf16[2048,4,1024]{2,0,1:T(8,128)(2,1)}) %all-gather.5.cloned.1.call-update) | async-done | bytes 16777232 | tf_op jit(solution)/shard_map/all_gather | solution.py:335
  143.1 10.3 %convert_bitcast_fusion.proj_ref = bf16[3,512,1024]{2,1,0:T(8,128)(2,1)S(1)} fusion(bf16[2048,4,1024]{2,0,1:T(8,128)(2,1)} %all-gather.5.cloned.1.call-done, bf16[512,2048]{1,0:T(8,128)(2,1)} %multiply_convert_fusion.1.block_ref), kind=kOutput, calls=%fused_computation.52 | convolution fusion | flops 6444023808 | bytes 17825792 | tf_op jit(solution)/shard_map/td,dcf->ctf/dot_general | solution.py:347
  155.0 2.3 collective-permute-start.5
  159.1 12.3 %attend.1 = bf16[512,1024]{1,0:T(8,128)(2,1)} custom-call(s32[512,1]{1,0:T(8,128)} %copy.54.starts_ref, bf16[3,512,1024]{2,1,0:T(8,128)(2,1)} %copy-done.8, bf16[2,64,1024]{2,1,0:T(8,128)(2,1)} %copy-done.15), custom_call_target="tpu_custom_call" | custom-call | tf_op jit(solution)/shard_map/attend/pallas_call | solution.py:227
  171.4 4.9 fusion.29
  177.9 39.6 %collective-permute-done.6 = bf16[512,2048]{1,0:T(8,128)(2,1)S(1)} collective-permute-done((bf16[512,2048]{1,0:T(8,128)(2,1)S(1)}, bf16[512,2048]{1,0:T(8,128)(2,1)S(1)}, u32[]{:S(2)}, u32[]{:S(2)}) %collective-permute-start.6) | collective-permute-done | bytes 2097184 | tf_op jit(solution)/shard_map/ppermute | solution.py:266
  221.3 101.9 %all-gather.3.cloned.1.call-done = bf16[2048,3,2752]{0,2,1:T(8,128)(2,1)} async-done(((bf16[128,3,2752]{0,2,1:T(8,128)(2,1)}), bf16[2048,3,2752]{0,2,1:T(8,128)(2,1)}) %all-gather.3.cloned.1.call-update) | async-done | bytes 33816592 | tf_op jit(solution)/shard_map/all_gather | solution.py:336
  323.2 16.5 %convolution_bitcast_fusion = f32[2,512,2752]{2,1,0:T(8,128)S(1)} fusion(bf16[2048,3,2752]{0,2,1:T(8,128)(2,1)} %all-gather.3.cloned.1.call-done, bf16[512,2048]{1,0:T(8,128)(2,1)S(1)} %multiply_convert_fusion.block_ref), kind=kOutput, calls=%fused_computation.9 | convolution fusion | flops 11542724608 | bytes 47185920 | tf_op jit(solution)/shard_map/td,dcf->ctf/dot_general | solution.py:353
  341.6 2.5 copy-done.4
  344.0 3.2 copy.56
  347.4 4.0 select_columns.4
  351.7 12.7 %fusion.7 = f32[512,2752]{0,1:T(8,128)} fusion(bf16[512,2048]{1,0:T(8,128)(2,1)} %block_ref.1, bf16[2048,3,2752]{0,2,1:T(8,128)(2,1)} %all-gather.3.cloned.1.call-done), kind=kOutput, calls=%fused_computation.8 | convolution fusion | flops 5771362304 | bytes 19005440 | tf_op jit(solution)/shard_map/td,df->tf/dot_general | solution.py:360
  364.4 4.5 copy.57.right_two_ref
  368.9 10.8 %pair_terms.4 = bf16[8,2,1,64,2752]{4,3,2,1,0:T(8,128)(2,1)} custom-call(bf16[512,1024]{1,0:T(8,128)(2,1)} %get-tuple-element.157.left_ref, bf16[512,1024]{1,0:T(8,128)(2,1)} %collective-permute-done.left_two_ref, bf16[1,512,2752]{2,1,0:T(8,128)(2,1)} %bitcast.295, bf16[1,512,2752]{2,1,0:T(8,128)(2,1)} %copy.57.right_two_ref), custom_call_target="tpu_custom_call" | custom-call | flops 5771362304 | bytes 11272192 | tf_op jit(solution)/shard_map/pair_terms/pallas_call | solution.py:137
  382.9 6.2 copy.58
  389.2 7.8 fusion.31
  396.9 3.0 pad_maximum_fusion.right_ref
  399.9 8.3 %copy.61 = bf16[2,512,2752]{1,2,0:T(8,128)(2,1)} copy(bf16[2,512,2752]{2,1,0:T(8,128)(2,1)} %pad_maximum_fusion.right_ref) | data formatting | bytes 11272192 | tf_op jit(solution)/shard_map/optimization_barrier | solution.py:76
  408.2 4.0 select_columns.5
  416.0 18.5 %bitcast_convert_fusion.1 = bf16[512,2048]{1,0:T(8,128)(2,1)S(1)} fusion(bf16[2,512,2752]{2,1,0:T(8,128)(2,1)} %pad_maximum_fusion.right_ref, bf16[2048,3,2752]{0,2,1:T(8,128)(2,1)} %all-gather.3.cloned.1.call-done), kind=kOutput, calls=%fused_computation.33 | convolution fusion | flops 11543773184 | bytes 30408704 | tf_op jit(solution)/shard_map/ctf,dcf->td/dot_general | solution.py:372
  439.4 8.2 %copy.62.right_two_ref = bf16[2,512,2752]{2,1,0:T(8,128)(2,1)} copy(bf16[2,512,2752]{1,2,0:T(8,128)(2,1)} %collective-permute-done.15) | data formatting | bytes 11272192 | tf_op jit(solution)/shard_map/ppermute | solution.py:84
  447.6 20.0 %pair_terms.5 = bf16[8,2,2,64,2752]{4,3,2,1,0:T(8,128)(2,1)} custom-call(bf16[512,1024]{1,0:T(8,128)(2,1)} %get-tuple-element.178.left_ref, bf16[512,1024]{1,0:T(8,128)(2,1)} %collective-permute-done.14.left_two_ref, bf16[2,512,2752]{2,1,0:T(8,128)(2,1)} %pad_maximum_fusion.right_ref, bf16[2,512,2752]{2,1,0:T(8,128)(2,1)} %copy.62.right_two_ref), custom_call_target="tpu_custom_call" | custom-call | flops 11542724608 | bytes 22544384 | tf_op jit(solution)/shard_map/pair_terms/pallas_call | solution.py:137
  474.6 10.1 %fusion.28 = bf16[512,2048]{1,0:T(8,128)(2,1)} fusion(bf16[512,2752]{1,0:T(8,128)(2,1)S(1)} %copy-done.10, bf16[2048,3,2752]{0,2,1:T(8,128)(2,1)} %all-gather.3.cloned.1.call-done), kind=kOutput, calls=%fused_computation.53 | convolution fusion | flops 5772410880 | bytes 16187392 | tf_op jit(solution)/shard_map/tf,df->td/dot_general | solution.py:385
  484.6 10.2 %collective-permute-done.18 = bf16[2,64,2752]{2,1,0:T(8,128)(2,1)S(1)} collective-permute-done((bf16[2,64,2752]{2,1,0:T(8,128)(2,1)S(1)}, bf16[2,64,2752]{2,1,0:T(8,128)(2,1)S(1)}, u32[]{:S(2)}, u32[]{:S(2)}) %collective-permute-start.18) | collective-permute-done | bytes 704544 | tf_op jit(solution)/shard_map/ppermute | solution.py:54
  502.6 3.3 multiply_reduce_fusion.3
  505.9 4.8 fusion.91
  510.6 6.2 fusion.36.grad_ref
  516.9 4.5 collective-permute-done.22
  521.7 2.8 fusion.45
  529.5 2.5 convert_element_type.947
  531.9 4.0 select_columns.7
  537.3 4.0 select_columns.6
  541.4 17.6 %attend_back.1 = (bf16[3,512,1024]{2,1,0:T(8,128)(2,1)}, bf16[2,64,1024]{2,1,0:T(8,128)(2,1)}, f32[2,64,1024]{2,1,0:T(8,128)}) custom-call(s32[512,1]{1,0:T(8,128)} %copy.54.starts_ref, bf16[3,512,1024]{2,1,0:T(8,128)(2,1)} %copy-done.8, bf16[2,64,1024]{2,1,0:T(8,128)(2,1)} %copy-done.15, bf16[512,1024]{1,0:T(8,128)(2,1)} %fusion.36.grad_ref), custom_call_target="tpu_custom_call" | custom-call | tf_op jit(solution)/shard_map/attend_back/pallas_call | solution.py:245
  560.6 9.0 %collective-permute-done.26 = bf16[1,64,2752]{2,1,0:T(8,128)(2,1)S(1)} collective-permute-done((bf16[1,64,2752]{2,1,0:T(8,128)(2,1)S(1)}, bf16[1,64,2752]{2,1,0:T(8,128)(2,1)S(1)}, u32[]{:S(2)}, u32[]{:S(2)}) %collective-permute-start.26) | collective-permute-done | bytes 352288 | tf_op jit(solution)/shard_map/ppermute | solution.py:54
  570.8 2.9 fusion.43
  579.1 2.2 collective-permute-start.29
  581.4 18.2 %collective-permute-start.30 = (bf16[1,64,2752]{2,1,0:T(8,128)(2,1)S(1)}, bf16[1,64,2752]{2,1,0:T(8,128)(2,1)S(1)}, u32[]{:S(2)}, u32[]{:S(2)}) collective-permute-start(bf16[1,64,2752]{2,1,0:T(8,128)(2,1)S(1)} %get-tuple-element.218), channel_id=1, source_target_pairs={{8,0},{10,2},{16,8},{18,10},{24,16},{26,18},{28,24},{30,26},{20,28... | collective-permute-start | bytes 1056776 | tf_op jit(solution)/shard_map/ppermute | solution.py:54
  600.3 6.0 pair_terms.6
  612.1 2.2 collective-permute-start.37
  616.3 10.9 %bitcast_convert_fusion = bf16[512,2048]{1,0:T(8,128)(2,1)} fusion(bf16[3,512,1024]{2,1,0:T(8,128)(2,1)S(1)} %copy-done.25, bf16[2048,4,1024]{2,0,1:T(8,128)(2,1)} %all-gather.5.cloned.1.call-done), kind=kOutput, calls=%fused_computation.32 | convolution fusion | flops 6443499520 | bytes 17825792 | tf_op jit(solution)/shard_map/ctf,dcf->td/dot_general | solution.py:419
  627.2 6.3 collective-permute-done.38
  634.2 2.8 fusion.39
  645.0 15.7 %pair_terms.7 = bf16[8,2,3,64,1024]{4,3,2,1,0:T(8,128)(2,1)} custom-call(bf16[512,1024]{1,0:T(8,128)(2,1)} %get-tuple-element.244.left_ref, bf16[512,1024]{1,0:T(8,128)(2,1)} %copy-done.27, bf16[3,512,1024]{2,1,0:T(8,128)(2,1)} %fusion.73.right_ref, bf16[3,512,1024]{2,1,0:T(8,128)(2,1)} %collective-permute-done.45.right_two_ref), custom_call_target="tpu_custom_call" | custom-call | flops 6442450944 | bytes 12582912 | tf_op jit(solution)/shard_map/pair_terms/pallas_call | solution.py:137
  663.2 2.3 fusion.37
  670.8 10.9 %collective-permute-done.52 = bf16[512,2048]{1,0:T(8,128)(2,1)} collective-permute-done((bf16[512,2048]{1,0:T(8,128)(2,1)S(1)}, bf16[512,2048]{1,0:T(8,128)(2,1)}, u32[]{:S(2)}, u32[]{:S(2)}) %collective-permute-start.52) | collective-permute-done | bytes 2097184 | tf_op jit(solution)/shard_map/ppermute | solution.py:266
  683.7 4.1 add_convert_fusion
  687.8 2.1 collective-permute-done.49
  690.8 3.0 collective-permute-done.50
  704.0 7.6 collective-permute-done.53
  717.9 22.2 %collective-permute-done.61 = bf16[512,2048]{1,0:T(8,128)(2,1)S(1)} collective-permute-done((bf16[512,2048]{1,0:T(8,128)(2,1)}, bf16[512,2048]{1,0:T(8,128)(2,1)S(1)}, u32[]{:S(2)}, u32[]{:S(2)}) %collective-permute-start.61) | collective-permute-done | bytes 2097184 | tf_op jit(solution)/shard_map/ppermute | solution.py:266
  742.1 3.1 multiply_reduce_fusion
  745.2 4.9 fusion.19
  750.8 2.9 copy.66
  753.7 2.2 copy.65
  762.6 3.9 collective-permute-done.66
  774.1 3.7 collective-permute-done.67
  779.9 2.8 collective-permute-start.68
  785.9 3.5 collective-permute-done.68
  789.4 2.8 collective-permute-done.72
  798.2 3.1 collective-permute-done.69
  (285 shorter events, 140.9 us)
Async XLA Ops:
  7.2 135.9 %all-gather.5.cloned.1.call-start = ((), (), s32[]{:S(2)}) async-start(), calls=%async_computation.1 | async-start | bytes 17825792 | tf_op jit(solution)/shard_map/all_gather | solution.py:335
  13.8 309.4 %all-gather.3.cloned.1.call-start = ((), (), s32[]{:S(2)}) async-start(), calls=%async_computation | async-start | bytes 35930112 | tf_op jit(solution)/shard_map/all_gather | solution.py:336
  176.3 41.2 %collective-permute-start.6 = (bf16[512,2048]{1,0:T(8,128)(2,1)S(1)}, bf16[512,2048]{1,0:T(8,128)(2,1)S(1)}, u32[]{:S(2)}, u32[]{:S(2)}) collective-permute-start(bf16[512,2048]{1,0:T(8,128)(2,1)S(1)} %fusion.29), channel_id=1, source_target_pairs={{0,1},{1,0},{2,3},{3,2},{4,5},{5,4},{6,7},{7,6},{8,9},{9,8},{10,11... | collective-permute-start | bytes 6291464 | tf_op jit(solution)/shard_map/ppermute | solution.py:266
  347.2 17.2 %collective-permute-start.7 = (bf16[1,512,2752]{1,2,0:T(8,128)(2,1)}, bf16[1,512,2752]{1,2,0:T(8,128)(2,1)}, u32[]{:S(2)}, u32[]{:S(2)}) collective-permute-start(bf16[1,512,2752]{1,2,0:T(8,128)(2,1)} %copy.56), channel_id=1, source_target_pairs={{0,2},{2,0},{4,6},{6,4},{8,10},{10,8},{12,14},{14,12},{16,18},{18,... | collective-permute-start | bytes 8454152 | tf_op jit(solution)/shard_map/ppermute | solution.py:84
  351.4 17.5 %collective-permute-start = (bf16[512,1024]{1,0:T(8,128)(2,1)}, bf16[512,1024]{1,0:T(8,128)(2,1)}, u32[]{:S(2)}, u32[]{:S(2)}) collective-permute-start(bf16[512,1024]{1,0:T(8,128)(2,1)} %get-tuple-element.158), channel_id=1, source_target_pairs={{0,2},{2,0},{4,6},{6,4},{8,10},{10,8},{12,14},{14,12},{16,18},{18,... | collective-permute-start | bytes 3145736 | tf_op jit(solution)/shard_map/ppermute | solution.py:84
  380.9 19.1 %collective-permute-start.8 = (bf16[1,64,2752]{2,1,0:T(8,128)(2,1)S(1)}, bf16[1,64,2752]{2,1,0:T(8,128)(2,1)S(1)}, u32[]{:S(2)}, u32[]{:S(2)}) collective-permute-start(bf16[1,64,2752]{2,1,0:T(8,128)(2,1)S(1)} %get-tuple-element.164), channel_id=1, source_target_pairs={{0,8},{2,10},{8,16},{10,18},{16,24},{18,26},{24,28},{26,30},{28,20... | collective-permute-start | bytes 1056776 | tf_op jit(solution)/shard_map/ppermute | solution.py:54
  381.4 18.5 %collective-permute-start.9 = (bf16[1,64,2752]{2,1,0:T(8,128)(2,1)S(1)}, bf16[1,64,2752]{2,1,0:T(8,128)(2,1)S(1)}, u32[]{:S(2)}, u32[]{:S(2)}) collective-permute-start(bf16[1,64,2752]{2,1,0:T(8,128)(2,1)S(1)} %get-tuple-element.165), channel_id=1, source_target_pairs={{8,0},{10,2},{16,8},{18,10},{24,16},{26,18},{28,24},{30,26},{20,28... | collective-permute-start | bytes 1056776 | tf_op jit(solution)/shard_map/ppermute | solution.py:54
  408.2 31.2 %collective-permute-start.15 = (bf16[2,512,2752]{1,2,0:T(8,128)(2,1)}, bf16[2,512,2752]{1,2,0:T(8,128)(2,1)}, u32[]{:S(2)}, u32[]{:S(2)}) collective-permute-start(bf16[2,512,2752]{1,2,0:T(8,128)(2,1)} %copy.61), channel_id=1, source_target_pairs={{0,2},{2,0},{4,6},{6,4},{8,10},{10,8},{12,14},{14,12},{16,18},{18,... | collective-permute-start | bytes 16908296 | tf_op jit(solution)/shard_map/ppermute | solution.py:84
  412.2 35.4 %collective-permute-start.14 = (bf16[512,1024]{1,0:T(8,128)(2,1)}, bf16[512,1024]{1,0:T(8,128)(2,1)}, u32[]{:S(2)}, u32[]{:S(2)}) collective-permute-start(bf16[512,1024]{1,0:T(8,128)(2,1)} %get-tuple-element.179), channel_id=1, source_target_pairs={{0,2},{2,0},{4,6},{6,4},{8,10},{10,8},{12,14},{14,12},{16,18},{18,... | collective-permute-start | bytes 3145736 | tf_op jit(solution)/shard_map/ppermute | solution.py:84
  414.0 20.6 %collective-permute-start.10 = (bf16[1,64,2752]{2,1,0:T(8,128)(2,1)S(1)}, bf16[1,64,2752]{2,1,0:T(8,128)(2,1)S(1)}, u32[]{:S(2)}, u32[]{:S(2)}) collective-permute-start(bf16[1,64,2752]{2,1,0:T(8,128)(2,1)S(1)} %get-tuple-element.171), channel_id=1, source_target_pairs={{0,8},{2,10},{8,16},{10,18},{16,24},{18,26},{24,28},{26,30},{28,20... | collective-permute-start | bytes 1056776 | tf_op jit(solution)/shard_map/ppermute | solution.py:54
  414.5 20.0 %collective-permute-start.11 = (bf16[1,64,2752]{2,1,0:T(8,128)(2,1)S(1)}, bf16[1,64,2752]{2,1,0:T(8,128)(2,1)S(1)}, u32[]{:S(2)}, u32[]{:S(2)}) collective-permute-start(bf16[1,64,2752]{2,1,0:T(8,128)(2,1)S(1)} %get-tuple-element.172), channel_id=1, source_target_pairs={{8,0},{10,2},{16,8},{18,10},{24,16},{26,18},{28,24},{30,26},{20,28... | collective-permute-start | bytes 1056776 | tf_op jit(solution)/shard_map/ppermute | solution.py:54
  435.8 31.8 %collective-permute-start.12 = (bf16[1,64,2752]{2,1,0:T(8,128)(2,1)S(1)}, bf16[1,64,2752]{2,1,0:T(8,128)(2,1)S(1)}, u32[]{:S(2)}, u32[]{:S(2)}) collective-permute-start(bf16[1,64,2752]{2,1,0:T(8,128)(2,1)S(1)} %get-tuple-element.176), channel_id=1, source_target_pairs={{0,8},{2,10},{8,16},{10,18},{16,24},{18,26},{24,28},{26,30},{28,20... | collective-permute-start | bytes 1056776 | tf_op jit(solution)/shard_map/ppermute | solution.py:54
  436.4 31.2 %collective-permute-start.13 = (bf16[1,64,2752]{2,1,0:T(8,128)(2,1)S(1)}, bf16[1,64,2752]{2,1,0:T(8,128)(2,1)S(1)}, u32[]{:S(2)}, u32[]{:S(2)}) collective-permute-start(bf16[1,64,2752]{2,1,0:T(8,128)(2,1)S(1)} %get-tuple-element.177), channel_id=1, source_target_pairs={{8,0},{10,2},{16,8},{18,10},{24,16},{26,18},{28,24},{30,26},{20,28... | collective-permute-start | bytes 1056776 | tf_op jit(solution)/shard_map/ppermute | solution.py:54
  437.9 64.6 %collective-permute-start.24 = (bf16[512,2048]{1,0:T(8,128)(2,1)S(1)}, bf16[512,2048]{1,0:T(8,128)(2,1)}, u32[]{:S(2)}, u32[]{:S(2)}) collective-permute-start(bf16[512,2048]{1,0:T(8,128)(2,1)S(1)} %bitcast_convert_fusion.1), channel_id=1, source_target_pairs={{0,1},{1,0},{2,3},{3,2},{4,5},{5,4},{6,7},{7,6},{8,9},{9,8},{10,11... | collective-permute-start | bytes 6291464 | tf_op jit(solution)/shard_map/ppermute | solution.py:266
  470.5 14.2 %collective-permute-start.16 = (bf16[1,64,2752]{2,1,0:T(8,128)(2,1)S(1)}, bf16[1,64,2752]{2,1,0:T(8,128)(2,1)S(1)}, u32[]{:S(2)}, u32[]{:S(2)}) collective-permute-start(bf16[1,64,2752]{2,1,0:T(8,128)(2,1)S(1)} %get-tuple-element.184), channel_id=1, source_target_pairs={{0,8},{2,10},{8,16},{10,18},{16,24},{18,26},{24,28},{26,30},{28,20... | collective-permute-start | bytes 1056776 | tf_op jit(solution)/shard_map/ppermute | solution.py:54
  471.0 13.6 %collective-permute-start.17 = (bf16[1,64,2752]{2,1,0:T(8,128)(2,1)S(1)}, bf16[1,64,2752]{2,1,0:T(8,128)(2,1)S(1)}, u32[]{:S(2)}, u32[]{:S(2)}) collective-permute-start(bf16[1,64,2752]{2,1,0:T(8,128)(2,1)S(1)} %get-tuple-element.185), channel_id=1, source_target_pairs={{8,0},{10,2},{16,8},{18,10},{24,16},{26,18},{28,24},{30,26},{20,28... | collective-permute-start | bytes 1056776 | tf_op jit(solution)/shard_map/ppermute | solution.py:54
  472.5 22.3 %collective-permute-start.18 = (bf16[2,64,2752]{2,1,0:T(8,128)(2,1)S(1)}, bf16[2,64,2752]{2,1,0:T(8,128)(2,1)S(1)}, u32[]{:S(2)}, u32[]{:S(2)}) collective-permute-start(bf16[2,64,2752]{2,1,0:T(8,128)(2,1)S(1)} %get-tuple-element.186), channel_id=1, source_target_pairs={{0,8},{2,10},{8,16},{10,18},{16,24},{18,26},{24,28},{26,30},{28,20... | collective-permute-start | bytes 2113544 | tf_op jit(solution)/shard_map/ppermute | solution.py:54
  473.0 22.1 %collective-permute-start.19 = (bf16[2,64,2752]{2,1,0:T(8,128)(2,1)S(1)}, bf16[2,64,2752]{2,1,0:T(8,128)(2,1)S(1)}, u32[]{:S(2)}, u32[]{:S(2)}) collective-permute-start(bf16[2,64,2752]{2,1,0:T(8,128)(2,1)S(1)} %get-tuple-element.187), channel_id=1, source_target_pairs={{8,0},{10,2},{16,8},{18,10},{24,16},{26,18},{28,24},{30,26},{20,28... | collective-permute-start | bytes 2113544 | tf_op jit(solution)/shard_map/ppermute | solution.py:54
  498.1 18.8 %collective-permute-start.20 = (bf16[1,64,2752]{2,1,0:T(8,128)(2,1)S(1)}, bf16[1,64,2752]{2,1,0:T(8,128)(2,1)S(1)}, u32[]{:S(2)}, u32[]{:S(2)}) collective-permute-start(bf16[1,64,2752]{2,1,0:T(8,128)(2,1)S(1)} %get-tuple-element.193), channel_id=1, source_target_pairs={{0,8},{2,10},{8,16},{10,18},{16,24},{18,26},{24,28},{26,30},{28,20... | collective-permute-start | bytes 1056776 | tf_op jit(solution)/shard_map/ppermute | solution.py:54
  498.7 18.2 %collective-permute-start.21 = (bf16[1,64,2752]{2,1,0:T(8,128)(2,1)S(1)}, bf16[1,64,2752]{2,1,0:T(8,128)(2,1)S(1)}, u32[]{:S(2)}, u32[]{:S(2)}) collective-permute-start(bf16[1,64,2752]{2,1,0:T(8,128)(2,1)S(1)} %get-tuple-element.194), channel_id=1, source_target_pairs={{8,0},{10,2},{16,8},{18,10},{24,16},{26,18},{28,24},{30,26},{20,28... | collective-permute-start | bytes 1056776 | tf_op jit(solution)/shard_map/ppermute | solution.py:54
  500.1 21.3 %collective-permute-start.22 = (bf16[2,64,2752]{2,1,0:T(8,128)(2,1)S(1)}, bf16[2,64,2752]{2,1,0:T(8,128)(2,1)S(1)}, u32[]{:S(2)}, u32[]{:S(2)}) collective-permute-start(bf16[2,64,2752]{2,1,0:T(8,128)(2,1)S(1)} %get-tuple-element.195), channel_id=1, source_target_pairs={{0,8},{2,10},{8,16},{10,18},{16,24},{18,26},{24,28},{26,30},{28,20... | collective-permute-start | bytes 2113544 | tf_op jit(solution)/shard_map/ppermute | solution.py:54
  500.7 20.9 %collective-permute-start.23 = (bf16[2,64,2752]{2,1,0:T(8,128)(2,1)S(1)}, bf16[2,64,2752]{2,1,0:T(8,128)(2,1)S(1)}, u32[]{:S(2)}, u32[]{:S(2)}) collective-permute-start(bf16[2,64,2752]{2,1,0:T(8,128)(2,1)S(1)} %get-tuple-element.196), channel_id=1, source_target_pairs={{8,0},{10,2},{16,8},{18,10},{24,16},{26,18},{28,24},{30,26},{20,28... | collective-permute-start | bytes 2113544 | tf_op jit(solution)/shard_map/ppermute | solution.py:54
  526.5 44.3 %collective-permute-start.27 = (bf16[2,64,2752]{2,1,0:T(8,128)(2,1)}, bf16[2,64,2752]{2,1,0:T(8,128)(2,1)}, u32[]{:S(2)}, u32[]{:S(2)}) collective-permute-start(bf16[2,64,2752]{2,1,0:T(8,128)(2,1)} %get-tuple-element.206), channel_id=1, source_target_pairs={{0,8},{2,10},{8,16},{10,18},{16,24},{18,26},{24,28},{26,30},{28,20... | collective-permute-start | bytes 2113544 | tf_op jit(solution)/shard_map/ppermute | solution.py:54
  527.1 43.7 %collective-permute-start.28 = (bf16[2,64,2752]{2,1,0:T(8,128)(2,1)}, bf16[2,64,2752]{2,1,0:T(8,128)(2,1)}, u32[]{:S(2)}, u32[]{:S(2)}) collective-permute-start(bf16[2,64,2752]{2,1,0:T(8,128)(2,1)} %get-tuple-element.207), channel_id=1, source_target_pairs={{8,0},{10,2},{16,8},{18,10},{24,16},{26,18},{28,24},{30,26},{20,28... | collective-permute-start | bytes 2113544 | tf_op jit(solution)/shard_map/ppermute | solution.py:54
  528.5 30.5 %collective-permute-start.78 = (f32[1024]{0:T(1024)S(1)}, f32[1024]{0:T(1024)S(1)}, u32[]{:S(2)}, u32[]{:S(2)}) collective-permute-start(f32[1024]{0:T(1024)S(1)} %slice_select_fusion), channel_id=1, source_target_pairs={{0,16},{2,18},{4,20},{6,22},{8,24},{10,26},{12,28},{14,30},{16,0},... | collective-permute-start | bytes 12296 | tf_op jit(solution)/shard_map/ppermute | solution.py:294
  535.9 43.2 %collective-permute-start.34 = (bf16[1,512,1024]{2,1,0:T(8,128)(2,1)S(1)}, bf16[1,512,1024]{2,1,0:T(8,128)(2,1)}, u32[]{:S(2)}, u32[]{:S(2)}) collective-permute-start(bf16[1,512,1024]{2,1,0:T(8,128)(2,1)S(1)} %bitcast.298), channel_id=1, source_target_pairs={{0,2},{2,0},{4,6},{6,4},{8,10},{10,8},{12,14},{14,12},{16,18},{18,... | collective-permute-start | bytes 3145736 | tf_op jit(solution)/shard_map/ppermute | solution.py:84
  536.0 24.4 %collective-permute-start.25 = (bf16[1,64,2752]{2,1,0:T(8,128)(2,1)}, bf16[1,64,2752]{2,1,0:T(8,128)(2,1)S(1)}, u32[]{:S(2)}, u32[]{:S(2)}) collective-permute-start(bf16[1,64,2752]{2,1,0:T(8,128)(2,1)} %get-tuple-element.204), channel_id=1, source_target_pairs={{0,8},{2,10},{8,16},{10,18},{16,24},{18,26},{24,28},{26,30},{28,20... | collective-permute-start | bytes 1056776 | tf_op jit(solution)/shard_map/ppermute | solution.py:54
  559.0 10.5 %collective-permute-start.26 = (bf16[1,64,2752]{2,1,0:T(8,128)(2,1)S(1)}, bf16[1,64,2752]{2,1,0:T(8,128)(2,1)S(1)}, u32[]{:S(2)}, u32[]{:S(2)}) collective-permute-start(bf16[1,64,2752]{2,1,0:T(8,128)(2,1)S(1)} %get-tuple-element.205), channel_id=1, source_target_pairs={{8,0},{10,2},{16,8},{18,10},{24,16},{26,18},{28,24},{30,26},{20,28... | collective-permute-start | bytes 1056776 | tf_op jit(solution)/shard_map/ppermute | solution.py:54
  560.4 40.0 %collective-permute-start.33 = (bf16[512,1024]{1,0:T(8,128)(2,1)}, bf16[512,1024]{1,0:T(8,128)(2,1)}, u32[]{:S(2)}, u32[]{:S(2)}) collective-permute-start(bf16[512,1024]{1,0:T(8,128)(2,1)} %get-tuple-element.223), channel_id=1, source_target_pairs={{0,2},{2,0},{4,6},{6,4},{8,10},{10,8},{12,14},{14,12},{16,18},{18,... | collective-permute-start | bytes 3145736 | tf_op jit(solution)/shard_map/ppermute | solution.py:84
  575.7 32.5 %collective-permute-start.31 = (bf16[2,64,2752]{2,1,0:T(8,128)(2,1)}, bf16[2,64,2752]{2,1,0:T(8,128)(2,1)S(1)}, u32[]{:S(2)}, u32[]{:S(2)}) collective-permute-start(bf16[2,64,2752]{2,1,0:T(8,128)(2,1)} %get-tuple-element.219), channel_id=1, source_target_pairs={{0,8},{2,10},{8,16},{10,18},{16,24},{18,26},{24,28},{26,30},{28,20... | collective-permute-start | bytes 2113544 | tf_op jit(solution)/shard_map/ppermute | solution.py:54
  576.5 31.7 %collective-permute-start.32 = (bf16[2,64,2752]{2,1,0:T(8,128)(2,1)S(1)}, bf16[2,64,2752]{2,1,0:T(8,128)(2,1)}, u32[]{:S(2)}, u32[]{:S(2)}) collective-permute-start(bf16[2,64,2752]{2,1,0:T(8,128)(2,1)S(1)} %get-tuple-element.220), channel_id=1, source_target_pairs={{8,0},{10,2},{16,8},{18,10},{24,16},{26,18},{28,24},{30,26},{20,28... | collective-permute-start | bytes 2113544 | tf_op jit(solution)/shard_map/ppermute | solution.py:54
  579.1 27.2 %collective-permute-start.29 = (bf16[1,64,2752]{2,1,0:T(8,128)(2,1)}, bf16[1,64,2752]{2,1,0:T(8,128)(2,1)S(1)}, u32[]{:S(2)}, u32[]{:S(2)}) collective-permute-start(bf16[1,64,2752]{2,1,0:T(8,128)(2,1)} %get-tuple-element.217), channel_id=1, source_target_pairs={{0,8},{2,10},{8,16},{10,18},{16,24},{18,26},{24,28},{26,30},{28,20... | collective-permute-start | bytes 1056776 | tf_op jit(solution)/shard_map/ppermute | solution.py:54
  581.4 26.9 %collective-permute-start.30 = (bf16[1,64,2752]{2,1,0:T(8,128)(2,1)S(1)}, bf16[1,64,2752]{2,1,0:T(8,128)(2,1)S(1)}, u32[]{:S(2)}, u32[]{:S(2)}) collective-permute-start(bf16[1,64,2752]{2,1,0:T(8,128)(2,1)S(1)} %get-tuple-element.218), channel_id=1, source_target_pairs={{8,0},{10,2},{16,8},{18,10},{24,16},{26,18},{28,24},{30,26},{20,28... | collective-permute-start | bytes 1056776 | tf_op jit(solution)/shard_map/ppermute | solution.py:54
  609.4 33.8 %collective-permute-start.45 = (bf16[3,512,1024]{2,1,0:T(8,128)(2,1)}, bf16[3,512,1024]{2,1,0:T(8,128)(2,1)}, u32[]{:S(2)}, u32[]{:S(2)}) collective-permute-start(bf16[3,512,1024]{2,1,0:T(8,128)(2,1)} %fusion.73.right_ref), channel_id=1, source_target_pairs={{0,2},{2,0},{4,6},{6,4},{8,10},{10,8},{12,14},{14,12},{16,18},{18,... | collective-permute-start | bytes 9437192 | tf_op jit(solution)/shard_map/ppermute | solution.py:84
  611.4 22.8 %collective-permute-start.36 = (bf16[2,64,2752]{2,1,0:T(8,128)(2,1)S(1)}, bf16[2,64,2752]{2,1,0:T(8,128)(2,1)S(1)}, u32[]{:S(2)}, u32[]{:S(2)}) collective-permute-start(bf16[2,64,2752]{2,1,0:T(8,128)(2,1)S(1)} %get-tuple-element.231), channel_id=1, source_target_pairs={{0,8},{2,10},{8,16},{10,18},{16,24},{18,26},{24,28},{26,30},{28,20... | collective-permute-start | bytes 2113544 | tf_op jit(solution)/shard_map/ppermute | solution.py:54
  612.1 22.1 %collective-permute-start.37 = (bf16[2,64,2752]{2,1,0:T(8,128)(2,1)S(1)}, bf16[2,64,2752]{2,1,0:T(8,128)(2,1)S(1)}, u32[]{:S(2)}, u32[]{:S(2)}) collective-permute-start(bf16[2,64,2752]{2,1,0:T(8,128)(2,1)S(1)} %get-tuple-element.232), channel_id=1, source_target_pairs={{8,0},{10,2},{16,8},{18,10},{24,16},{26,18},{28,24},{30,26},{20,28... | collective-permute-start | bytes 2113544 | tf_op jit(solution)/shard_map/ppermute | solution.py:54
  614.3 19.3 %collective-permute-start.38 = (bf16[1,64,1024]{2,1,0:T(8,128)(2,1)S(1)}, bf16[1,64,1024]{2,1,0:T(8,128)(2,1)S(1)}, u32[]{:S(2)}, u32[]{:S(2)}) collective-permute-start(bf16[1,64,1024]{2,1,0:T(8,128)(2,1)S(1)} %get-tuple-element.233), channel_id=1, source_target_pairs={{0,8},{2,10},{8,16},{10,18},{16,24},{18,26},{24,28},{26,30},{28,20... | collective-permute-start | bytes 393224 | tf_op jit(solution)/shard_map/ppermute | solution.py:54
  614.3 19.3 %collective-permute-start.39 = (bf16[1,64,1024]{2,1,0:T(8,128)(2,1)S(1)}, bf16[1,64,1024]{2,1,0:T(8,128)(2,1)S(1)}, u32[]{:S(2)}, u32[]{:S(2)}) collective-permute-start(bf16[1,64,1024]{2,1,0:T(8,128)(2,1)S(1)} %get-tuple-element.234), channel_id=1, source_target_pairs={{8,0},{10,2},{16,8},{18,10},{24,16},{26,18},{28,24},{30,26},{20,28... | collective-permute-start | bytes 393224 | tf_op jit(solution)/shard_map/ppermute | solution.py:54
  633.6 48.1 %collective-permute-start.52 = (bf16[512,2048]{1,0:T(8,128)(2,1)S(1)}, bf16[512,2048]{1,0:T(8,128)(2,1)}, u32[]{:S(2)}, u32[]{:S(2)}) collective-permute-start(bf16[512,2048]{1,0:T(8,128)(2,1)S(1)} %copy-done.14), channel_id=1, source_target_pairs={{0,1},{1,0},{2,3},{3,2},{4,5},{5,4},{6,7},{7,6},{8,9},{9,8},{10,11... | collective-permute-start | bytes 6291464 | tf_op jit(solution)/shard_map/ppermute | solution.py:266
  638.7 22.0 %collective-permute-start.40 = (bf16[2,64,2752]{2,1,0:T(8,128)(2,1)}, bf16[2,64,2752]{2,1,0:T(8,128)(2,1)}, u32[]{:S(2)}, u32[]{:S(2)}) collective-permute-start(bf16[2,64,2752]{2,1,0:T(8,128)(2,1)} %get-tuple-element.240), channel_id=1, source_target_pairs={{0,8},{2,10},{8,16},{10,18},{16,24},{18,26},{24,28},{26,30},{28,20... | collective-permute-start | bytes 2113544 | tf_op jit(solution)/shard_map/ppermute | solution.py:54
  638.9 21.7 %collective-permute-start.41 = (bf16[2,64,2752]{2,1,0:T(8,128)(2,1)}, bf16[2,64,2752]{2,1,0:T(8,128)(2,1)}, u32[]{:S(2)}, u32[]{:S(2)}) collective-permute-start(bf16[2,64,2752]{2,1,0:T(8,128)(2,1)} %get-tuple-element.241), channel_id=1, source_target_pairs={{8,0},{10,2},{16,8},{18,10},{24,16},{26,18},{28,24},{30,26},{20,28... | collective-permute-start | bytes 2113544 | tf_op jit(solution)/shard_map/ppermute | solution.py:54
  643.0 17.7 %collective-permute-start.42 = (bf16[1,64,1024]{2,1,0:T(8,128)(2,1)}, bf16[1,64,1024]{2,1,0:T(8,128)(2,1)}, u32[]{:S(2)}, u32[]{:S(2)}) collective-permute-start(bf16[1,64,1024]{2,1,0:T(8,128)(2,1)} %get-tuple-element.242), channel_id=1, source_target_pairs={{0,8},{2,10},{8,16},{10,18},{16,24},{18,26},{24,28},{26,30},{28,20... | collective-permute-start | bytes 393224 | tf_op jit(solution)/shard_map/ppermute | solution.py:54
  643.2 17.5 %collective-permute-start.43 = (bf16[1,64,1024]{2,1,0:T(8,128)(2,1)}, bf16[1,64,1024]{2,1,0:T(8,128)(2,1)}, u32[]{:S(2)}, u32[]{:S(2)}) collective-permute-start(bf16[1,64,1024]{2,1,0:T(8,128)(2,1)} %get-tuple-element.243), channel_id=1, source_target_pairs={{8,0},{10,2},{16,8},{18,10},{24,16},{26,18},{28,24},{30,26},{20,28... | collective-permute-start | bytes 393224 | tf_op jit(solution)/shard_map/ppermute | solution.py:54
  665.5 16.2 %collective-permute-start.48 = (bf16[1,64,1024]{2,1,0:T(8,128)(2,1)S(1)}, bf16[1,64,1024]{2,1,0:T(8,128)(2,1)S(1)}, u32[]{:S(2)}, u32[]{:S(2)}) collective-permute-start(bf16[1,64,1024]{2,1,0:T(8,128)(2,1)S(1)} %get-tuple-element.254), channel_id=1, source_target_pairs={{0,8},{2,10},{8,16},{10,18},{16,24},{18,26},{24,28},{26,30},{28,20... | collective-permute-start | bytes 393224 | tf_op jit(solution)/shard_map/ppermute | solution.py:54
  667.0 28.4 %collective-permute-start.46 = (bf16[2,64,2752]{2,1,0:T(8,128)(2,1)S(1)}, bf16[2,64,2752]{2,1,0:T(8,128)(2,1)S(1)}, u32[]{:S(2)}, u32[]{:S(2)}) collective-permute-start(bf16[2,64,2752]{2,1,0:T(8,128)(2,1)S(1)} %get-tuple-element.252), channel_id=1, source_target_pairs={{0,8},{2,10},{8,16},{10,18},{16,24},{18,26},{24,28},{26,30},{28,20... | collective-permute-start | bytes 2113544 | tf_op jit(solution)/shard_map/ppermute | solution.py:54
  668.1 27.2 %collective-permute-start.47 = (bf16[2,64,2752]{2,1,0:T(8,128)(2,1)S(1)}, bf16[2,64,2752]{2,1,0:T(8,128)(2,1)S(1)}, u32[]{:S(2)}, u32[]{:S(2)}) collective-permute-start(bf16[2,64,2752]{2,1,0:T(8,128)(2,1)S(1)} %get-tuple-element.253), channel_id=1, source_target_pairs={{8,0},{10,2},{16,8},{18,10},{24,16},{26,18},{28,24},{30,26},{20,28... | collective-permute-start | bytes 2113544 | tf_op jit(solution)/shard_map/ppermute | solution.py:54
  669.0 20.9 %collective-permute-start.49 = (bf16[1,64,1024]{2,1,0:T(8,128)(2,1)S(1)}, bf16[1,64,1024]{2,1,0:T(8,128)(2,1)S(1)}, u32[]{:S(2)}, u32[]{:S(2)}) collective-permute-start(bf16[1,64,1024]{2,1,0:T(8,128)(2,1)S(1)} %get-tuple-element.255), channel_id=1, source_target_pairs={{8,0},{10,2},{16,8},{18,10},{24,16},{26,18},{28,24},{30,26},{20,28... | collective-permute-start | bytes 393224 | tf_op jit(solution)/shard_map/ppermute | solution.py:54
  681.7 12.1 %collective-permute-start.50 = (bf16[3,64,1024]{2,1,0:T(8,128)(2,1)S(1)}, bf16[3,64,1024]{2,1,0:T(8,128)(2,1)S(1)}, u32[]{:S(2)}, u32[]{:S(2)}) collective-permute-start(bf16[3,64,1024]{2,1,0:T(8,128)(2,1)S(1)} %get-tuple-element.256), channel_id=1, source_target_pairs={{0,8},{2,10},{8,16},{10,18},{16,24},{18,26},{24,28},{26,30},{28,20... | collective-permute-start | bytes 1179656 | tf_op jit(solution)/shard_map/ppermute | solution.py:54
  681.7 13.6 %collective-permute-start.51 = (bf16[3,64,1024]{2,1,0:T(8,128)(2,1)S(1)}, bf16[3,64,1024]{2,1,0:T(8,128)(2,1)S(1)}, u32[]{:S(2)}, u32[]{:S(2)}) collective-permute-start(bf16[3,64,1024]{2,1,0:T(8,128)(2,1)S(1)} %get-tuple-element.257), channel_id=1, source_target_pairs={{8,0},{10,2},{16,8},{18,10},{24,16},{26,18},{28,24},{30,26},{20,28... | collective-permute-start | bytes 1179656 | tf_op jit(solution)/shard_map/ppermute | solution.py:54
  689.9 12.0 %collective-permute-start.80 = (f32[256]{0:T(256)S(1)}, f32[256]{0:T(256)S(1)}, u32[]{:S(2)}, u32[]{:S(2)}) collective-permute-start(f32[256]{0:T(256)S(1)} %broadcast_select_fusion.4), channel_id=1, source_target_pairs={{0,4},{2,6},{4,0},{6,2},{8,12},{10,14},{12,8},{14,10},{16,20},{18,... | collective-permute-start | bytes 3080 | tf_op jit(solution)/shard_map/ppermute | solution.py:294
  693.8 46.3 %collective-permute-start.61 = (bf16[512,2048]{1,0:T(8,128)(2,1)}, bf16[512,2048]{1,0:T(8,128)(2,1)S(1)}, u32[]{:S(2)}, u32[]{:S(2)}) collective-permute-start(bf16[512,2048]{1,0:T(8,128)(2,1)} %bitcast_convert_fusion), channel_id=1, source_target_pairs={{0,1},{1,0},{2,3},{3,2},{4,5},{5,4},{6,7},{7,6},{8,9},{9,8},{10,11... | collective-permute-start | bytes 6291464 | tf_op jit(solution)/shard_map/ppermute | solution.py:266
  699.8 12.0 %collective-permute-start.55 = (bf16[3,64,1024]{2,1,0:T(8,128)(2,1)S(1)}, bf16[3,64,1024]{2,1,0:T(8,128)(2,1)S(1)}, u32[]{:S(2)}, u32[]{:S(2)}) collective-permute-start(bf16[3,64,1024]{2,1,0:T(8,128)(2,1)S(1)} %get-tuple-element.271), channel_id=1, source_target_pairs={{0,8},{2,10},{8,16},{10,18},{16,24},{18,26},{24,28},{26,30},{28,20... | collective-permute-start | bytes 1179656 | tf_op jit(solution)/shard_map/ppermute | solution.py:54
  700.8 11.0 %collective-permute-start.56 = (bf16[3,64,1024]{2,1,0:T(8,128)(2,1)S(1)}, bf16[3,64,1024]{2,1,0:T(8,128)(2,1)S(1)}, u32[]{:S(2)}, u32[]{:S(2)}) collective-permute-start(bf16[3,64,1024]{2,1,0:T(8,128)(2,1)S(1)} %get-tuple-element.272), channel_id=1, source_target_pairs={{8,0},{10,2},{16,8},{18,10},{24,16},{26,18},{28,24},{30,26},{20,28... | collective-permute-start | bytes 1179656 | tf_op jit(solution)/shard_map/ppermute | solution.py:54
  701.9 9.7 %collective-permute-start.53 = (bf16[1,64,1024]{2,1,0:T(8,128)(2,1)S(1)}, bf16[1,64,1024]{2,1,0:T(8,128)(2,1)S(1)}, u32[]{:S(2)}, u32[]{:S(2)}) collective-permute-start(bf16[1,64,1024]{2,1,0:T(8,128)(2,1)S(1)} %get-tuple-element.269), channel_id=1, source_target_pairs={{0,8},{2,10},{8,16},{10,18},{16,24},{18,26},{24,28},{26,30},{28,20... | collective-permute-start | bytes 393224 | tf_op jit(solution)/shard_map/ppermute | solution.py:54
  711.6 38.7 %collective-permute-start.81 = (f32[128]{0:T(128)S(1)}, f32[128]{0:T(128)S(1)}, u32[]{:S(2)}, u32[]{:S(2)}) collective-permute-start(f32[128]{0:T(128)S(1)} %broadcast_select_fusion.6), channel_id=1, source_target_pairs={{0,2},{2,0},{4,6},{6,4},{8,10},{10,8},{12,14},{14,12},{16,18},{18,... | collective-permute-start | bytes 1544 | tf_op jit(solution)/shard_map/ppermute | solution.py:294
  714.3 35.9 %collective-permute-start.57 = (bf16[1,64,1024]{2,1,0:T(8,128)(2,1)S(1)}, bf16[1,64,1024]{2,1,0:T(8,128)(2,1)S(1)}, u32[]{:S(2)}, u32[]{:S(2)}) collective-permute-start(bf16[1,64,1024]{2,1,0:T(8,128)(2,1)S(1)} %get-tuple-element.278), channel_id=1, source_target_pairs={{0,8},{2,10},{8,16},{10,18},{16,24},{18,26},{24,28},{26,30},{28,20... | collective-permute-start | bytes 393224 | tf_op jit(solution)/shard_map/ppermute | solution.py:54
  715.5 34.7 %collective-permute-start.58 = (bf16[1,64,1024]{2,1,0:T(8,128)(2,1)S(1)}, bf16[1,64,1024]{2,1,0:T(8,128)(2,1)S(1)}, u32[]{:S(2)}, u32[]{:S(2)}) collective-permute-start(bf16[1,64,1024]{2,1,0:T(8,128)(2,1)S(1)} %get-tuple-element.279), channel_id=1, source_target_pairs={{8,0},{10,2},{16,8},{18,10},{24,16},{26,18},{28,24},{30,26},{20,28... | collective-permute-start | bytes 393224 | tf_op jit(solution)/shard_map/ppermute | solution.py:54
  716.4 33.8 %collective-permute-start.59 = (bf16[3,64,1024]{2,1,0:T(8,128)(2,1)S(1)}, bf16[3,64,1024]{2,1,0:T(8,128)(2,1)S(1)}, u32[]{:S(2)}, u32[]{:S(2)}) collective-permute-start(bf16[3,64,1024]{2,1,0:T(8,128)(2,1)S(1)} %get-tuple-element.280), channel_id=1, source_target_pairs={{0,8},{2,10},{8,16},{10,18},{16,24},{18,26},{24,28},{26,30},{28,20... | collective-permute-start | bytes 1179656 | tf_op jit(solution)/shard_map/ppermute | solution.py:54
  740.1 10.0 %collective-permute-start.60 = (bf16[3,64,1024]{2,1,0:T(8,128)(2,1)S(1)}, bf16[3,64,1024]{2,1,0:T(8,128)(2,1)}, u32[]{:S(2)}, u32[]{:S(2)}) collective-permute-start(bf16[3,64,1024]{2,1,0:T(8,128)(2,1)S(1)} %get-tuple-element.281), channel_id=1, source_target_pairs={{8,0},{10,2},{16,8},{18,10},{24,16},{26,18},{28,24},{30,26},{20,28... | collective-permute-start | bytes 1179656 | tf_op jit(solution)/shard_map/ppermute | solution.py:54
  760.5 13.6 %collective-permute-start.64 = (f32[256]{0:T(256)S(1)}, f32[256]{0:T(256)S(1)}, u32[]{:S(2)}, u32[]{:S(2)}) collective-permute-start(f32[256]{0:T(256)S(1)} %broadcast_select_fusion.5), channel_id=1, source_target_pairs={{0,4},{2,6},{4,0},{6,2},{8,12},{10,14},{12,8},{14,10},{16,20},{18,... | collective-permute-start | bytes 3080 | tf_op jit(solution)/shard_map/ppermute | solution.py:294
  772.1 10.7 %collective-permute-start.74 = (bf16[1,64,1024]{2,1,0:T(8,128)(2,1)S(1)}, bf16[1,64,1024]{2,1,0:T(8,128)(2,1)S(1)}, u32[]{:S(2)}, u32[]{:S(2)}) collective-permute-start(bf16[1,64,1024]{2,1,0:T(8,128)(2,1)S(1)} %get-tuple-element.388), channel_id=1, source_target_pairs={{0,8},{2,10},{8,16},{10,18},{16,24},{18,26},{24,28},{26,30},{28,20... | collective-permute-start | bytes 393224 | tf_op jit(solution)/shard_map/ppermute | solution.py:54
  782.7 13.0 %collective-permute-start.65 = (f32[128]{0:T(128)S(1)}, f32[128]{0:T(128)S(1)}, u32[]{:S(2)}, u32[]{:S(2)}) collective-permute-start(f32[128]{0:T(128)S(1)} %broadcast_select_fusion.8), channel_id=1, source_target_pairs={{0,2},{2,0},{4,6},{6,4},{8,10},{10,8},{12,14},{14,12},{16,18},{18,... | collective-permute-start | bytes 1544 | tf_op jit(solution)/shard_map/ppermute | solution.py:294
  783.8 12.3 %collective-permute-start.75 = (bf16[1,64,1024]{2,1,0:T(8,128)(2,1)S(1)}, bf16[1,64,1024]{2,1,0:T(8,128)(2,1)S(1)}, u32[]{:S(2)}, u32[]{:S(2)}) collective-permute-start(bf16[1,64,1024]{2,1,0:T(8,128)(2,1)S(1)} %get-tuple-element.386), channel_id=1, source_target_pairs={{0,8},{2,10},{8,16},{10,18},{16,24},{18,26},{24,28},{26,30},{28,20... | collective-permute-start | bytes 393224 | tf_op jit(solution)/shard_map/ppermute | solution.py:54
  785.8 10.3 %collective-permute-start.77 = (bf16[1,64,1024]{2,1,0:T(8,128)(2,1)S(1)}, bf16[1,64,1024]{2,1,0:T(8,128)(2,1)S(1)}, u32[]{:S(2)}, u32[]{:S(2)}) collective-permute-start(bf16[1,64,1024]{2,1,0:T(8,128)(2,1)S(1)} %get-tuple-element.387), channel_id=1, source_target_pairs={{8,0},{10,2},{16,8},{18,10},{24,16},{26,18},{28,24},{30,26},{20,28... | collective-permute-start | bytes 393224 | tf_op jit(solution)/shard_map/ppermute | solution.py:54
  (51 other events, 618.3 us)
Sparse Core Ops, SparseCore 0:
  13.9 129.1 all-gather.4
  145.2 177.9 all-gather.2

commit v5 on v4

--- a/solution.py
+++ b/solution.py
@@ -2,6 +2,7 @@
 import jax.numpy as jnp
 from jax import lax
 from jax.experimental import pallas as pl
+from jax.experimental.layout import Layout, with_layout_constraint
 from jax.experimental.pallas import tpu as pltpu
 from jax.sharding import PartitionSpec as P
 
@@ -66,17 +67,41 @@
         return jnp.concatenate(self.sums, axis=1)
 
 
-def beside(rings, work, *given):
+def beside(rings, extra, work, *given):
     rings = [ring for ring in rings if ring.open()]
-    sums, given = lax.optimization_barrier(([ring.sums for ring in rings], given))
+    sums, blocks, given = lax.optimization_barrier(
+        ([ring.sums for ring in rings], [block for block, axis, route in extra], given)
+    )
     for ring, held in zip(rings, sums):
         ring.sums = held
     arrived = [ring.send() for ring in rings]
+    others = [
+        lax.ppermute(block, axis, route) for block, (held, axis, route) in zip(blocks, extra)
+    ]
     made = work(*given)
-    arrived, made = lax.optimization_barrier((arrived, made))
-    for ring, blocks in zip(rings, arrived):
-        ring.take(blocks)
-    return made
+    arrived, others, made = lax.optimization_barrier((arrived, others, made))
+    for ring, sums in zip(rings, arrived):
+        ring.take(sums)
+    return made, others
+
+
+def row_major(block):
+    return with_layout_constraint(block, Layout(major_to_minor=tuple(range(block.ndim))))
+
+
+def to_partner(block):
+    size = lax.axis_size("seq")
+    return (row_major(block), "seq", [(i, i ^ 1) for i in range(size)])
+
+
+def tp_rows(block, first, last):
+    tokens = block.shape[0]
+    part = block[first * tokens // 4 : last * tokens // 4]
+    return (part, "tp", [(0, 1), (1, 0)])
+
+
+def tp_join(block, parts):
+    return block.astype(jnp.float32) + jnp.concatenate(parts).astype(jnp.float32)
 
 
 def partner(block):
@@ -171,14 +196,14 @@
     return exponent / jnp.sum(exponent, axis=-1, keepdims=True)
 
 
-def attend_kernel(starts_ref, proj_ref, before_ref, mixed_ref):
-    count = proj_ref.shape[1] // SPAN
-    keys = jnp.concatenate([before_ref[0], proj_ref[1]], axis=0)
-    values = jnp.concatenate([before_ref[1], proj_ref[2]], axis=0)
+def attend_kernel(starts_ref, queries_ref, keys_ref, values_ref, before_ref, mixed_ref):
+    count = queries_ref.shape[0] // SPAN
+    keys = jnp.concatenate([before_ref[0], keys_ref[...]], axis=0)
+    values = jnp.concatenate([before_ref[1], values_ref[...]], axis=0)
     for block in range(count):
         rows = slice(block * SPAN, (block + 1) * SPAN)
         seen = slice(block * SPAN, (block + 1) * SPAN + WINDOW)
-        probs = block_scores(proj_ref[0, rows], keys[seen], starts_ref, block)
+        probs = block_scores(queries_ref[rows, :], keys[seen], starts_ref, block)
         mixed = jnp.dot(
             probs.astype(jnp.bfloat16), values[seen], preferred_element_type=jnp.float32
         )
@@ -186,14 +211,26 @@
 
 
 def attend_back_kernel(
-    starts_ref, proj_ref, before_ref, grad_ref, out_ref, rim_ref, tail_ref, keys_ref, values_ref
+    starts_ref,
+    queries_ref,
+    keys_ref,
+    values_ref,
+    before_ref,
+    grad_ref,
+    grad_queries_ref,
+    grad_keys_ref,
+    grad_values_ref,
+    rim_ref,
+    tail_ref,
+    key_sum_ref,
+    value_sum_ref,
 ):
-    count = proj_ref.shape[1] // SPAN
+    count = queries_ref.shape[0] // SPAN
     scale = HEAD_DIM ** (-0.5)
-    keys = jnp.concatenate([before_ref[0], proj_ref[1]], axis=0)
-    values = jnp.concatenate([before_ref[1], proj_ref[2]], axis=0)
-    keys_ref[...] = jnp.zeros_like(keys_ref)
-    values_ref[...] = jnp.zeros_like(values_ref)
+    keys = jnp.concatenate([before_ref[0], keys_ref[...]], axis=0)
+    values = jnp.concatenate([before_ref[1], values_ref[...]], axis=0)
+    key_sum_ref[...] = jnp.zeros_like(key_sum_ref)
+    value_sum_ref[...] = jnp.zeros_like(value_sum_ref)
 
     def crossed(left, right):
         return lax.dot_general(
@@ -203,7 +240,7 @@
     for block in range(count):
         rows = slice(block * SPAN, (block + 1) * SPAN)
         seen = slice(block * SPAN, (block + 1) * SPAN + WINDOW)
-        queries = proj_ref[0, rows]
+        queries = queries_ref[rows, :]
         grads = grad_ref[rows, :]
         probs = block_scores(queries, keys[seen], starts_ref, block)
         grad_probs = lax.dot_general(
@@ -212,54 +249,59 @@
         inner = jnp.sum(probs * grad_probs, axis=-1, keepdims=True)
         grad_scores = (probs * (grad_probs - inner)).astype(jnp.bfloat16)
         grad_queries = jnp.dot(grad_scores, keys[seen], preferred_element_type=jnp.float32)
-        out_ref[0, rows] = (grad_queries * scale).astype(jnp.bfloat16)
-        keys_ref[seen, :] += crossed(grad_scores, queries) * scale
-        values_ref[seen, :] += crossed(probs.astype(jnp.bfloat16), grads)
+        grad_queries_ref[rows, :] = (grad_queries * scale).astype(jnp.bfloat16)
+        key_sum_ref[seen, :] += crossed(grad_scores, queries) * scale
+        value_sum_ref[seen, :] += crossed(probs.astype(jnp.bfloat16), grads)
     tokens = count * SPAN
-    for plane, total_ref in enumerate((keys_ref, values_ref)):
+    totals = ((key_sum_ref, grad_keys_ref), (value_sum_ref, grad_values_ref))
+    for plane, (total_ref, out_ref) in enumerate(totals):
         rim_ref[plane] = total_ref[:WINDOW, :].astype(jnp.bfloat16)
-        out_ref[1 + plane] = total_ref[WINDOW:, :].astype(jnp.bfloat16)
+        out_ref[...] = total_ref[WINDOW:, :].astype(jnp.bfloat16)
         tail_ref[plane] = total_ref[tokens:, :]
 
 
+def head_specs(tokens, heads):
+    starts_spec = pl.BlockSpec((tokens, 1), lambda h: (0, 0))
+    part_specs = [
+        pl.BlockSpec((tokens, HEAD_DIM), lambda h, part=part: (0, part * heads + h))
+        for part in range(3)
+    ]
+    rim_spec = pl.BlockSpec((2, WINDOW, HEAD_DIM), lambda h: (0, 0, h))
+    return starts_spec, part_specs, rim_spec
+
+
 def attend(starts, proj, before):
-    planes, tokens, width = proj.shape
+    tokens, width = proj.shape[0], proj.shape[1] // 3
+    heads = width // HEAD_DIM
+    starts_spec, part_specs, rim_spec = head_specs(tokens, heads)
     return pl.pallas_call(
         attend_kernel,
-        grid=(width // HEAD_DIM,),
-        in_specs=[
-            pl.BlockSpec((tokens, 1), lambda h: (0, 0)),
-            pl.BlockSpec((planes, tokens, HEAD_DIM), lambda h: (0, 0, h)),
-            pl.BlockSpec((2, WINDOW, HEAD_DIM), lambda h: (0, 0, h)),
-        ],
-        out_specs=pl.BlockSpec((tokens, HEAD_DIM), lambda h: (0, h)),
+        grid=(heads,),
+        in_specs=[starts_spec, *part_specs, rim_spec],
+        out_specs=part_specs[0],
         out_shape=jax.ShapeDtypeStruct((tokens, width), jnp.bfloat16),
         name="attend",
-    )(starts, proj, before)
+    )(starts, proj, proj, proj, before)
 
 
 def attend_back(starts, proj, before, grad_mixed):
-    planes, tokens, width = proj.shape
-    rim_spec = pl.BlockSpec((2, WINDOW, HEAD_DIM), lambda h: (0, 0, h))
-    proj_spec = pl.BlockSpec((planes, tokens, HEAD_DIM), lambda h: (0, 0, h))
+    tokens, width = grad_mixed.shape
+    heads = width // HEAD_DIM
+    starts_spec, part_specs, rim_spec = head_specs(tokens, heads)
+    whole = jax.ShapeDtypeStruct((tokens, width), jnp.bfloat16)
     return pl.pallas_call(
         attend_back_kernel,
-        grid=(width // HEAD_DIM,),
-        in_specs=[
-            pl.BlockSpec((tokens, 1), lambda h: (0, 0)),
-            proj_spec,
-            rim_spec,
-            pl.BlockSpec((tokens, HEAD_DIM), lambda h: (0, h)),
-        ],
-        out_specs=[proj_spec, rim_spec, rim_spec],
-        out_shape=[
-            jax.ShapeDtypeStruct(proj.shape, jnp.bfloat16),
+        grid=(heads,),
+        in_specs=[starts_spec, *part_specs, rim_spec, part_specs[0]],
+        out_specs=[part_specs[0]] * 3 + [rim_spec] * 2,
+        out_shape=[whole] * 3
+        + [
             jax.ShapeDtypeStruct((2, WINDOW, width), jnp.bfloat16),
             jax.ShapeDtypeStruct((2, WINDOW, width), jnp.float32),
         ],
         scratch_shapes=[pltpu.VMEM((tokens + WINDOW, HEAD_DIM), jnp.float32)] * 2,
         name="attend_back",
-    )(starts, proj, before, grad_mixed)
+    )(starts, proj, proj, proj, before, grad_mixed)
 
 
 def tp_send(sent):
@@ -328,64 +370,76 @@
     f32 = jnp.float32
     bf16 = jnp.bfloat16
 
-    first_own = jnp.concatenate([w_qkv, w_out.T[:, None]], axis=1)
-    second_own = jnp.concatenate([w_gate_up, w_down.T[:, None]], axis=1)
+    local_width = w_qkv.shape[2]
+    qkv_width = 3 * local_width
+    rest_width = qkv_width + local_width
+    first_own = jnp.concatenate(
+        [w_qkv.reshape(-1, qkv_width), w_out.T, w_down.T], axis=1
+    )
     gains = jnp.stack([gain_one, gain_two])
-    first_own, second_own, gains = lax.optimization_barrier((first_own, second_own, gains))
+    first_own, second_own, gains = lax.optimization_barrier((first_own, w_gate_up, gains))
     first_weights = lax.all_gather(first_own, "seq", axis=0, tiled=True)
-    second_weights = lax.all_gather(second_own, "seq", axis=0, tiled=True)
+    gate_up_full = lax.all_gather(second_own, "seq", axis=0, tiled=True)
     gains = gather_small(gains).astype(f32)
     gain_a = gains[0]
     gain_b = gains[1]
-    qkv_full = first_weights[:, :3]
-    out_full = first_weights[:, 3]
-    gate_up_full = second_weights[:, :2]
-    down_full = second_weights[:, 2]
+    qkv_full = first_weights[:, :qkv_width]
+    out_full = first_weights[:, qkv_width:rest_width]
+    down_full = first_weights[:, rest_width:]
 
     token_rows = tokens.astype(f32)
     normed = rms_scale(token_rows, gain_a).astype(bf16)
-    proj = jnp.einsum("td,dcf->ctf", normed, qkv_full, preferred_element_type=f32).astype(bf16)
-    before = shifted(proj[1:, token_count - WINDOW :], "seq", 1)
+    cot_pair = pair_columns(cotangent, chips, core)
+    normed_pair = pair_columns(normed, chips, core)
+    proj = jnp.dot(normed, qkv_full, preferred_element_type=f32).astype(bf16)
+    last = proj[token_count - WINDOW :]
+    last = jnp.stack([last[:, local_width : 2 * local_width], last[:, 2 * local_width :]])
+    before = shifted(last, "seq", 1)
     attn_mixed = attend(starts, proj, before)
     attn_out = tp_sum(jnp.einsum("tf,df->td", attn_mixed, out_full, preferred_element_type=f32))
     middle = token_rows + attn_out
     normed_two = rms_scale(middle, gain_b).astype(bf16)
+    normed_two_pair = pair_columns(normed_two, chips, core)
+    mixed_two = partner(attn_mixed[None])
+    grad_hidden = jnp.einsum("td,df->tf", cotangent, down_full, preferred_element_type=f32)
+    early = (cot_pair, normed_pair, normed_two_pair, mixed_two, grad_hidden, normed_two)
+    early, gate_up_full = lax.optimization_barrier((early, gate_up_full))
+    cot_pair, normed_pair, normed_two_pair, mixed_two, grad_hidden, normed_two = early
+
     gate_up = jnp.einsum("td,dcf->ctf", normed_two, gate_up_full, preferred_element_type=f32)
     hidden = gated(gate_up[0], gate_up[1]).astype(bf16)
-    cot_pair = pair_columns(cotangent, chips, core)
-    normed_two_pair = pair_columns(normed_two, chips, core)
-    normed_pair = pair_columns(normed, chips, core)
-    hidden, cot_held = lax.optimization_barrier((hidden, cotangent))
-    hidden_two = partner(hidden[None])
-    grad_hidden = jnp.einsum("td,df->tf", cot_held, down_full, preferred_element_type=f32)
-    down_terms = pair_terms(cot_pair, hidden[None], hidden_two, chips)
-    down = Ring(down_terms, chips, place)
-
-    def through_gate(grad_hidden, gate_up):
-        unused_value, gate_pull = jax.vjp(gated, gate_up[0], gate_up[1])
-        return jnp.stack(gate_pull(grad_hidden)).astype(bf16)
-
-    grad_gate_up = beside([down], through_gate, grad_hidden, gate_up)
-    grad_gate_up_two = partner(grad_gate_up)
+    unused_value, gate_pull = jax.vjp(gated, gate_up[0], gate_up[1])
+    grad_gate_up = jnp.stack(gate_pull(grad_hidden)).astype(bf16)
 
     def through_gate_up(grad_gate_up):
         return jnp.einsum(
             "ctf,dcf->td", grad_gate_up, gate_up_full, preferred_element_type=f32
         ).astype(bf16)
 
-    sent_two = beside([down], through_gate_up, grad_gate_up)
-    grad_normed_two = tp_send(sent_two)
+    swaps = [to_partner(hidden[None]), to_partner(grad_gate_up)]
+    sent_two, (hidden_two, grad_gate_up_two) = beside([], swaps, through_gate_up, grad_gate_up)
+
+    def down_product(hidden):
+        return pair_terms(cot_pair, row_major(hidden[None]), row_major(hidden_two), chips)
+
+    down_terms, (part_a,) = beside([], [tp_rows(sent_two, 0, 1)], down_product, hidden)
+    down = Ring(down_terms, chips, place)
 
     def gate_up_product(grad_gate_up):
-        return pair_terms(normed_two_pair, grad_gate_up, grad_gate_up_two, chips)
-
-    gate_up_ring = Ring(beside([down], gate_up_product, grad_gate_up), chips, place)
+        right = row_major(grad_gate_up), row_major(grad_gate_up_two)
+        return pair_terms(normed_two_pair, *right, chips)
+
+    gate_up_terms, (part_b,) = beside(
+        [down], [tp_rows(sent_two, 1, 3)], gate_up_product, grad_gate_up
+    )
+    gate_up_ring = Ring(gate_up_terms, chips, place)
+    rings = [down, gate_up_ring]
 
     def through_down(hidden):
         return jnp.einsum("tf,df->td", hidden, down_full, preferred_element_type=f32).astype(bf16)
 
-    rings = [down, gate_up_ring]
-    branch = tp_send(beside(rings, through_down, hidden))
+    sent_branch, (part_c,) = beside(rings, [tp_rows(sent_two, 3, 4)], through_down, hidden)
+    grad_normed_two = tp_join(sent_two, [part_a, part_b, part_c])
 
     def through_norm_two(middle):
         unused_norm, norm_pull = jax.vjp(rms_scale, middle, gain_b)
@@ -395,57 +449,71 @@
         grad_mixed = jnp.einsum("td,df->tf", grad_attn, out_full, preferred_element_type=f32)
         return grad_middle, grad_gain_two, grad_attn, grad_mixed.astype(bf16)
 
-    grad_middle, grad_gain_two, grad_attn, grad_mixed = beside(rings, through_norm_two, middle)
+    made, (branch_a,) = beside(rings, [tp_rows(sent_branch, 0, 2)], through_norm_two, middle)
+    grad_middle, grad_gain_two, grad_attn, grad_mixed = made
     grad_gain_two = scatter_small(grad_gain_two)
-    mixed_two = partner(attn_mixed[None])
-    grad_attn_pair = pair_columns(grad_attn, chips, core)
-
-    def through_attention(grad_mixed):
-        return attend_back(starts, proj, before, grad_mixed)
-
-    grad_proj, rim, tail = beside(rings, through_attention, grad_mixed)
-    arrived = shifted(rim, "seq", -1).astype(f32)
-
-    def out_product(grad_proj):
-        out_terms = pair_terms(grad_attn_pair, attn_mixed[None], mixed_two, chips)
-        edge = (tail + arrived).astype(bf16)
-        return out_terms, grad_proj.at[1:, token_count - WINDOW :].set(edge)
-
-    out_terms, grad_proj = beside(rings, out_product, grad_proj)
+
+    def through_attention(grad_mixed, grad_attn):
+        grad_attn_pair = pair_columns(grad_attn, chips, core)
+        return grad_attn_pair, attend_back(starts, proj, before, grad_mixed)
+
+    made, (branch_b,) = beside(
+        rings, [tp_rows(sent_branch, 2, 4)], through_attention, grad_mixed, grad_attn
+    )
+    grad_attn_pair, (grad_queries, grad_keys, grad_values, rim, tail) = made
+    branch = tp_join(sent_branch, [branch_a, branch_b])
+    size = 2 * chips
+    back_route = [(i + 1, i) for i in range(size - 1)]
+
+    def out_product(attn_mixed):
+        return pair_terms(grad_attn_pair, attn_mixed[None], mixed_two, chips)
+
+    out_terms, (arrived,) = beside(rings, [(rim, "seq", back_route)], out_product, attn_mixed)
     rings.append(Ring(out_terms, chips, place))
-    grad_proj_two = partner(grad_proj)
-
-    def through_qkv(grad_proj):
-        return jnp.einsum(
-            "ctf,dcf->td", grad_proj, qkv_full, preferred_element_type=f32
-        ).astype(bf16)
-
-    grad_normed = tp_send(beside(rings, through_qkv, grad_proj))
+
+    def through_qkv(grad_queries):
+        edge = (tail + arrived.astype(f32)).astype(bf16)
+        inner = token_count - WINDOW
+        whole_keys = jnp.concatenate([grad_keys[:inner], edge[0]])
+        whole_values = jnp.concatenate([grad_values[:inner], edge[1]])
+        grad_proj = jnp.concatenate([grad_queries, whole_keys, whole_values], axis=1)
+        sent = jnp.einsum("tf,df->td", grad_proj, qkv_full, preferred_element_type=f32)
+        return grad_proj, sent.astype(bf16)
+
+    (grad_proj, sent_one), unused_none = beside(rings, [], through_qkv, grad_queries)
+
+    def finish(middle):
+        return (middle + branch).astype(bf16)
+
+    result, (grad_proj_two, part_a) = beside(
+        rings, [to_partner(grad_proj[None]), tp_rows(sent_one, 0, 2)], finish, middle
+    )
 
     def qkv_product(grad_proj):
-        return pair_terms(normed_pair, grad_proj, grad_proj_two, chips)
-
-    rings.append(Ring(beside(rings, qkv_product, grad_proj), chips, place))
-
-    def finish(middle):
-        return (middle + branch).astype(bf16), down.result()[0].T
-
-    result, grad_w_down = beside(rings, finish, middle)
-
-    def finish_gate_up(whole):
-        return whole.transpose(1, 0, 2)
-
-    grad_w_gate_up = beside(rings, finish_gate_up, gate_up_ring.result())
+        return pair_terms(normed_pair, grad_proj[None], grad_proj_two, chips)
+
+    qkv_terms, (part_b,) = beside(rings, [tp_rows(sent_one, 2, 4)], qkv_product, grad_proj)
+    rings.append(Ring(qkv_terms, chips, place))
+    grad_normed = tp_join(sent_one, [part_a, part_b])
 
     def through_norm(token_rows):
         unused_first, first_pull = jax.vjp(rms_scale, token_rows, gain_a)
         grad_rows_norm, grad_gain_one = first_pull(grad_normed)
         return grad_middle + grad_rows_norm, grad_gain_one
 
-    grad_tokens, grad_gain_one = beside(rings, through_norm, token_rows)
+    (grad_tokens, grad_gain_one), unused_none = beside(rings, [], through_norm, token_rows)
     grad_gain_one = scatter_small(grad_gain_one)
+
+    def finish_down(whole):
+        return whole[0].T
+
+    def finish_gate_up(whole):
+        return whole.transpose(1, 0, 2)
+
+    grad_w_down, unused_none = beside(rings, [], finish_down, down.result())
+    grad_w_gate_up, unused_none = beside(rings, [], finish_gate_up, gate_up_ring.result())
     grad_w_out = rings[2].result()[0].T
-    grad_w_qkv = rings[3].result().transpose(1, 0, 2)
+    grad_w_qkv = rings[3].result().reshape(-1, 3, local_width)
     return (
         result,
         grad_tokens,

time: 818 us -> 774 us (0.946)
  waiting for transfers between devices: 357 us -> 305 us
  other arithmetic: 95.1 us -> 105 us
    all_gather x1, waiting for transfers between devices: 102 us -> 18.4 us  [local(): gate_up_full = lax.all_gather(second_own, 'seq', axis=0, tiled=True)]
    ppermute x4 -> x1, waiting for transfers between devices: 72.8 us -> 22.6 us  [tp_send(): lax.ppermute(sent, 'tp', [(0, 1), (1, 0)]).astype(jnp.float32)]
    ppermute x56, waiting for transfers between devices: 64.9 us -> 114 us  [send(): return [lax.ppermute(self.sums[d], 'seq', self.routes[d]) for d in range(2)]]
    all_gather x1, waiting for transfers between devices: 112 us -> 135 us  [local(): first_weights = lax.all_gather(first_own, 'seq', axis=0, tiled=True)]
    ppermute x56, starting transfers between devices: 79.6 us -> 60.5 us  [send(): return [lax.ppermute(self.sums[d], 'seq', self.routes[d]) for d in range(2)]]
    ppermute x8 -> x5, starting transfers between devices: 1.3 us -> 17 us  [partner(): return lax.ppermute(block, 'seq', [(i, i ^ 1) for i in range(size)])]
    ppermute x2 -> x0, local copies, waits for them, and re-layouts: 12.8 us -> none  [partner(): return lax.ppermute(block, 'seq', [(i, i ^ 1) for i in range(size)])]
    optimization_barrier x2 -> x4, local copies, waits for them, and re-layouts: 14.5 us -> 23.7 us  [the longest x2 12.8 us: beside(): arrived, others, made = lax.optimization_barrier((arrived, others, made))]
  transfers between devices with their start and end apart: 84 -> 88, of which waited for: 28 -> 32; matrix products, arithmetic and copies ran while one was open for 23% -> 19% of each run, Pallas kernels for 11% -> 12%
where the time goes in v5:
time: 774 us; the launch traced here: 768 us
  waiting for transfers between devices  305 us (39%)
  starting transfers between devices  105 us (14%)
  other arithmetic  105 us (14%)
  Pallas kernels  95.4 us (12%)
  matrix products  90.8 us (12%)
  local copies, waits for them, and re-layouts  50.2 us (6%)
  between operations  15.1 us (2%)
    all_gather x1, waiting for transfers between devices, local(): first_weights = lax.all_gather(first_own, 'seq', axis=0, tiled=True)  135 us
    ppermute x56, waiting for transfers between devices, send(): return [lax.ppermute(self.sums[d], 'seq', self.routes[d]) for d in range(2)]  114 us
    ppermute x56, starting transfers between devices, send(): return [lax.ppermute(self.sums[d], 'seq', self.routes[d]) for d in range(2)]  60.5 us
    pallas_call x4, Pallas kernels, pair_terms(): pl.pallas_call(pair_kernel, grid=(planes, chips // group), in_specs=[left...  48.6 us
    convert_element_type x24, other arithmetic, take(): total.astype(jnp.bfloat16)  36.7 us
    ppermute x1, waiting for transfers between devices, tp_send(): lax.ppermute(sent, 'tp', [(0, 1), (1, 0)]).astype(jnp.float32)  22.6 us
    all_gather x1, waiting for transfers between devices, local(): gate_up_full = lax.all_gather(second_own, 'seq', axis=0, tiled=True)  18.4 us
    dot_general x1, matrix products, through_gate_up(): jnp.einsum('ctf,dcf->td', grad_gate_up, gate_up_full, preferred_element_t...  18.3 us
  transfers between devices with their start and end apart: 88, of which 32 were waited for; matrix products, arithmetic and copies ran while one was open for 19% of the time, Pallas kernels for 12%

profile of v5, /device:TPU:0, one launch (start us, length us, event | category | flops | bytes accessed | tf_op | source)
XLA Modules:
  0.0 767.5 jit_solution(2467684725722980663)
XLA Ops:
  9.6 2.5 pad_maximum_fusion.4
  14.2 2.8 collective-permute-start.2
  22.3 3.1 collective-permute-start.4
  29.7 134.8 %all-gather.3.cloned.1.call-done = bf16[2048,6848]{0,1:T(8,128)(2,1)} async-done(((bf16[128,6848]{0,1:T(8,128)(2,1)}), bf16[2048,6848]{0,1:T(8,128)(2,1)}) %all-gather.3.cloned.1.call-update) | async-done | bytes 28049424 | tf_op jit(solution)/shard_map/all_gather | solution.py:381
  164.5 10.3 %fusion.18.queries_ref.keys_ref.values_ref = bf16[512,3072]{1,0:T(8,128)(2,1)S(1)} fusion(bf16[512,2048]{1,0:T(8,128)(2,1)} %multiply_convert_fusion.3.block_ref, bf16[2048,6848]{0,1:T(8,128)(2,1)} %all-gather.3.cloned.1.call-done), kind=kOutput, calls=%fused_computation.27 | convolution fusion | flops 6444023808 | bytes 17825792 | tf_op jit(solution)/shard_map/dot_general | solution.py:394
  175.7 2.7 collective-permute-start.6
  180.0 12.7 %attend.1 = bf16[512,1024]{1,0:T(8,128)(2,1)} custom-call(s32[512,1]{1,0:T(8,128)} %copy.57.starts_ref, bf16[512,3072]{1,0:T(8,128)(2,1)} %copy-done.2, bf16[512,3072]{1,0:T(8,128)(2,1)} %copy-done.2, bf16[512,3072]{1,0:T(8,128)(2,1)} %copy-done.2, bf16[2,64,1024]{2,1,0:T(8,128)(2,1)} %copy-done.17), custom_call_target="tpu_custom_call" | custom-call | tf_op jit(solution)/shard_map/attend/pallas_call | solution.py:277
  192.7 6.3 fusion.35
  200.4 4.0 select_columns.4
  204.5 8.5 %collective-permute-start = (bf16[512,1024]{1,0:T(8,128)(2,1)}, bf16[512,1024]{1,0:T(8,128)(2,1)}, u32[]{:S(2)}, u32[]{:S(2)}) collective-permute-start(bf16[512,1024]{1,0:T(8,128)(2,1)} %get-tuple-element.187), channel_id=1, source_target_pairs={{0,2},{2,0},{4,6},{6,4},{8,10},{10,8},{12,14},{14,12},{16,18},{18,... | collective-permute-start | bytes 3145736 | tf_op jit(solution)/shard_map/ppermute | solution.py:109
  212.9 4.0 select_columns.5
  217.5 22.6 %collective-permute-done.7 = bf16[512,2048]{1,0:T(8,128)(2,1)} collective-permute-done((bf16[512,2048]{1,0:T(8,128)(2,1)}, bf16[512,2048]{1,0:T(8,128)(2,1)}, u32[]{:S(2)}, u32[]{:S(2)}) %collective-permute-start.7) | collective-permute-done | bytes 2097184 | tf_op jit(solution)/shard_map/ppermute | solution.py:308
  240.1 3.2 multiply_reduce_fusion.6
  247.1 4.0 select_columns.6
  251.1 8.0 %collective-permute-start.8 = (bf16[512,1024]{1,0:T(8,128)(2,1)}, bf16[512,1024]{1,0:T(8,128)(2,1)}, u32[]{:S(2)}, u32[]{:S(2)}) collective-permute-start(bf16[512,1024]{1,0:T(8,128)(2,1)} %get-tuple-element.193), channel_id=1, source_target_pairs={{0,2},{2,0},{4,6},{6,4},{8,10},{10,8},{12,14},{14,12},{16,18},{18,... | collective-permute-start | bytes 3145736 | tf_op jit(solution)/shard_map/ppermute | solution.py:109
  259.1 12.4 %fusion.15 = f32[512,2752]{1,0:T(8,128)} fusion(bf16[512,2048]{1,0:T(8,128)(2,1)S(1)} %copy-done.10, bf16[2048,6848]{0,1:T(8,128)(2,1)} %all-gather.3.cloned.1.call-done), kind=kOutput, calls=%fused_computation.26 | convolution fusion | flops 5771362304 | bytes 19005440 | tf_op jit(solution)/shard_map/td,df->tf/dot_general | solution.py:404
  271.5 18.4 %all-gather.5.cloned.1.call-done = bf16[2048,2,2752]{0,2,1:T(8,128)(2,1)} async-done(((bf16[128,2,2752]{0,2,1:T(8,128)(2,1)}), bf16[2048,2,2752]{0,2,1:T(8,128)(2,1)}) %all-gather.5.cloned.1.call-update) | async-done | bytes 22544400 | tf_op jit(solution)/shard_map/all_gather | solution.py:382
  289.9 17.3 %convolution_bitcast_fusion = f32[2,512,2752]{2,1,0:T(8,128)S(1)} fusion(bf16[2048,2,2752]{0,2,1:T(8,128)(2,1)} %all-gather.5.cloned.1.call-done, bf16[512,2048]{1,0:T(8,128)(2,1)} %multiply_convert_fusion.2.block_ref), kind=kOutput, calls=%fused_computation.8 | convolution fusion | flops 11542724608 | bytes 35913728 | tf_op jit(solution)/shard_map/td,dcf->ctf/dot_general | solution.py:409
  309.0 7.1 fusion.39
  316.2 2.9 pad_maximum_fusion.right_ref
  319.1 8.3 %copy.61 = bf16[2,512,2752]{1,2,0:T(8,128)(2,1)} copy(bf16[2,512,2752]{2,1,0:T(8,128)(2,1)} %pad_maximum_fusion.right_ref) | data formatting | bytes 11272192 | tf_op jit(solution)/shard_map/optimization_barrier | solution.py:72
  327.6 2.7 copy.60
  330.6 18.3 %bitcast_convert_fusion = bf16[512,2048]{1,0:T(8,128)(2,1)S(1)} fusion(bf16[2,512,2752]{2,1,0:T(8,128)(2,1)} %pad_maximum_fusion.right_ref, bf16[2048,2,2752]{0,2,1:T(8,128)(2,1)} %all-gather.5.cloned.1.call-done), kind=kOutput, calls=%fused_computation.30 | convolution fusion | flops 11543773184 | bytes 30277632 | tf_op jit(solution)/shard_map/ctf,dcf->td/dot_general | solution.py:415
  350.8 4.5 copy.63.right_two_ref
  356.8 8.3 %copy.64.right_two_ref = bf16[2,512,2752]{2,1,0:T(8,128)(2,1)} copy(bf16[2,512,2752]{1,2,0:T(8,128)(2,1)} %collective-permute-done.11) | data formatting | bytes 11272192 | tf_op jit(solution)/shard_map/optimization_barrier | solution.py:82
  365.1 10.8 %pair_terms.4 = bf16[8,2,1,64,2752]{4,3,2,1,0:T(8,128)(2,1)} custom-call(bf16[512,1024]{1,0:T(8,128)(2,1)} %get-tuple-element.203.left_ref, bf16[512,1024]{1,0:T(8,128)(2,1)} %collective-permute-done.left_two_ref, bf16[1,512,2752]{2,1,0:T(8,128)(2,1)} %bitcast.279, bf16[1,512,2752]{2,1,0:T(8,128)(2,1)} %copy.63.right_two_ref), custom_call_target="tpu_custom_call" | custom-call | flops 5771362304 | bytes 11272192 | tf_op jit(solution)/shard_map/pair_terms/pallas_call | solution.py:162
  380.7 19.9 %pair_terms.5 = bf16[8,2,2,64,2752]{4,3,2,1,0:T(8,128)(2,1)} custom-call(bf16[512,1024]{1,0:T(8,128)(2,1)} %get-tuple-element.211.left_ref, bf16[512,1024]{1,0:T(8,128)(2,1)} %collective-permute-done.8.left_two_ref, bf16[2,512,2752]{2,1,0:T(8,128)(2,1)} %pad_maximum_fusion.right_ref, bf16[2,512,2752]{2,1,0:T(8,128)(2,1)} %copy.64.right_two_ref), custom_call_target="tpu_custom_call" | custom-call | flops 11542724608 | bytes 22544384 | tf_op jit(solution)/shard_map/pair_terms/pallas_call | solution.py:162
  400.7 2.7 collective-permute-done.15
  410.9 9.5 %fusion.29 = bf16[512,2048]{1,0:T(8,128)(2,1)S(1)} fusion(bf16[512,2752]{1,0:T(8,128)(2,1)S(1)} %copy-done.14, bf16[2048,6848]{0,1:T(8,128)(2,1)} %all-gather.3.cloned.1.call-done), kind=kOutput, calls=%fused_computation.52 | convolution fusion | flops 5772410880 | bytes 16187392 | tf_op jit(solution)/shard_map/tf,df->td/dot_general | solution.py:439
  420.4 10.7 %collective-permute-done.16 = bf16[1,64,2752]{2,1,0:T(8,128)(2,1)S(1)} collective-permute-done((bf16[1,64,2752]{2,1,0:T(8,128)(2,1)S(1)}, bf16[1,64,2752]{2,1,0:T(8,128)(2,1)S(1)}, u32[]{:S(2)}, u32[]{:S(2)}) %collective-permute-start.16) | collective-permute-done | bytes 352288 | tf_op jit(solution)/shard_map/ppermute | solution.py:55
  436.2 2.8 multiply_reduce_fusion.3
  441.6 5.3 fusion.97
  448.9 5.5 fusion.41.grad_ref
  454.5 8.6 %collective-permute-done.21 = bf16[1,64,2752]{2,1,0:T(8,128)(2,1)S(1)} collective-permute-done((bf16[1,64,2752]{2,1,0:T(8,128)(2,1)S(1)}, bf16[1,64,2752]{2,1,0:T(8,128)(2,1)S(1)}, u32[]{:S(2)}, u32[]{:S(2)}) %collective-permute-start.21) | collective-permute-done | bytes 352288 | tf_op jit(solution)/shard_map/ppermute | solution.py:55
  463.5 2.9 fusion.52
  468.5 4.0 select_columns.7
  476.9 8.3 %collective-permute-done.26 = bf16[1,64,2752]{2,1,0:T(8,128)(2,1)S(1)} collective-permute-done((bf16[1,64,2752]{2,1,0:T(8,128)(2,1)S(1)}, bf16[1,64,2752]{2,1,0:T(8,128)(2,1)S(1)}, u32[]{:S(2)}, u32[]{:S(2)}) %collective-permute-start.26) | collective-permute-done | bytes 352288 | tf_op jit(solution)/shard_map/ppermute | solution.py:55
  486.6 18.0 %attend_back.1 = (bf16[512,1024]{1,0:T(8,128)(2,1)}, bf16[512,1024]{1,0:T(8,128)(2,1)}, bf16[512,1024]{1,0:T(8,128)(2,1)}, bf16[2,64,1024]{2,1,0:T(8,128)(2,1)}, f32[2,64,1024]{2,1,0:T(8,128)}) custom-call(s32[512,1]{1,0:T(8,128)} %copy.57.starts_ref, bf16[512,3072]{1,0:T(8,128)(2,1)} %copy-done.2, bf16[512,3072]{1,0:T(8,128)(2,1)} %copy-done.2, ...), custom_call_target="tpu_custom_call" | custom-call | tf_op jit(solution)/shard_map/attend_back/pallas_call | solution.py:292
  504.7 3.3 fusion.50
  516.9 6.0 pair_terms.6
  523.0 11.5 %collective-permute-done.32 = bf16[1,64,2752]{2,1,0:T(8,128)(2,1)S(1)} collective-permute-done((bf16[1,64,2752]{2,1,0:T(8,128)(2,1)}, bf16[1,64,2752]{2,1,0:T(8,128)(2,1)S(1)}, u32[]{:S(2)}, u32[]{:S(2)}) %collective-permute-start.32) | collective-permute-done | bytes 352288 | tf_op jit(solution)/shard_map/ppermute | solution.py:55
  540.5 2.4 collective-permute-start.39
  547.0 11.2 %fusion.32 = bf16[512,2048]{1,0:T(8,128)(2,1)S(1)} fusion(bf16[2048,6848]{0,1:T(8,128)(2,1)} %all-gather.3.cloned.1.call-done, bf16[64,1024]{1,0:T(8,128)(2,1)S(1)} %get-tuple-element.480, bf16[448,1024]{1,0:T(8,128)(2,1)S(1)} %slice.81, bf16[64,1024]{1,0:T(8,128)(2,1)S(1)} %get-tuple-element.479, bf16[448,1024]{1,0:T(8,128)(2,1)S(1)} %slice.79, ...), kind=kOutput, calls=%fused_computation.53 | convolution fusion | flops 6459228160 | bytes 17825792 | tf_op jit(solution)/shard_map/tf,df->td/dot_general | solution.py:480
  558.3 11.0 %collective-permute-done.41 = bf16[1,64,1024]{2,1,0:T(8,128)(2,1)S(1)} collective-permute-done((bf16[1,64,1024]{2,1,0:T(8,128)(2,1)S(1)}, bf16[1,64,1024]{2,1,0:T(8,128)(2,1)S(1)}, u32[]{:S(2)}, u32[]{:S(2)}) %collective-permute-start.41) | collective-permute-done | bytes 131104 | tf_op jit(solution)/shard_map/ppermute | solution.py:55
  571.2 11.9 %maximum_maximum_fusion = bf16[512,3072]{1,0:T(8,128)(2,1)} fusion(bf16[64,1024]{1,0:T(8,128)(2,1)S(1)} %get-tuple-element.480, bf16[448,1024]{1,0:T(8,128)(2,1)S(1)} %slice.81, bf16[64,1024]{1,0:T(8,128)(2,1)S(1)} %get-tuple-element.479, bf16[448,1024]{1,0:T(8,128)(2,1)S(1)} %slice.79, bf16[512,1024]{1,0:T(8,128)(2,1)S(1)} %copy-done.18), kind=kLoop, calls=%fused_computation.51 | loop fusion | flops 15728640 | bytes 6291456 | tf_op jit(solution)/shard_map/concatenate | solution.py:479
  586.4 2.8 fusion.46
  593.4 2.9 collective-permute-done.82
  596.5 3.5 collective-permute-done.83
  600.9 2.5 convert_element_type.1060
  607.1 8.3 %collective-permute-done.47 = bf16[1,64,1024]{2,1,0:T(8,128)(2,1)S(1)} collective-permute-done((bf16[1,64,1024]{2,1,0:T(8,128)(2,1)}, bf16[1,64,1024]{2,1,0:T(8,128)(2,1)S(1)}, u32[]{:S(2)}, u32[]{:S(2)}) %collective-permute-start.47) | collective-permute-done | bytes 131104 | tf_op jit(solution)/shard_map/ppermute | solution.py:55
  618.6 5.5 add_convert_fusion
  624.1 14.1 %collective-permute-done.44 = bf16[1,64,2752]{2,1,0:T(8,128)(2,1)S(1)} collective-permute-done((bf16[1,64,2752]{2,1,0:T(8,128)(2,1)S(1)}, bf16[1,64,2752]{2,1,0:T(8,128)(2,1)S(1)}, u32[]{:S(2)}, u32[]{:S(2)}) %collective-permute-start.44) | collective-permute-done | bytes 352288 | tf_op jit(solution)/shard_map/ppermute | solution.py:55
  640.0 2.8 fusion.44
  649.4 11.8 %pair_terms.7 = bf16[8,2,1,64,3072]{4,3,2,1,0:T(8,128)(2,1)} custom-call(bf16[512,1024]{1,0:T(8,128)(2,1)} %get-tuple-element.318.left_ref, bf16[512,1024]{1,0:T(8,128)(2,1)} %collective-permute-done.5.left_two_ref, bf16[1,512,3072]{2,1,0:T(8,128)(2,1)} %bitcast.61.right_ref, bf16[1,512,3072]{2,1,0:T(8,128)(2,1)} %collective-permute-done.49.right_two_ref), custom_call_target="tpu_custom_call" | custom-call | flops 6442450944 | bytes 12582912 | tf_op jit(solution)/shard_map/pair_terms/pallas_call | solution.py:162
  666.4 2.5 multiply_reduce_fusion
  673.1 4.5 fusion.22
  679.7 2.5 collective-permute-done.56
  689.3 7.7 %collective-permute-done.64 = bf16[1,64,1024]{2,1,0:T(8,128)(2,1)S(1)} collective-permute-done((bf16[1,64,1024]{2,1,0:T(8,128)(2,1)S(1)}, bf16[1,64,1024]{2,1,0:T(8,128)(2,1)S(1)}, u32[]{:S(2)}, u32[]{:S(2)}) %collective-permute-start.64) | collective-permute-done | bytes 131104 | tf_op jit(solution)/shard_map/ppermute | solution.py:55
  703.6 6.7 collective-permute-done.68
  715.2 6.2 collective-permute-done.72
  724.9 7.7 collective-permute-done.73
  734.7 2.5 collective-permute-start.74
  743.2 2.8 collective-permute-done.78
  749.6 2.9 copy.70
  (297 shorter events, 155.7 us)
Async XLA Ops:
  7.2 157.3 %all-gather.3.cloned.1.call-start = ((), (), s32[]{:S(2)}) async-start(), calls=%async_computation | async-start | bytes 29802496 | tf_op jit(solution)/shard_map/all_gather | solution.py:381
  12.1 277.9 %all-gather.5.cloned.1.call-start = ((), (), s32[]{:S(2)}) async-start(), calls=%async_computation.1 | async-start | bytes 23953408 | tf_op jit(solution)/shard_map/all_gather | solution.py:382
  199.0 41.1 %collective-permute-start.7 = (bf16[512,2048]{1,0:T(8,128)(2,1)}, bf16[512,2048]{1,0:T(8,128)(2,1)}, u32[]{:S(2)}, u32[]{:S(2)}) collective-permute-start(bf16[512,2048]{1,0:T(8,128)(2,1)} %fusion.35), channel_id=1, source_target_pairs={{0,1},{1,0},{2,3},{3,2},{4,5},{5,4},{6,7},{7,6},{8,9},{9,8},{10,11... | collective-permute-start | bytes 6291464 | tf_op jit(solution)/shard_map/ppermute | solution.py:308
  204.5 67.0 %collective-permute-start = (bf16[512,1024]{1,0:T(8,128)(2,1)}, bf16[512,1024]{1,0:T(8,128)(2,1)}, u32[]{:S(2)}, u32[]{:S(2)}) collective-permute-start(bf16[512,1024]{1,0:T(8,128)(2,1)} %get-tuple-element.187), channel_id=1, source_target_pairs={{0,2},{2,0},{4,6},{6,4},{8,10},{10,8},{12,14},{14,12},{16,18},{18,... | collective-permute-start | bytes 3145736 | tf_op jit(solution)/shard_map/ppermute | solution.py:109
  216.9 54.5 %collective-permute-start.5 = (bf16[512,1024]{1,0:T(8,128)(2,1)}, bf16[512,1024]{1,0:T(8,128)(2,1)}, u32[]{:S(2)}, u32[]{:S(2)}) collective-permute-start(bf16[512,1024]{1,0:T(8,128)(2,1)} %get-tuple-element.190), channel_id=1, source_target_pairs={{0,2},{2,0},{4,6},{6,4},{8,10},{10,8},{12,14},{14,12},{16,18},{18,... | collective-permute-start | bytes 3145736 | tf_op jit(solution)/shard_map/ppermute | solution.py:109
  216.9 73.0 %collective-permute-start.9 = (bf16[1,512,1024]{2,1,0:T(8,128)(2,1)S(1)}, bf16[1,512,1024]{2,1,0:T(8,128)(2,1)}, u32[]{:S(2)}, u32[]{:S(2)}) collective-permute-start(bf16[1,512,1024]{2,1,0:T(8,128)(2,1)S(1)} %bitcast.281), channel_id=1, source_target_pairs={{0,2},{2,0},{4,6},{6,4},{8,10},{10,8},{12,14},{14,12},{16,18},{18,... | collective-permute-start | bytes 3145736 | tf_op jit(solution)/shard_map/ppermute | solution.py:109
  251.1 38.9 %collective-permute-start.8 = (bf16[512,1024]{1,0:T(8,128)(2,1)}, bf16[512,1024]{1,0:T(8,128)(2,1)}, u32[]{:S(2)}, u32[]{:S(2)}) collective-permute-start(bf16[512,1024]{1,0:T(8,128)(2,1)} %get-tuple-element.193), channel_id=1, source_target_pairs={{0,2},{2,0},{4,6},{6,4},{8,10},{10,8},{12,14},{14,12},{16,18},{18,... | collective-permute-start | bytes 3145736 | tf_op jit(solution)/shard_map/ppermute | solution.py:109
  327.4 21.5 %collective-permute-start.11 = (bf16[2,512,2752]{1,2,0:T(8,128)(2,1)}, bf16[2,512,2752]{1,2,0:T(8,128)(2,1)}, u32[]{:S(2)}, u32[]{:S(2)}) collective-permute-start(bf16[2,512,2752]{1,2,0:T(8,128)(2,1)} %copy.61), channel_id=1, source_target_pairs={{0,2},{2,0},{4,6},{6,4},{8,10},{10,8},{12,14},{14,12},{16,18},{18,... | collective-permute-start | bytes 16908296 | tf_op jit(solution)/shard_map/ppermute | solution.py:79
  330.3 18.6 %collective-permute-start.10 = (bf16[1,512,2752]{1,2,0:T(8,128)(2,1)}, bf16[1,512,2752]{1,2,0:T(8,128)(2,1)}, u32[]{:S(2)}, u32[]{:S(2)}) collective-permute-start(bf16[1,512,2752]{1,2,0:T(8,128)(2,1)} %copy.60), channel_id=1, source_target_pairs={{0,2},{2,0},{4,6},{6,4},{8,10},{10,8},{12,14},{14,12},{16,18},{18,... | collective-permute-start | bytes 8454152 | tf_op jit(solution)/shard_map/ppermute | solution.py:79
  355.3 20.5 %collective-permute-start.12 = (bf16[128,2048]{1,0:T(8,128)(2,1)S(1)}, bf16[128,2048]{1,0:T(8,128)(2,1)S(1)}, u32[]{:S(2)}, u32[]{:S(2)}) collective-permute-start(bf16[128,2048]{1,0:T(8,128)(2,1)S(1)} %get-tuple-element.202), channel_id=1, source_target_pairs={{0,1},{1,0},{2,3},{3,2},{4,5},{5,4},{6,7},{7,6},{8,9},{9,8},{10,11... | collective-permute-start | bytes 1572872 | tf_op jit(solution)/shard_map/ppermute | solution.py:79
  378.1 25.2 %collective-permute-start.15 = (bf16[256,2048]{1,0:T(8,128)(2,1)}, bf16[256,2048]{1,0:T(8,128)(2,1)S(1)}, u32[]{:S(2)}, u32[]{:S(2)}) collective-permute-start(bf16[256,2048]{1,0:T(8,128)(2,1)} %slice.75), channel_id=1, source_target_pairs={{0,1},{1,0},{2,3},{3,2},{4,5},{5,4},{6,7},{7,6},{8,9},{9,8},{10,11... | collective-permute-start | bytes 3145736 | tf_op jit(solution)/shard_map/ppermute | solution.py:79
  378.7 22.0 %collective-permute-start.13 = (bf16[1,64,2752]{2,1,0:T(8,128)(2,1)}, bf16[1,64,2752]{2,1,0:T(8,128)(2,1)S(1)}, u32[]{:S(2)}, u32[]{:S(2)}) collective-permute-start(bf16[1,64,2752]{2,1,0:T(8,128)(2,1)} %get-tuple-element.208), channel_id=1, source_target_pairs={{0,8},{2,10},{8,16},{10,18},{16,24},{18,26},{24,28},{26,30},{28,20... | collective-permute-start | bytes 1056776 | tf_op jit(solution)/shard_map/ppermute | solution.py:55
  379.2 21.4 %collective-permute-start.14 = (bf16[1,64,2752]{2,1,0:T(8,128)(2,1)}, bf16[1,64,2752]{2,1,0:T(8,128)(2,1)}, u32[]{:S(2)}, u32[]{:S(2)}) collective-permute-start(bf16[1,64,2752]{2,1,0:T(8,128)(2,1)} %get-tuple-element.209), channel_id=1, source_target_pairs={{8,0},{10,2},{16,8},{18,10},{24,16},{26,18},{28,24},{30,26},{20,28... | collective-permute-start | bytes 1056776 | tf_op jit(solution)/shard_map/ppermute | solution.py:55
  406.2 25.2 %collective-permute-start.18 = (bf16[2,64,2752]{2,1,0:T(8,128)(2,1)S(1)}, bf16[2,64,2752]{2,1,0:T(8,128)(2,1)S(1)}, u32[]{:S(2)}, u32[]{:S(2)}) collective-permute-start(bf16[2,64,2752]{2,1,0:T(8,128)(2,1)S(1)} %get-tuple-element.220), channel_id=1, source_target_pairs={{0,8},{2,10},{8,16},{10,18},{16,24},{18,26},{24,28},{26,30},{28,20... | collective-permute-start | bytes 2113544 | tf_op jit(solution)/shard_map/ppermute | solution.py:55
  406.8 24.6 %collective-permute-start.19 = (bf16[2,64,2752]{2,1,0:T(8,128)(2,1)S(1)}, bf16[2,64,2752]{2,1,0:T(8,128)(2,1)S(1)}, u32[]{:S(2)}, u32[]{:S(2)}) collective-permute-start(bf16[2,64,2752]{2,1,0:T(8,128)(2,1)S(1)} %get-tuple-element.221), channel_id=1, source_target_pairs={{8,0},{10,2},{16,8},{18,10},{24,16},{26,18},{28,24},{30,26},{20,28... | collective-permute-start | bytes 2113544 | tf_op jit(solution)/shard_map/ppermute | solution.py:55
  408.3 23.2 %collective-permute-start.20 = (bf16[128,2048]{1,0:T(8,128)(2,1)S(1)}, bf16[128,2048]{1,0:T(8,128)(2,1)S(1)}, u32[]{:S(2)}, u32[]{:S(2)}) collective-permute-start(bf16[128,2048]{1,0:T(8,128)(2,1)S(1)} %copy-done.22), channel_id=1, source_target_pairs={{0,1},{1,0},{2,3},{3,2},{4,5},{5,4},{6,7},{7,6},{8,9},{9,8},{10,11... | collective-permute-start | bytes 1572872 | tf_op jit(solution)/shard_map/ppermute | solution.py:79
  408.8 22.3 %collective-permute-start.16 = (bf16[1,64,2752]{2,1,0:T(8,128)(2,1)S(1)}, bf16[1,64,2752]{2,1,0:T(8,128)(2,1)S(1)}, u32[]{:S(2)}, u32[]{:S(2)}) collective-permute-start(bf16[1,64,2752]{2,1,0:T(8,128)(2,1)S(1)} %get-tuple-element.218), channel_id=1, source_target_pairs={{0,8},{2,10},{8,16},{10,18},{16,24},{18,26},{24,28},{26,30},{28,20... | collective-permute-start | bytes 1056776 | tf_op jit(solution)/shard_map/ppermute | solution.py:55
  409.4 22.0 %collective-permute-start.17 = (bf16[1,64,2752]{2,1,0:T(8,128)(2,1)S(1)}, bf16[1,64,2752]{2,1,0:T(8,128)(2,1)S(1)}, u32[]{:S(2)}, u32[]{:S(2)}) collective-permute-start(bf16[1,64,2752]{2,1,0:T(8,128)(2,1)S(1)} %get-tuple-element.219), channel_id=1, source_target_pairs={{8,0},{10,2},{16,8},{18,10},{24,16},{26,18},{28,24},{30,26},{20,28... | collective-permute-start | bytes 1056776 | tf_op jit(solution)/shard_map/ppermute | solution.py:55
  439.0 24.6 %collective-permute-start.25 = (bf16[256,2048]{1,0:T(8,128)(2,1)S(1)}, bf16[256,2048]{1,0:T(8,128)(2,1)}, u32[]{:S(2)}, u32[]{:S(2)}) collective-permute-start(bf16[256,2048]{1,0:T(8,128)(2,1)S(1)} %get-tuple-element.233), channel_id=1, source_target_pairs={{0,1},{1,0},{2,3},{3,2},{4,5},{5,4},{6,7},{7,6},{8,9},{9,8},{10,11... | collective-permute-start | bytes 3145736 | tf_op jit(solution)/shard_map/ppermute | solution.py:79
  439.6 24.0 %collective-permute-start.23 = (bf16[2,64,2752]{2,1,0:T(8,128)(2,1)S(1)}, bf16[2,64,2752]{2,1,0:T(8,128)(2,1)S(1)}, u32[]{:S(2)}, u32[]{:S(2)}) collective-permute-start(bf16[2,64,2752]{2,1,0:T(8,128)(2,1)S(1)} %get-tuple-element.231), channel_id=1, source_target_pairs={{0,8},{2,10},{8,16},{10,18},{16,24},{18,26},{24,28},{26,30},{28,20... | collective-permute-start | bytes 2113544 | tf_op jit(solution)/shard_map/ppermute | solution.py:55
  440.3 23.2 %collective-permute-start.24 = (bf16[2,64,2752]{2,1,0:T(8,128)(2,1)S(1)}, bf16[2,64,2752]{2,1,0:T(8,128)(2,1)S(1)}, u32[]{:S(2)}, u32[]{:S(2)}) collective-permute-start(bf16[2,64,2752]{2,1,0:T(8,128)(2,1)S(1)} %get-tuple-element.232), channel_id=1, source_target_pairs={{8,0},{10,2},{16,8},{18,10},{24,16},{26,18},{28,24},{30,26},{20,28... | collective-permute-start | bytes 2113544 | tf_op jit(solution)/shard_map/ppermute | solution.py:55
  446.9 16.2 %collective-permute-start.21 = (bf16[1,64,2752]{2,1,0:T(8,128)(2,1)S(1)}, bf16[1,64,2752]{2,1,0:T(8,128)(2,1)S(1)}, u32[]{:S(2)}, u32[]{:S(2)}) collective-permute-start(bf16[1,64,2752]{2,1,0:T(8,128)(2,1)S(1)} %get-tuple-element.229), channel_id=1, source_target_pairs={{0,8},{2,10},{8,16},{10,18},{16,24},{18,26},{24,28},{26,30},{28,20... | collective-permute-start | bytes 1056776 | tf_op jit(solution)/shard_map/ppermute | solution.py:55
  447.7 15.9 %collective-permute-start.22 = (bf16[1,64,2752]{2,1,0:T(8,128)(2,1)S(1)}, bf16[1,64,2752]{2,1,0:T(8,128)(2,1)S(1)}, u32[]{:S(2)}, u32[]{:S(2)}) collective-permute-start(bf16[1,64,2752]{2,1,0:T(8,128)(2,1)S(1)} %get-tuple-element.230), channel_id=1, source_target_pairs={{8,0},{10,2},{16,8},{18,10},{24,16},{26,18},{28,24},{30,26},{20,28... | collective-permute-start | bytes 1056776 | tf_op jit(solution)/shard_map/ppermute | solution.py:55
  472.5 32.2 %collective-permute-start.31 = (bf16[512,1024]{1,0:T(8,128)(2,1)}, bf16[512,1024]{1,0:T(8,128)(2,1)}, u32[]{:S(2)}, u32[]{:S(2)}) collective-permute-start(bf16[512,1024]{1,0:T(8,128)(2,1)} %get-tuple-element.251), channel_id=1, source_target_pairs={{0,2},{2,0},{4,6},{6,4},{8,10},{10,8},{12,14},{14,12},{16,18},{18,... | collective-permute-start | bytes 3145736 | tf_op jit(solution)/shard_map/ppermute | solution.py:109
  472.5 32.2 %collective-permute-start.30 = (bf16[256,2048]{1,0:T(8,128)(2,1)S(1)}, bf16[256,2048]{1,0:T(8,128)(2,1)S(1)}, u32[]{:S(2)}, u32[]{:S(2)}) collective-permute-start(bf16[256,2048]{1,0:T(8,128)(2,1)S(1)} %copy-done.19), channel_id=1, source_target_pairs={{0,1},{1,0},{2,3},{3,2},{4,5},{5,4},{6,7},{7,6},{8,9},{9,8},{10,11... | collective-permute-start | bytes 3145736 | tf_op jit(solution)/shard_map/ppermute | solution.py:79
  473.9 11.3 %collective-permute-start.26 = (bf16[1,64,2752]{2,1,0:T(8,128)(2,1)S(1)}, bf16[1,64,2752]{2,1,0:T(8,128)(2,1)S(1)}, u32[]{:S(2)}, u32[]{:S(2)}) collective-permute-start(bf16[1,64,2752]{2,1,0:T(8,128)(2,1)S(1)} %get-tuple-element.244), channel_id=1, source_target_pairs={{0,8},{2,10},{8,16},{10,18},{16,24},{18,26},{24,28},{26,30},{28,20... | collective-permute-start | bytes 1056776 | tf_op jit(solution)/shard_map/ppermute | solution.py:55
  474.8 29.8 %collective-permute-start.28 = (bf16[2,64,2752]{2,1,0:T(8,128)(2,1)}, bf16[2,64,2752]{2,1,0:T(8,128)(2,1)}, u32[]{:S(2)}, u32[]{:S(2)}) collective-permute-start(bf16[2,64,2752]{2,1,0:T(8,128)(2,1)} %get-tuple-element.246), channel_id=1, source_target_pairs={{0,8},{2,10},{8,16},{10,18},{16,24},{18,26},{24,28},{26,30},{28,20... | collective-permute-start | bytes 2113544 | tf_op jit(solution)/shard_map/ppermute | solution.py:55
  475.8 28.9 %collective-permute-start.29 = (bf16[2,64,2752]{2,1,0:T(8,128)(2,1)}, bf16[2,64,2752]{2,1,0:T(8,128)(2,1)}, u32[]{:S(2)}, u32[]{:S(2)}) collective-permute-start(bf16[2,64,2752]{2,1,0:T(8,128)(2,1)} %get-tuple-element.247), channel_id=1, source_target_pairs={{8,0},{10,2},{16,8},{18,10},{24,16},{26,18},{28,24},{30,26},{20,28... | collective-permute-start | bytes 2113544 | tf_op jit(solution)/shard_map/ppermute | solution.py:55
  485.2 19.5 %collective-permute-start.27 = (bf16[1,64,2752]{2,1,0:T(8,128)(2,1)}, bf16[1,64,2752]{2,1,0:T(8,128)(2,1)}, u32[]{:S(2)}, u32[]{:S(2)}) collective-permute-start(bf16[1,64,2752]{2,1,0:T(8,128)(2,1)} %get-tuple-element.245), channel_id=1, source_target_pairs={{8,0},{10,2},{16,8},{18,10},{24,16},{26,18},{28,24},{30,26},{20,28... | collective-permute-start | bytes 1056776 | tf_op jit(solution)/shard_map/ppermute | solution.py:55
  510.2 24.7 %collective-permute-start.34 = (bf16[2,64,2752]{2,1,0:T(8,128)(2,1)}, bf16[2,64,2752]{2,1,0:T(8,128)(2,1)}, u32[]{:S(2)}, u32[]{:S(2)}) collective-permute-start(bf16[2,64,2752]{2,1,0:T(8,128)(2,1)} %get-tuple-element.265), channel_id=1, source_target_pairs={{0,8},{2,10},{8,16},{10,18},{16,24},{18,26},{24,28},{26,30},{28,20... | collective-permute-start | bytes 2113544 | tf_op jit(solution)/shard_map/ppermute | solution.py:55
  510.7 24.1 %collective-permute-start.35 = (bf16[2,64,2752]{2,1,0:T(8,128)(2,1)}, bf16[2,64,2752]{2,1,0:T(8,128)(2,1)}, u32[]{:S(2)}, u32[]{:S(2)}) collective-permute-start(bf16[2,64,2752]{2,1,0:T(8,128)(2,1)} %get-tuple-element.266), channel_id=1, source_target_pairs={{8,0},{10,2},{16,8},{18,10},{24,16},{26,18},{28,24},{30,26},{20,28... | collective-permute-start | bytes 2113544 | tf_op jit(solution)/shard_map/ppermute | solution.py:55
  512.2 22.3 %collective-permute-start.32 = (bf16[1,64,2752]{2,1,0:T(8,128)(2,1)}, bf16[1,64,2752]{2,1,0:T(8,128)(2,1)S(1)}, u32[]{:S(2)}, u32[]{:S(2)}) collective-permute-start(bf16[1,64,2752]{2,1,0:T(8,128)(2,1)} %get-tuple-element.263), channel_id=1, source_target_pairs={{0,8},{2,10},{8,16},{10,18},{16,24},{18,26},{24,28},{26,30},{28,20... | collective-permute-start | bytes 1056776 | tf_op jit(solution)/shard_map/ppermute | solution.py:55
  512.8 22.1 %collective-permute-start.33 = (bf16[1,64,2752]{2,1,0:T(8,128)(2,1)}, bf16[1,64,2752]{2,1,0:T(8,128)(2,1)}, u32[]{:S(2)}, u32[]{:S(2)}) collective-permute-start(bf16[1,64,2752]{2,1,0:T(8,128)(2,1)} %get-tuple-element.264), channel_id=1, source_target_pairs={{8,0},{10,2},{16,8},{18,10},{24,16},{26,18},{28,24},{30,26},{20,28... | collective-permute-start | bytes 1056776 | tf_op jit(solution)/shard_map/ppermute | solution.py:55
  540.5 42.5 %collective-permute-start.39 = (bf16[2,64,2752]{2,1,0:T(8,128)(2,1)S(1)}, bf16[2,64,2752]{2,1,0:T(8,128)(2,1)S(1)}, u32[]{:S(2)}, u32[]{:S(2)}) collective-permute-start(bf16[2,64,2752]{2,1,0:T(8,128)(2,1)S(1)} %get-tuple-element.280), channel_id=1, source_target_pairs={{0,8},{2,10},{8,16},{10,18},{16,24},{18,26},{24,28},{26,30},{28,20... | collective-permute-start | bytes 2113544 | tf_op jit(solution)/shard_map/ppermute | solution.py:55
  543.0 40.1 %collective-permute-start.40 = (bf16[2,64,2752]{2,1,0:T(8,128)(2,1)S(1)}, bf16[2,64,2752]{2,1,0:T(8,128)(2,1)S(1)}, u32[]{:S(2)}, u32[]{:S(2)}) collective-permute-start(bf16[2,64,2752]{2,1,0:T(8,128)(2,1)S(1)} %get-tuple-element.281), channel_id=1, source_target_pairs={{8,0},{10,2},{16,8},{18,10},{24,16},{26,18},{28,24},{30,26},{20,28... | collective-permute-start | bytes 2113544 | tf_op jit(solution)/shard_map/ppermute | solution.py:55
  543.0 40.1 %collective-permute-start.37 = (bf16[1,64,2752]{2,1,0:T(8,128)(2,1)S(1)}, bf16[1,64,2752]{2,1,0:T(8,128)(2,1)S(1)}, u32[]{:S(2)}, u32[]{:S(2)}) collective-permute-start(bf16[1,64,2752]{2,1,0:T(8,128)(2,1)S(1)} %get-tuple-element.278), channel_id=1, source_target_pairs={{0,8},{2,10},{8,16},{10,18},{16,24},{18,26},{24,28},{26,30},{28,20... | collective-permute-start | bytes 1056776 | tf_op jit(solution)/shard_map/ppermute | solution.py:55
  545.0 38.0 %collective-permute-start.38 = (bf16[1,64,2752]{2,1,0:T(8,128)(2,1)S(1)}, bf16[1,64,2752]{2,1,0:T(8,128)(2,1)S(1)}, u32[]{:S(2)}, u32[]{:S(2)}) collective-permute-start(bf16[1,64,2752]{2,1,0:T(8,128)(2,1)S(1)} %get-tuple-element.279), channel_id=1, source_target_pairs={{8,0},{10,2},{16,8},{18,10},{24,16},{26,18},{28,24},{30,26},{20,28... | collective-permute-start | bytes 1056776 | tf_op jit(solution)/shard_map/ppermute | solution.py:55
  545.0 24.3 %collective-permute-start.41 = (bf16[1,64,1024]{2,1,0:T(8,128)(2,1)S(1)}, bf16[1,64,1024]{2,1,0:T(8,128)(2,1)S(1)}, u32[]{:S(2)}, u32[]{:S(2)}) collective-permute-start(bf16[1,64,1024]{2,1,0:T(8,128)(2,1)S(1)} %get-tuple-element.282), channel_id=1, source_target_pairs={{0,8},{2,10},{8,16},{10,18},{16,24},{18,26},{24,28},{26,30},{28,20... | collective-permute-start | bytes 393224 | tf_op jit(solution)/shard_map/ppermute | solution.py:55
  569.3 13.7 %collective-permute-start.42 = (bf16[1,64,1024]{2,1,0:T(8,128)(2,1)S(1)}, bf16[1,64,1024]{2,1,0:T(8,128)(2,1)S(1)}, u32[]{:S(2)}, u32[]{:S(2)}) collective-permute-start(bf16[1,64,1024]{2,1,0:T(8,128)(2,1)S(1)} %get-tuple-element.283), channel_id=1, source_target_pairs={{8,0},{10,2},{16,8},{18,10},{24,16},{26,18},{28,24},{30,26},{20,28... | collective-permute-start | bytes 393224 | tf_op jit(solution)/shard_map/ppermute | solution.py:55
  591.2 47.0 %collective-permute-start.49 = (bf16[1,512,3072]{2,1,0:T(8,128)(2,1)}, bf16[1,512,3072]{2,1,0:T(8,128)(2,1)}, u32[]{:S(2)}, u32[]{:S(2)}) collective-permute-start(bf16[1,512,3072]{2,1,0:T(8,128)(2,1)} %bitcast.56), channel_id=1, source_target_pairs={{0,2},{2,0},{4,6},{6,4},{8,10},{10,8},{12,14},{14,12},{16,18},{18,... | collective-permute-start | bytes 9437192 | tf_op jit(solution)/shard_map/ppermute | solution.py:79
  603.4 34.9 %collective-permute-start.50 = (bf16[256,2048]{1,0:T(8,128)(2,1)}, bf16[256,2048]{1,0:T(8,128)(2,1)S(1)}, u32[]{:S(2)}, u32[]{:S(2)}) collective-permute-start(bf16[256,2048]{1,0:T(8,128)(2,1)} %get-tuple-element.304), channel_id=1, source_target_pairs={{0,1},{1,0},{2,3},{3,2},{4,5},{5,4},{6,7},{7,6},{8,9},{9,8},{10,11... | collective-permute-start | bytes 3145736 | tf_op jit(solution)/shard_map/ppermute | solution.py:79
  604.0 13.4 %collective-permute-start.43 = (bf16[1,64,2752]{2,1,0:T(8,128)(2,1)}, bf16[1,64,2752]{2,1,0:T(8,128)(2,1)S(1)}, u32[]{:S(2)}, u32[]{:S(2)}) collective-permute-start(bf16[1,64,2752]{2,1,0:T(8,128)(2,1)} %get-tuple-element.297), channel_id=1, source_target_pairs={{0,8},{2,10},{8,16},{10,18},{16,24},{18,26},{24,28},{26,30},{28,20... | collective-permute-start | bytes 1056776 | tf_op jit(solution)/shard_map/ppermute | solution.py:55
  615.4 22.9 %collective-permute-start.45 = (bf16[2,64,2752]{2,1,0:T(8,128)(2,1)}, bf16[2,64,2752]{2,1,0:T(8,128)(2,1)S(1)}, u32[]{:S(2)}, u32[]{:S(2)}) collective-permute-start(bf16[2,64,2752]{2,1,0:T(8,128)(2,1)} %get-tuple-element.299), channel_id=1, source_target_pairs={{0,8},{2,10},{8,16},{10,18},{16,24},{18,26},{24,28},{26,30},{28,20... | collective-permute-start | bytes 2113544 | tf_op jit(solution)/shard_map/ppermute | solution.py:55
  616.4 21.8 %collective-permute-start.46 = (bf16[2,64,2752]{2,1,0:T(8,128)(2,1)}, bf16[2,64,2752]{2,1,0:T(8,128)(2,1)S(1)}, u32[]{:S(2)}, u32[]{:S(2)}) collective-permute-start(bf16[2,64,2752]{2,1,0:T(8,128)(2,1)} %get-tuple-element.300), channel_id=1, source_target_pairs={{8,0},{10,2},{16,8},{18,10},{24,16},{26,18},{28,24},{30,26},{20,28... | collective-permute-start | bytes 2113544 | tf_op jit(solution)/shard_map/ppermute | solution.py:55
  617.4 20.8 %collective-permute-start.44 = (bf16[1,64,2752]{2,1,0:T(8,128)(2,1)S(1)}, bf16[1,64,2752]{2,1,0:T(8,128)(2,1)S(1)}, u32[]{:S(2)}, u32[]{:S(2)}) collective-permute-start(bf16[1,64,2752]{2,1,0:T(8,128)(2,1)S(1)} %get-tuple-element.298), channel_id=1, source_target_pairs={{8,0},{10,2},{16,8},{18,10},{24,16},{26,18},{28,24},{30,26},{20,28... | collective-permute-start | bytes 1056776 | tf_op jit(solution)/shard_map/ppermute | solution.py:55
  642.8 20.2 %collective-permute-start.55 = (bf16[256,2048]{1,0:T(8,128)(2,1)}, bf16[256,2048]{1,0:T(8,128)(2,1)S(1)}, u32[]{:S(2)}, u32[]{:S(2)}) collective-permute-start(bf16[256,2048]{1,0:T(8,128)(2,1)} %get-tuple-element.317), channel_id=1, source_target_pairs={{0,1},{1,0},{2,3},{3,2},{4,5},{5,4},{6,7},{7,6},{8,9},{9,8},{10,11... | collective-permute-start | bytes 3145736 | tf_op jit(solution)/shard_map/ppermute | solution.py:79
  644.1 18.4 %collective-permute-start.51 = (bf16[2,64,2752]{2,1,0:T(8,128)(2,1)}, bf16[2,64,2752]{2,1,0:T(8,128)(2,1)}, u32[]{:S(2)}, u32[]{:S(2)}) collective-permute-start(bf16[2,64,2752]{2,1,0:T(8,128)(2,1)} %get-tuple-element.313), channel_id=1, source_target_pairs={{0,8},{2,10},{8,16},{10,18},{16,24},{18,26},{24,28},{26,30},{28,20... | collective-permute-start | bytes 2113544 | tf_op jit(solution)/shard_map/ppermute | solution.py:55
  645.9 16.6 %collective-permute-start.52 = (bf16[2,64,2752]{2,1,0:T(8,128)(2,1)}, bf16[2,64,2752]{2,1,0:T(8,128)(2,1)}, u32[]{:S(2)}, u32[]{:S(2)}) collective-permute-start(bf16[2,64,2752]{2,1,0:T(8,128)(2,1)} %get-tuple-element.314), channel_id=1, source_target_pairs={{8,0},{10,2},{16,8},{18,10},{24,16},{26,18},{28,24},{30,26},{20,28... | collective-permute-start | bytes 2113544 | tf_op jit(solution)/shard_map/ppermute | solution.py:55
  646.2 16.3 %collective-permute-start.53 = (bf16[1,64,1024]{2,1,0:T(8,128)(2,1)}, bf16[1,64,1024]{2,1,0:T(8,128)(2,1)}, u32[]{:S(2)}, u32[]{:S(2)}) collective-permute-start(bf16[1,64,1024]{2,1,0:T(8,128)(2,1)} %get-tuple-element.315), channel_id=1, source_target_pairs={{0,8},{2,10},{8,16},{10,18},{16,24},{18,26},{24,28},{26,30},{28,20... | collective-permute-start | bytes 393224 | tf_op jit(solution)/shard_map/ppermute | solution.py:55
  647.9 14.6 %collective-permute-start.54 = (bf16[1,64,1024]{2,1,0:T(8,128)(2,1)}, bf16[1,64,1024]{2,1,0:T(8,128)(2,1)}, u32[]{:S(2)}, u32[]{:S(2)}) collective-permute-start(bf16[1,64,1024]{2,1,0:T(8,128)(2,1)} %get-tuple-element.316), channel_id=1, source_target_pairs={{8,0},{10,2},{16,8},{18,10},{24,16},{26,18},{28,24},{30,26},{20,28... | collective-permute-start | bytes 393224 | tf_op jit(solution)/shard_map/ppermute | solution.py:55
  662.5 61.9 %collective-permute-start.85 = (f32[128]{0:T(128)S(1)}, f32[128]{0:T(128)S(1)}, u32[]{:S(2)}, u32[]{:S(2)}) collective-permute-start(f32[128]{0:T(128)S(1)} %broadcast_select_fusion.6), channel_id=1, source_target_pairs={{0,2},{2,0},{4,6},{6,4},{8,10},{10,8},{12,14},{14,12},{16,18},{18,... | collective-permute-start | bytes 1544 | tf_op jit(solution)/shard_map/ppermute | solution.py:336
  669.0 14.7 %collective-permute-start.58 = (bf16[1,64,3072]{2,1,0:T(8,128)(2,1)S(1)}, bf16[1,64,3072]{2,1,0:T(8,128)(2,1)S(1)}, u32[]{:S(2)}, u32[]{:S(2)}) collective-permute-start(bf16[1,64,3072]{2,1,0:T(8,128)(2,1)S(1)} %get-tuple-element.327), channel_id=1, source_target_pairs={{0,8},{2,10},{8,16},{10,18},{16,24},{18,26},{24,28},{26,30},{28,20... | collective-permute-start | bytes 1179656 | tf_op jit(solution)/shard_map/ppermute | solution.py:55
  670.8 12.9 %collective-permute-start.59 = (bf16[1,64,3072]{2,1,0:T(8,128)(2,1)S(1)}, bf16[1,64,3072]{2,1,0:T(8,128)(2,1)S(1)}, u32[]{:S(2)}, u32[]{:S(2)}) collective-permute-start(bf16[1,64,3072]{2,1,0:T(8,128)(2,1)S(1)} %get-tuple-element.328), channel_id=1, source_target_pairs={{8,0},{10,2},{16,8},{18,10},{24,16},{26,18},{28,24},{30,26},{20,28... | collective-permute-start | bytes 1179656 | tf_op jit(solution)/shard_map/ppermute | solution.py:55
  671.1 11.2 %collective-permute-start.56 = (bf16[1,64,1024]{2,1,0:T(8,128)(2,1)S(1)}, bf16[1,64,1024]{2,1,0:T(8,128)(2,1)S(1)}, u32[]{:S(2)}, u32[]{:S(2)}) collective-permute-start(bf16[1,64,1024]{2,1,0:T(8,128)(2,1)S(1)} %get-tuple-element.325), channel_id=1, source_target_pairs={{0,8},{2,10},{8,16},{10,18},{16,24},{18,26},{24,28},{26,30},{28,20... | collective-permute-start | bytes 393224 | tf_op jit(solution)/shard_map/ppermute | solution.py:55
  672.8 10.9 %collective-permute-start.57 = (bf16[1,64,1024]{2,1,0:T(8,128)(2,1)S(1)}, bf16[1,64,1024]{2,1,0:T(8,128)(2,1)S(1)}, u32[]{:S(2)}, u32[]{:S(2)}) collective-permute-start(bf16[1,64,1024]{2,1,0:T(8,128)(2,1)S(1)} %get-tuple-element.326), channel_id=1, source_target_pairs={{8,0},{10,2},{16,8},{18,10},{24,16},{26,18},{28,24},{30,26},{20,28... | collective-permute-start | bytes 393224 | tf_op jit(solution)/shard_map/ppermute | solution.py:55
  685.0 13.2 %collective-permute-start.66 = (bf16[1,64,3072]{2,1,0:T(8,128)(2,1)S(1)}, bf16[1,64,3072]{2,1,0:T(8,128)(2,1)S(1)}, u32[]{:S(2)}, u32[]{:S(2)}) collective-permute-start(bf16[1,64,3072]{2,1,0:T(8,128)(2,1)S(1)} %get-tuple-element.343), channel_id=1, source_target_pairs={{0,8},{2,10},{8,16},{10,18},{16,24},{18,26},{24,28},{26,30},{28,20... | collective-permute-start | bytes 1179656 | tf_op jit(solution)/shard_map/ppermute | solution.py:55
  686.1 12.1 %collective-permute-start.67 = (bf16[1,64,3072]{2,1,0:T(8,128)(2,1)S(1)}, bf16[1,64,3072]{2,1,0:T(8,128)(2,1)S(1)}, u32[]{:S(2)}, u32[]{:S(2)}) collective-permute-start(bf16[1,64,3072]{2,1,0:T(8,128)(2,1)S(1)} %get-tuple-element.344), channel_id=1, source_target_pairs={{8,0},{10,2},{16,8},{18,10},{24,16},{26,18},{28,24},{30,26},{20,28... | collective-permute-start | bytes 1179656 | tf_op jit(solution)/shard_map/ppermute | solution.py:55
  699.4 12.4 %collective-permute-start.70 = (bf16[1,64,3072]{2,1,0:T(8,128)(2,1)S(1)}, bf16[1,64,3072]{2,1,0:T(8,128)(2,1)S(1)}, u32[]{:S(2)}, u32[]{:S(2)}) collective-permute-start(bf16[1,64,3072]{2,1,0:T(8,128)(2,1)S(1)} %get-tuple-element.354), channel_id=1, source_target_pairs={{0,8},{2,10},{8,16},{10,18},{16,24},{18,26},{24,28},{26,30},{28,20... | collective-permute-start | bytes 1179656 | tf_op jit(solution)/shard_map/ppermute | solution.py:55
  700.6 11.1 %collective-permute-start.71 = (bf16[1,64,3072]{2,1,0:T(8,128)(2,1)S(1)}, bf16[1,64,3072]{2,1,0:T(8,128)(2,1)S(1)}, u32[]{:S(2)}, u32[]{:S(2)}) collective-permute-start(bf16[1,64,3072]{2,1,0:T(8,128)(2,1)S(1)} %get-tuple-element.355), channel_id=1, source_target_pairs={{8,0},{10,2},{16,8},{18,10},{24,16},{26,18},{28,24},{30,26},{20,28... | collective-permute-start | bytes 1179656 | tf_op jit(solution)/shard_map/ppermute | solution.py:55
  714.1 10.8 %collective-permute-start.62 = (f32[256]{0:T(256)S(1)}, f32[256]{0:T(256)S(1)}, u32[]{:S(2)}, u32[]{:S(2)}) collective-permute-start(f32[256]{0:T(256)S(1)} %broadcast_select_fusion.5), channel_id=1, source_target_pairs={{0,4},{2,6},{4,0},{6,2},{8,12},{10,14},{12,8},{14,10},{16,20},{18,... | collective-permute-start | bytes 3080 | tf_op jit(solution)/shard_map/ppermute | solution.py:336
  723.8 10.7 %collective-permute-start.77 = (bf16[1,64,3072]{2,1,0:T(8,128)(2,1)S(1)}, bf16[1,64,3072]{2,1,0:T(8,128)(2,1)S(1)}, u32[]{:S(2)}, u32[]{:S(2)}) collective-permute-start(bf16[1,64,3072]{2,1,0:T(8,128)(2,1)S(1)} %get-tuple-element.430), channel_id=1, source_target_pairs={{8,0},{10,2},{16,8},{18,10},{24,16},{26,18},{28,24},{30,26},{20,28... | collective-permute-start | bytes 1179656 | tf_op jit(solution)/shard_map/ppermute | solution.py:55
  737.2 11.9 %collective-permute-start.63 = (f32[128]{0:T(128)S(1)}, f32[128]{0:T(128)S(1)}, u32[]{:S(2)}, u32[]{:S(2)}) collective-permute-start(f32[128]{0:T(128)S(1)} %broadcast_select_fusion.8), channel_id=1, source_target_pairs={{0,2},{2,0},{4,6},{6,4},{8,10},{10,8},{12,14},{14,12},{16,18},{18,... | collective-permute-start | bytes 1544 | tf_op jit(solution)/shard_map/ppermute | solution.py:336
  739.0 15.7 %collective-permute-start.80 = (bf16[1,64,1024]{2,1,0:T(8,128)(2,1)}, bf16[1,64,1024]{2,1,0:T(8,128)(2,1)S(1)}, u32[]{:S(2)}, u32[]{:S(2)}) collective-permute-start(bf16[1,64,1024]{2,1,0:T(8,128)(2,1)} %get-tuple-element.459), channel_id=1, source_target_pairs={{0,8},{2,10},{8,16},{10,18},{16,24},{18,26},{24,28},{26,30},{28,20... | collective-permute-start | bytes 393224 | tf_op jit(solution)/shard_map/ppermute | solution.py:55
  741.0 13.7 %collective-permute-start.81 = (bf16[1,64,1024]{2,1,0:T(8,128)(2,1)}, bf16[1,64,1024]{2,1,0:T(8,128)(2,1)S(1)}, u32[]{:S(2)}, u32[]{:S(2)}) collective-permute-start(bf16[1,64,1024]{2,1,0:T(8,128)(2,1)} %get-tuple-element.460), channel_id=1, source_target_pairs={{8,0},{10,2},{16,8},{18,10},{24,16},{26,18},{28,24},{30,26},{20,28... | collective-permute-start | bytes 393224 | tf_op jit(solution)/shard_map/ppermute | solution.py:55
  (52 other events, 471.4 us)
Sparse Core Ops, SparseCore 0:
  12.2 152.2 all-gather.2
  166.0 123.9 all-gather.4
